TPU v7x, 32 devices: a whole 2x2x4 slice. The times are simulated.
32 devices in a mesh: seq: 8 (over y, x, core), fsdp: 4 (over z).
Axes of the slice: x: 2, y: 2, z: 4, core: 2. Of those that a mesh axis runs over, the one named last changes fastest.
Arguments:
- tokens: bfloat16 [4, 1024, 2048], P('fsdp', 'seq'), may hold values from -6 to 6
- cotangent: bfloat16 [4, 1024, 2048], P('fsdp', 'seq'), may hold values from -6 to 6
- lengths: int32 [4], replicated, may hold values from 256 to 1024, as said below
- routes: int32 [4, 1024, 8], P('fsdp', 'seq'), may hold values from 0 to 63, all different within a row; in each aligned block of 128 rows (0 to 127, 128 to 255, ..., all dimensions but the last counted through in order) at most 24 rows name the same one
- norm_gains: bfloat16 [4, 2048], P(None, ('seq', 'fsdp')), may hold values from 0.5 to 1.5
- qkv_weight: bfloat16 [2048, 6144], P(('seq', 'fsdp')), may hold values from -0.125 to 0.125
- proj_weight: bfloat16 [2048, 2048], P(('seq', 'fsdp')), may hold values from -2 to 2
- router_weight: bfloat16 [2048, 64], P(('seq', 'fsdp')), may hold values from -0.15625 to 0.15625
- expert_up: bfloat16 [64, 2048, 2048], P(('seq', 'fsdp')), may hold values from -0.125 to 0.125
- expert_down: bfloat16 [64, 1024, 2048], P(('seq', 'fsdp')), may hold values from -6 to 6
Outputs:
- layer_out: bfloat16 [4, 1024, 2048], P('fsdp', 'seq')
- input_grad: bfloat16 [4, 1024, 2048], P('fsdp', 'seq')
- gains_grad: float32 [4, 2048], P(None, ('seq', 'fsdp'))
- qkv_grad: float32 [2048, 6144], P(('seq', 'fsdp'))
- proj_grad: float32 [2048, 2048], P(('seq', 'fsdp'))
- router_grad: float32 [2048, 64], P(('seq', 'fsdp'))
- up_grad: float32 [64, 2048, 2048], P(('seq', 'fsdp'))
- down_grad: float32 [64, 1024, 2048], P(('seq', 'fsdp'))
- balance_loss: float32 [1], replicated
Inputs may be any that keep to these rules, and one draw needn't show every extreme that they name: `lengths`: valid tokens of each slot; some slot in every draw has all 1024. Each token names 8 different experts; within each aligned block of 128 positions of a slot (the rows of one device) no expert is named by more than 24 routes.
All inputs are finite; a program needn't handle non-finite values.
Results may differ from a plain program's by a relative error of at most 0.02.
Values may be sent and summed in bfloat16 or wider, within the bound.
A program may use at most 320 MiB of HBM per device.

v0:
```python
import jax
import jax.numpy as jnp
from jax import lax
from jax.sharding import PartitionSpec as P

HEADS = 16
FF = 1024


epsilon = 1e-06
rope_base = 10000.0


def rms_scale(values, gain):
    return values * lax.rsqrt(jnp.mean(values * values, axis=-1, keepdims=True) + epsilon) * gain


def rotate(values, positions):
    half_dim = values.shape[-1] // 2
    frequency = rope_base ** (-jnp.arange(half_dim, dtype=jnp.float32) * 2.0 / values.shape[-1])
    angles = positions.astype(jnp.float32)[:, None] * frequency[None, :]
    cosine = jnp.cos(angles)[:, None, :]
    sine_part = jnp.sin(angles)[:, None, :]
    first_half = values[..., :half_dim]
    second_half = values[..., half_dim:]
    return jnp.concatenate(
        [
            first_half * cosine - second_half * sine_part,
            second_half * cosine + first_half * sine_part,
        ],
        axis=-1,
    )


def front(raw, gain_query, gain_key, positions, head_count):
    model_width = raw.shape[1] // 3
    rows_here = raw.shape[0]
    query_part = rms_scale(raw[:, :model_width], gain_query).reshape(rows_here, head_count, -1)
    key_part = rms_scale(raw[:, model_width : 2 * model_width], gain_key).reshape(
        rows_here, head_count, -1
    )
    value_part = raw[:, 2 * model_width :].reshape(rows_here, head_count, -1)
    return (rotate(query_part, positions), rotate(key_part, positions), value_part)


def attend_forward(queries, keys_all, values_all, key_valid, block_rows):
    scaling = queries.shape[-1] ** (-0.5)
    block_count = queries.shape[0] // block_rows
    blocked = queries.reshape(block_count, block_rows, queries.shape[1], queries.shape[2])

    def one_block(query_block):
        scores = (
            jnp.einsum("qhd,khd->hqk", query_block, keys_all, preferred_element_type=jnp.float32)
            * scaling
        )
        scores = jnp.where(key_valid[None, None, :], scores, -1e30)
        top_score = jnp.max(scores, axis=-1, keepdims=True)
        weights = jnp.exp(scores - top_score)
        denominator = jnp.sum(weights, axis=-1, keepdims=True)
        attn_weights = (weights / denominator).astype(jnp.bfloat16)
        log_total = top_score[..., 0] + jnp.log(denominator[..., 0])
        result = jnp.einsum(
            "hqk,khd->qhd", attn_weights, values_all, preferred_element_type=jnp.float32
        )
        return (result, log_total)

    results, log_totals = lax.map(one_block, blocked)
    return (results.reshape(queries.shape), log_totals)


def attend_backward(queries, keys_all, values_all, key_valid, log_totals, grad_heads, block_rows):
    scaling = queries.shape[-1] ** (-0.5)
    block_count = queries.shape[0] // block_rows
    query_blocks = queries.reshape(block_count, block_rows, queries.shape[1], queries.shape[2])
    grad_blocks = grad_heads.reshape(block_count, block_rows, queries.shape[1], queries.shape[2])

    def one_block(carry, inputs):
        key_grad, value_grad = carry
        query_block, grad_block, log_block = inputs
        scores = (
            jnp.einsum("qhd,khd->hqk", query_block, keys_all, preferred_element_type=jnp.float32)
            * scaling
        )
        scores = jnp.where(key_valid[None, None, :], scores, -1e30)
        attn_probs = jnp.exp(scores - log_block[..., None])
        value_grad = value_grad + jnp.einsum(
            "hqk,qhd->khd",
            attn_probs.astype(jnp.bfloat16),
            grad_block,
            preferred_element_type=jnp.float32,
        )
        weights_grad = jnp.einsum(
            "qhd,khd->hqk", grad_block, values_all, preferred_element_type=jnp.float32
        )
        row_inner = jnp.sum(attn_probs * weights_grad, axis=-1, keepdims=True)
        score_grad = (attn_probs * (weights_grad - row_inner) * scaling).astype(jnp.bfloat16)
        query_grad = jnp.einsum(
            "hqk,khd->qhd", score_grad, keys_all, preferred_element_type=jnp.float32
        )
        key_grad = key_grad + jnp.einsum(
            "hqk,qhd->khd", score_grad, query_block, preferred_element_type=jnp.float32
        )
        return ((key_grad, value_grad), query_grad)

    zeros_heads = jnp.zeros(keys_all.shape, jnp.float32)
    sums, query_grads = lax.scan(
        one_block, (zeros_heads, zeros_heads), (query_blocks, grad_blocks, log_totals)
    )
    return (query_grads.reshape(queries.shape), sums[0], sums[1])


def local(
    tokens,
    cotangent,
    lengths,
    routes,
    norm_gains,
    qkv_weight,
    proj_weight,
    router_weight,
    expert_up,
    expert_down,
):
    shard_len = tokens.shape[1]
    model_width = tokens.shape[2]
    slot_len = shard_len * lax.axis_size("seq")
    experts = router_weight.shape[1]
    top_count = routes.shape[2]
    capacity = 3 * shard_len * top_count // (2 * experts)
    piece_ff = expert_down.shape[1]
    pieces_dev = expert_up.shape[0]
    split_count = FF // piece_ff
    head_count = HEADS
    head_dim = model_width // head_count
    block_rows = min(512, slot_len)
    length = lax.dynamic_index_in_dim(lengths, lax.axis_index("fsdp"), 0, keepdims=False)
    valid_total = jnp.sum(lengths).astype(jnp.float32).reshape(1)
    positions = lax.axis_index("seq") * shard_len + jnp.arange(shard_len, dtype=jnp.int32)
    row_valid = (positions < length).astype(jnp.float32)
    local_routes = routes[0]
    route_match = (
        local_routes[:, :, None] == jnp.arange(experts, dtype=jnp.int32)[None, None, :]
    ).astype(jnp.float32)
    count_part = jnp.sum(route_match * row_valid[:, None, None], axis=(0, 1))
    full_qkv, full_proj, full_router, full_gains = (
        lax.all_gather(qkv_weight, ("seq", "fsdp"), axis=0, tiled=True),
        lax.all_gather(proj_weight, ("seq", "fsdp"), axis=0, tiled=True),
        lax.all_gather(router_weight, ("seq", "fsdp"), axis=0, tiled=True),
        lax.all_gather(norm_gains, ("seq", "fsdp"), axis=1, tiled=True),
    )
    gain_table = full_gains.astype(jnp.float32)
    resid_in = tokens[0].astype(jnp.float32)
    normed_one = rms_scale(resid_in, gain_table[0]).astype(jnp.bfloat16)
    qkv_raw = jnp.dot(normed_one, full_qkv, preferred_element_type=jnp.float32)

    def front_part(raw, gain_query, gain_key):
        return front(raw, gain_query, gain_key, positions, head_count)

    rotated_query, rotated_key, value_heads = front_part(qkv_raw, gain_table[1], gain_table[2])
    head_query, head_key, head_value = (
        lax.all_to_all(
            rotated_query.astype(jnp.bfloat16)[None], "seq", split_axis=2, concat_axis=1, tiled=True
        ),
        lax.all_to_all(
            rotated_key.astype(jnp.bfloat16)[None], "seq", split_axis=2, concat_axis=1, tiled=True
        ),
        lax.all_to_all(
            value_heads.astype(jnp.bfloat16)[None], "seq", split_axis=2, concat_axis=1, tiled=True
        ),
    )
    head_query = head_query[0]
    head_key = head_key[0]
    head_value = head_value[0]
    key_valid = jnp.arange(slot_len, dtype=jnp.int32) < length
    attn_heads, log_totals = attend_forward(head_query, head_key, head_value, key_valid, block_rows)
    attn_tokens = lax.all_to_all(
        attn_heads.astype(jnp.bfloat16)[None], "seq", split_axis=1, concat_axis=2, tiled=True
    )[0].reshape(shard_len, model_width)
    resid_mid = resid_in + jnp.dot(attn_tokens, full_proj, preferred_element_type=jnp.float32)
    normed_two = rms_scale(resid_mid, gain_table[3]).astype(jnp.bfloat16)
    router_logits = jnp.dot(normed_two, full_router, preferred_element_type=jnp.float32)
    router_probs = jax.nn.softmax(router_logits, axis=-1)
    prob_part = jnp.sum(router_probs * row_valid[:, None], axis=0)
    count_total, prob_total = lax.psum((count_part, prob_part), ("seq", "fsdp"))
    flat_routes = local_routes.reshape(-1)
    flat_match = route_match.reshape(-1, experts).astype(jnp.int32)
    earlier = jnp.cumsum(flat_match, axis=0) - flat_match
    slot_index = flat_routes * capacity + jnp.sum(earlier * flat_match, axis=1)
    owner_row = jnp.arange(shard_len * top_count, dtype=jnp.int32) // top_count
    fill_table = (
        jnp.full((experts * capacity,), shard_len, dtype=jnp.int32).at[slot_index].set(owner_row)
    )
    padded_rows = jnp.concatenate([normed_two, jnp.zeros((1, model_width), jnp.bfloat16)], axis=0)
    slot_rows = padded_rows[fill_table].reshape(experts, 1, capacity, model_width)
    send_rows = jnp.broadcast_to(slot_rows, (experts, split_count, capacity, model_width)).reshape(
        -1, capacity, model_width
    )
    received = lax.all_to_all(
        send_rows, ("seq", "fsdp"), split_axis=0, concat_axis=0, tiled=True
    ).reshape(-1, pieces_dev, capacity, model_width)
    hidden = jnp.einsum("spmd,pdf->spmf", received, expert_up, preferred_element_type=jnp.float32)
    gate_pre = hidden[..., :piece_ff]
    up_pre = hidden[..., piece_ff:]
    activation = (jax.nn.silu(gate_pre) * up_pre).astype(jnp.bfloat16)
    piece_out = jnp.einsum(
        "spmf,pfd->spmd", activation, expert_down, preferred_element_type=jnp.float32
    ).astype(jnp.bfloat16)
    returned = lax.all_to_all(
        piece_out.reshape(-1, capacity, model_width),
        ("seq", "fsdp"),
        split_axis=0,
        concat_axis=0,
        tiled=True,
    )
    combined = jnp.sum(
        returned.reshape(experts, split_count, capacity, model_width).astype(jnp.float32), axis=1
    ).reshape(experts * capacity, model_width)
    route_out = combined[slot_index].reshape(shard_len, top_count, model_width)
    gate_values = jnp.take_along_axis(router_probs, local_routes, axis=1)
    expert_sum = jnp.sum(gate_values[:, :, None] * route_out, axis=1)
    layer_out = (resid_mid + expert_sum).astype(jnp.bfloat16)[None]
    fraction = count_total / (top_count * valid_total)
    loss_value = (experts * jnp.sum(fraction * prob_total / valid_total)).reshape(1)
    grad_out = cotangent[0].astype(jnp.float32) * row_valid[:, None]
    gates_grad = jnp.sum(route_out * grad_out[:, None, :], axis=-1)
    gate_slot = (
        jnp.zeros((experts * capacity,), jnp.float32).at[slot_index].set(gate_values.reshape(-1))
    )
    grad_padded = jnp.concatenate([grad_out, jnp.zeros((1, model_width), jnp.float32)], axis=0)
    slot_grad = (
        (grad_padded[fill_table] * gate_slot[:, None])
        .astype(jnp.bfloat16)
        .reshape(experts, 1, capacity, model_width)
    )
    send_grad = jnp.broadcast_to(slot_grad, (experts, split_count, capacity, model_width)).reshape(
        -1, capacity, model_width
    )
    recv_grad = lax.all_to_all(
        send_grad, ("seq", "fsdp"), split_axis=0, concat_axis=0, tiled=True
    ).reshape(-1, pieces_dev, capacity, model_width)
    act_grad = jnp.einsum(
        "spmd,pfd->spmf", recv_grad, expert_down, preferred_element_type=jnp.float32
    )
    down_grad = jnp.einsum(
        "spmf,spmd->pfd", activation, recv_grad, preferred_element_type=jnp.float32
    )
    sigmoid_gate = jax.nn.sigmoid(gate_pre)
    gate_pre_grad = act_grad * up_pre * sigmoid_gate * (1.0 + gate_pre * (1.0 - sigmoid_gate))
    up_pre_grad = act_grad * gate_pre * sigmoid_gate
    hidden_grad = jnp.concatenate([gate_pre_grad, up_pre_grad], axis=-1).astype(jnp.bfloat16)
    up_grad = jnp.einsum(
        "spmd,spmf->pdf", received, hidden_grad, preferred_element_type=jnp.float32
    )
    rows_grad = jnp.einsum(
        "spmf,pdf->spmd", hidden_grad, expert_up, preferred_element_type=jnp.float32
    ).astype(jnp.bfloat16)
    back_rows = lax.all_to_all(
        rows_grad.reshape(-1, capacity, model_width),
        ("seq", "fsdp"),
        split_axis=0,
        concat_axis=0,
        tiled=True,
    )
    slot_input_grad = jnp.sum(
        back_rows.reshape(experts, split_count, capacity, model_width).astype(jnp.float32), axis=1
    ).reshape(experts * capacity, model_width)
    normed_two_grad = jnp.sum(
        slot_input_grad[slot_index].reshape(shard_len, top_count, model_width), axis=1
    )
    probs_grad = (
        jnp.sum(route_match * gates_grad[:, :, None], axis=1)
        + (experts * fraction / valid_total)[None, :] * row_valid[:, None]
    )
    logits_grad = router_probs * (
        probs_grad - jnp.sum(router_probs * probs_grad, axis=-1, keepdims=True)
    )
    back_qkv, back_proj, back_router = (full_qkv, full_proj, full_router)
    contract_rows = (((0,), (0,)), ((), ()))
    contract_cols = (((1,), (1,)), ((), ()))
    router_term = lax.dot_general(
        normed_two.astype(jnp.float32), logits_grad, contract_rows, precision=lax.Precision.HIGHEST
    )
    normed_two_grad = normed_two_grad + lax.dot_general(
        logits_grad, back_router.astype(jnp.float32), contract_cols, precision=lax.Precision.HIGHEST
    )
    norm_two_back = jax.vjp(rms_scale, resid_mid, gain_table[3])[1]
    mid_part, gain_three_grad = norm_two_back(normed_two_grad)
    mid_grad = grad_out + mid_part
    branch_grad = mid_grad.astype(jnp.bfloat16)
    attended_grad = lax.dot_general(
        branch_grad, back_proj, contract_cols, preferred_element_type=jnp.float32
    ).astype(jnp.bfloat16)
    heads_grad = lax.all_to_all(
        attended_grad.reshape(1, shard_len, head_count, head_dim),
        "seq",
        split_axis=2,
        concat_axis=1,
        tiled=True,
    )[0]
    query_grad, key_grad, value_grad = attend_backward(
        head_query, head_key, head_value, key_valid, log_totals, heads_grad, block_rows
    )
    query_tok, key_tok, value_tok = (
        lax.all_to_all(
            query_grad.astype(jnp.bfloat16)[None], "seq", split_axis=1, concat_axis=2, tiled=True
        ),
        lax.all_to_all(
            key_grad.astype(jnp.bfloat16)[None], "seq", split_axis=1, concat_axis=2, tiled=True
        ),
        lax.all_to_all(
            value_grad.astype(jnp.bfloat16)[None], "seq", split_axis=1, concat_axis=2, tiled=True
        ),
    )
    front_back = jax.vjp(front_part, qkv_raw, gain_table[1], gain_table[2])[1]
    raw_grad, gain_query_grad, gain_key_grad = front_back(
        (
            query_tok[0].astype(jnp.float32),
            key_tok[0].astype(jnp.float32),
            value_tok[0].astype(jnp.float32),
        )
    )
    raw_grad_low = raw_grad.astype(jnp.bfloat16)
    normed_one_grad = lax.dot_general(
        raw_grad_low, back_qkv, contract_cols, preferred_element_type=jnp.float32
    )
    norm_one_back = jax.vjp(rms_scale, resid_in, gain_table[0])[1]
    input_part, gain_one_grad = norm_one_back(normed_one_grad)
    input_grad = (mid_grad + input_part).astype(jnp.bfloat16)[None]
    gains_term = jnp.stack([gain_one_grad, gain_query_grad, gain_key_grad, gain_three_grad], axis=0)
    all_normed, all_raw, all_attn, all_branch = (
        lax.all_gather(normed_one, "fsdp", axis=0, tiled=True),
        lax.all_gather(raw_grad_low, "fsdp", axis=0, tiled=True),
        lax.all_gather(attn_tokens, "fsdp", axis=0, tiled=True),
        lax.all_gather(branch_grad, "fsdp", axis=0, tiled=True),
    )
    seq_count = lax.axis_size("seq")
    fsdp_count = lax.axis_size("fsdp")
    owned_rows = model_width // (seq_count * fsdp_count)

    def owned_columns(matrix):
        shaped = matrix.reshape(matrix.shape[0], seq_count, fsdp_count, owned_rows)
        return lax.dynamic_index_in_dim(shaped, lax.axis_index("fsdp"), 2, keepdims=False)

    qkv_blocks = jnp.einsum(
        "tsr,tc->src", owned_columns(all_normed), all_raw, preferred_element_type=jnp.float32
    )
    proj_blocks = jnp.einsum(
        "tsr,tc->src", owned_columns(all_attn), all_branch, preferred_element_type=jnp.float32
    )
    qkv_owned, proj_owned = (
        lax.psum_scatter(
            qkv_blocks.astype(jnp.bfloat16), "seq", scatter_dimension=0, tiled=True
        ).astype(jnp.float32),
        lax.psum_scatter(
            proj_blocks.astype(jnp.bfloat16), "seq", scatter_dimension=0, tiled=True
        ).astype(jnp.float32),
    )
    qkv_grad = qkv_owned[0]
    proj_grad = proj_owned[0]
    router_grad, gains_grad = (
        lax.psum_scatter(router_term, ("seq", "fsdp"), scatter_dimension=0, tiled=True),
        lax.psum_scatter(gains_term, ("seq", "fsdp"), scatter_dimension=1, tiled=True),
    )
    return (
        layer_out,
        input_grad,
        gains_grad,
        qkv_grad,
        proj_grad,
        router_grad,
        up_grad,
        down_grad,
        loss_value,
    )


def solution(mesh):
    return jax.shard_map(
        local,
        mesh=mesh,
        in_specs=(
            P("fsdp", "seq", None),
            P("fsdp", "seq", None),
            P(),
            P("fsdp", "seq", None),
            P(None, ("seq", "fsdp")),
            P(("seq", "fsdp"), None),
            P(("seq", "fsdp"), None),
            P(("seq", "fsdp"), None),
            P(("seq", "fsdp"), None, None),
            P(("seq", "fsdp"), None, None),
        ),
        out_specs=(
            P("fsdp", "seq", None),
            P("fsdp", "seq", None),
            P(None, ("seq", "fsdp")),
            P(("seq", "fsdp"), None),
            P(("seq", "fsdp"), None),
            P(("seq", "fsdp"), None),
            P(("seq", "fsdp"), None, None),
            P(("seq", "fsdp"), None, None),
            P(),
        ),
        check_vma=False,
    )
```

profile of v0, /device:TPU:0, one launch (start us, length us, event | category | flops | bytes accessed | tf_op | source)
XLA Modules:
  0.0 1708.5 jit_solution(7357455349049851875)
XLA Ops:
  8.7 70.7 %all-gather = bf16[32,64,4]{1,2,0:T(4,128)(2,1)S(1)} all-gather(bf16[1,64,4]{1,2,0:T(4,128)(2,1)} %bitcast.381), channel_id=1, replica_groups=mesh['seq'=8,'fsdp'=4] {'seq','fsdp'}, dimensions={0}, use_global_device_ids=true | all-gather | bytes 16896 | tf_op jit(solution)/shard_map/all_gather | solution.py:149
  83.9 84.7 %all-gather.8.cloned.1.call-done = bf16[2048,6144]{1,0:T(8,128)(2,1)} async-done(((bf16[64,6144]{1,0:T(8,128)(2,1)}), bf16[2048,6144]{1,0:T(8,128)(2,1)}) %all-gather.8.cloned.1.call-update) | async-done | bytes 25165840 | tf_op jit(solution)/shard_map/all_gather | solution.py:146
  168.5 10.1 fusion.144
  191.2 7.3 all-to-all-done
  203.8 8.5 all-to-all-done.1
  216.2 18.0 %reduce-window.6 = s32[64,8,128]{2,1,0:T(8,128)S(1)} reduce-window(s32[64,8,128]{2,1,0:T(8,128)S(1)} %convert_convert_fusion, s32[]{:T(128)} %constant.122.clone.1), window={size=1x1x128 pad=0_0x0_0x127_0}, to_apply=%region_10.11 | reduce-window | flops 8323072 | bytes 524292 | tf_op jit(solution)/shard_map/reduce-window
  237.8 7.8 while.28
  267.6 7.0 gather_fusion
  280.2 7.9 gather_fusion.2
  288.4 194.1 %all_gather.27 = bf16[2048,64]{1,0:T(8,128)(2,1)S(1)} all-gather(bf16[64,64]{1,0:T(8,128)(2,1)S(1)} %copy-done.56), channel_id=1, replica_groups=mesh['seq'=8,'fsdp'=4] {'seq','fsdp'}, dimensions={0}, use_global_device_ids=true | all-gather | bytes 270336 | tf_op jit(solution)/shard_map/all_gather | solution.py:148
  483.5 7.0 gather_fusion.4
  495.0 7.9 multiply_convert_fusion.1
  506.9 21.3 %fusion.84 = f32[32,2,24,2048]{3,2,0,1:T(8,128)} fusion(bf16[2,2048,2048]{2,1,0:T(8,128)(2,1)} %param.22, bf16[32,2,24,2048]{3,2,1,0:T(8,128)(2,1)} %bitcast.36), kind=kOutput, calls=%fused_computation.97 | convolution fusion | flops 12884901888 | bytes 35651584 | tf_op jit(solution)/shard_map/spmd,pdf->spmf/dot_general | solution.py:201
  528.2 115.6 %all-to-all-done.6 = bf16[64,24,2048]{2,1,0:T(8,128)(2,1)} async-done(((bf16[64,24,2048]{2,1,0:T(8,128)(2,1)}), bf16[64,24,2048]{2,1,0:T(8,128)(2,1)}, u32[]{:S(2)}, u32[]{:S(2)}) %all-to-all-start.6) | async-done | bytes 6291488 | tf_op jit(solution)/shard_map/all_to_all | solution.py:238
  643.8 17.3 %fusion.77 = (bf16[32,2,24,1024]{3,2,0,1:T(8,128)(2,1)}, bf16[32,2,24,1024]{3,2,0,1:T(8,128)(2,1)}, bf16[32,2,24,1024]{3,2,0,1:T(8,128)(2,1)}) fusion(f32[32,2,24,2048]{3,2,0,1:T(8,128)} %fusion.84, bf16[2,1024,2048]{2,1,0:T(8,128)(2,1)} %param.23, bf16[32,2,24,2048]{3,2,1,0:T(8,128)(2,1)} %bitcast.49), kind=kOutput, calls=%fused_computation.86 | convolution fusion | flops 6467616768 | bytes 36700160 | tf_op jit(solution)/shard_map/spmd,pfd->spmf/dot_general | solution.py:241
  661.1 10.9 convert_bitcast_fusion.1
  675.3 7.1 all-to-all-start.5
  682.4 19.4 %convert_bitcast_fusion = bf16[32,2,24,2048]{3,2,0,1:T(8,128)(2,1)} fusion(bf16[2,2048,2048]{2,1,0:T(8,128)(2,1)} %param.22, bf16[32,2,24,1024]{3,2,0,1:T(8,128)(2,1)} %get-tuple-element.337, bf16[32,2,24,1024]{3,2,0,1:T(8,128)(2,1)} %get-tuple-element.336), kind=kOutput, calls=%fused_computation.91 | convolution fusion | flops 12900630528 | bytes 29360128 | tf_op jit(solution)/shard_map/spmf,pdf->spmd/dot_general | solution.py:254
  701.8 6.6 copy.311
  708.5 110.8 %all-to-all-done.5 = bf16[64,24,2048]{2,1,0:T(8,128)(2,1)} async-done(((bf16[64,24,2048]{2,1,0:T(8,128)(2,1)}), bf16[64,24,2048]{2,1,0:T(8,128)(2,1)}, u32[]{:S(2)}, u32[]{:S(2)}) %all-to-all-start.5) | async-done | bytes 6291488 | tf_op jit(solution)/shard_map/all_to_all | solution.py:208
  819.3 7.1 all-to-all-start.7
  827.9 9.1 bitcast_convert_fusion.1
  837.0 14.1 gather_fusion.1
  851.1 142.9 %all-to-all-done.7 = bf16[64,24,2048]{2,1,0:T(8,128)(2,1)} async-done(((bf16[64,24,2048]{2,1,0:T(8,128)(2,1)}), bf16[64,24,2048]{2,1,0:T(8,128)(2,1)}, u32[]{:S(2)}, u32[]{:S(2)}) %all-to-all-start.7) | async-done | bytes 6291488 | tf_op jit(solution)/shard_map/all_to_all | solution.py:257
  994.0 9.3 bitcast_convert_fusion
  1007.7 13.5 gather_fusion.3
  1021.4 44.3 %psum.14 = f32[64]{0:T(128)S(1)} all-reduce(f32[64]{0:T(128)S(1)} %get-tuple-element.294), channel_id=1, replica_groups=mesh['seq'=8,'fsdp'=4] {'seq','fsdp'}, use_global_device_ids=true, to_apply=%region_20.21 | all-reduce | flops 64 | bytes 512 | tf_op jit(solution)/shard_map/psum | solution.py:184
  1066.9 5.7 bitcast_reduce_fusion
  1075.5 6.5 fusion.96
  1087.7 9.2 all-to-all-done.8
  1098.9 50.1 %while.29 = (s32[]{:T(128)}, f32[1024,2,128]{0,2,1:T(8,128)}, f32[1024,2,128]{0,2,1:T(8,128)S(1)}, bf16[2,512,2,128]{3,1,0,2:T(8,128)(2,1)}, bf16[2,512,2,128]{3...) while((s32[]{:T(128)}, f32[1024,2,128]{0,2,1:T(8,128)}, ...), condition=%wide.region_26.27_spmd.clone, body=%wide.region_24.26_spmd.clone.sunk | while | flops 1357911040 | bytes 53491872 | solution.py:106
  1105.5 8.0 fusion.200
  1116.3 7.7 fusion.202
  1130.4 8.2 fusion.200
  1141.4 7.6 fusion.202
  1157.9 6.7 all-to-all-done.10
  1169.3 8.5 all-to-all-done.11
  1184.4 7.3 all-to-all-done.9
  1202.5 15.1 fusion.98
  1226.5 92.9 %all-gather.14.cloned.1.call-done = bf16[512,6144]{1,0:T(8,128)(2,1)} async-done(((bf16[128,6144]{1,0:T(8,128)(2,1)}), bf16[512,6144]{1,0:T(8,128)(2,1)}) %all-gather.14.cloned.1.call-update) | async-done | bytes 6291472 | tf_op jit(solution)/shard_map/all_gather | solution.py:332
  1319.4 8.1 convolution_convert_fusion
  1329.3 22.7 %convolution_bitcast_fusion = f32[2,2048,2048]{2,1,0:T(8,128)} fusion(bf16[32,2,24,2048]{3,2,1,0:T(8,128)(2,1)} %bitcast.36, bf16[32,2,24,1024]{3,2,0,1:T(8,128)(2,1)} %get-tuple-element.337, bf16[32,2,24,1024]{3,2,0,1:T(8,128)(2,1)S(1)} %copy-done.87), kind=kOutput, calls=%fused_computation.65 | convolution fusion | flops 12897484800 | bytes 46137344 | tf_op jit(solution)/shard_map/spmd,spmf->pdf/dot_general | solution.py:251
  1352.2 13.8 convolution_bitcast_fusion.1
  1366.0 38.6 %psum.15 = f32[64]{0:T(128)S(1)} all-reduce(f32[64]{0:T(128)S(1)} %copy-done.83), channel_id=1, replica_groups=mesh['seq'=8,'fsdp'=4] {'seq','fsdp'}, use_global_device_ids=true, to_apply=%region_39.40 | all-reduce | flops 64 | bytes 512 | tf_op jit(solution)/shard_map/psum | solution.py:184
  1408.8 46.6 %reduce-scatter.13.cloned.1.call-done = f32[64,4]{1,0:T(8,128)} async-done(((f32[2048,4]{1,0:T(8,128)}), f32[64,4]{1,0:T(8,128)}) %reduce-scatter.13.cloned.1.call-update) | async-done | bytes 1040
  1456.8 40.1 %reduce-scatter.9.cloned.1.call-done = bf16[1,64,2048]{2,1,0:T(8,128)(2,1)} async-done(((bf16[8,64,2048]{2,1,0:T(8,128)(2,1)}), bf16[1,64,2048]{2,1,0:T(8,128)(2,1)}) %reduce-scatter.9.cloned.1.call-update) | async-done | bytes 262160 | tf_op jit(solution)/shard_map/reduce_scatter | solution.py:354
  1498.7 63.4 %reduce-scatter.7.cloned.1.call-done = bf16[1,64,6144]{2,1,0:T(8,128)(2,1)} async-done(((bf16[8,64,6144]{2,1,0:T(8,128)(2,1)}), bf16[1,64,6144]{2,1,0:T(8,128)(2,1)}) %reduce-scatter.7.cloned.1.call-update) | async-done | bytes 786448 | tf_op jit(solution)/shard_map/reduce_scatter | solution.py:351
  1564.5 135.7 %reduce-scatter.11.cloned.1.call-done = f32[64,64]{1,0:T(8,128)} async-done(((f32[2048,64]{1,0:T(8,128)}), f32[64,64]{1,0:T(8,128)}) %reduce-scatter.11.cloned.1.call-update) | async-done | bytes 16400 | tf_op jit(solution)/shard_map/reduce_scatter | solution.py:361
  (347 shorter events, 164.9 us)
Async XLA Ops:
  7.2 161.4 %all-gather.8.cloned.1.call-start = ((), (), s32[]{:S(2)}) async-start(), calls=%async_computation.16 | async-start | bytes 25952256 | tf_op jit(solution)/shard_map/all_gather | solution.py:146
  7.9 253.5 %all-gather.10.cloned.1.call-start = ((), (), s32[]{:S(2)}) async-start(), calls=%async_computation.17 | async-start | bytes 8650752 | tf_op jit(solution)/shard_map/all_gather | solution.py:147
  80.7 97.9 %copy-start.61 = (f32[128]{0:T(128)}, f32[128]{0:T(128)S(1)}, u32[]{:S(2)}) copy-start(f32[128]{0:T(128)S(1)} %fusion.134) | copy-start | bytes 1540
  81.1 100.0 %copy-start.32 = (f32[128,64]{1,0:T(8,128)}, f32[128,64]{1,0:T(8,128)S(1)}, u32[]{:S(2)}) copy-start(f32[128,64]{1,0:T(8,128)S(1)} %get-tuple-element.364) | copy-start | bytes 98308
  81.1 100.0 %copy-start.34 = (f32[128,64]{1,0:T(8,128)}, f32[128,64]{1,0:T(8,128)S(1)}, u32[]{:S(2)}) copy-start(f32[128,64]{1,0:T(8,128)S(1)} %get-tuple-element.365) | copy-start | bytes 98308
  81.3 98.4 %copy-start.43 = (f32[1,2048]{1,0:T(1,128)}, f32[1,2048]{1,0:T(1,128)S(1)}, u32[]{:S(2)}) copy-start(f32[1,2048]{1,0:T(1,128)S(1)} %get-tuple-element.361) | copy-start | bytes 24580
  81.3 98.5 %copy-start.45 = (f32[1,2048]{1,0:T(1,128)}, f32[1,2048]{1,0:T(1,128)S(1)}, u32[]{:S(2)}) copy-start(f32[1,2048]{1,0:T(1,128)S(1)} %get-tuple-element.362) | copy-start | bytes 24580
  81.3 185.2 %copy-start.47 = (f32[1,2048]{1,0:T(1,128)}, f32[1,2048]{1,0:T(1,128)S(1)}, u32[]{:S(2)}) copy-start(f32[1,2048]{1,0:T(1,128)S(1)} %get-tuple-element.360) | copy-start | bytes 24580
  184.5 13.9 all-to-all-start
  198.5 13.9 all-to-all-start.1
  212.4 25.3 %all-to-all-start.2 = ((bf16[1,128,16,128]{3,1,0,2:T(8,128)(2,1)}), bf16[1,128,16,128]{3,1,0,2:T(8,128)(2,1)S(1)}, u32[]{:S(2)}, u32[]{:S(2)}) async-start(bf16[1,128,16,128]{3,1,0,2:T(8,128)(2,1)} %copy.294), calls=%async_computation.2 | async-start | bytes 1048576 | tf_op jit(solution)/shard_map/all_to_all | solution.py:167
  247.0 14.0 all-to-all-start.3
  267.5 214.9 %copy-start.16 = (bf16[128,2048]{1,0:T(8,128)(2,1)}, bf16[128,2048]{1,0:T(8,128)(2,1)S(1)}, u32[]{:S(2)}) copy-start(bf16[128,2048]{1,0:T(8,128)(2,1)S(1)} %multiply_convert_fusion.3) | copy-start | bytes 1572868
  274.6 228.3 %all-to-all-start.4 = ((bf16[64,24,2048]{2,1,0:T(8,128)(2,1)}), bf16[64,24,2048]{2,1,0:T(8,128)(2,1)}, u32[]{:S(2)}, u32[]{:S(2)}) async-start(bf16[64,24,2048]{2,1,0:T(8,128)(2,1)} %bitcast.334), calls=%async_computation.4 | async-start | bytes 12582912 | tf_op jit(solution)/shard_map/all_to_all | solution.py:198
  502.9 141.0 %all-to-all-start.6 = ((bf16[64,24,2048]{2,1,0:T(8,128)(2,1)}), bf16[64,24,2048]{2,1,0:T(8,128)(2,1)}, u32[]{:S(2)}, u32[]{:S(2)}) async-start(bf16[64,24,2048]{2,1,0:T(8,128)(2,1)} %multiply_convert_fusion.1), calls=%async_computation.6 | async-start | bytes 12582912 | tf_op jit(solution)/shard_map/all_to_all | solution.py:238
  675.3 144.0 %all-to-all-start.5 = ((bf16[64,24,2048]{2,1,0:T(8,128)(2,1)}), bf16[64,24,2048]{2,1,0:T(8,128)(2,1)}, u32[]{:S(2)}, u32[]{:S(2)}) async-start(bf16[64,24,2048]{2,1,0:T(8,128)(2,1)} %bitcast.333), calls=%async_computation.5 | async-start | bytes 12582912 | tf_op jit(solution)/shard_map/all_to_all | solution.py:208
  819.3 174.7 %all-to-all-start.7 = ((bf16[64,24,2048]{2,1,0:T(8,128)(2,1)}), bf16[64,24,2048]{2,1,0:T(8,128)(2,1)}, u32[]{:S(2)}, u32[]{:S(2)}) async-start(bf16[64,24,2048]{2,1,0:T(8,128)(2,1)} %bitcast.332), calls=%async_computation.7 | async-start | bytes 12582912 | tf_op jit(solution)/shard_map/all_to_all | solution.py:257
  826.4 392.7 %all-gather.16.cloned.1.call-start = ((), (), s32[]{:S(2)}) async-start(), calls=%async_computation.21 | async-start | bytes 2621440 | tf_op jit(solution)/shard_map/all_gather | solution.py:333
  851.1 152.2 %copy-start.15 = (f32[128,2048]{1,0:T(8,128)S(1)}, f32[128,2048]{1,0:T(8,128)}, u32[]{:S(2)}) copy-start(f32[128,2048]{1,0:T(8,128)} %copy-done.14) | copy-start | bytes 3145732
  1007.6 58.6 %copy-start.39 = (f32[128,64]{0,1:T(8,128)S(1)}, f32[128,64]{0,1:T(8,128)}, u32[]{:S(2)}) copy-start(f32[128,64]{0,1:T(8,128)} %copy-done.38) | copy-start | bytes 98308
  1007.6 58.6 %copy-start.58 = (f32[128]{0:T(128)S(1)}, f32[128]{0:T(128)}, u32[]{:S(2)}) copy-start(f32[128]{0:T(128)} %copy-done.57) | copy-start | bytes 1540
  1007.7 58.6 %copy-start.73 = (f32[128]{0:T(128)S(1)}, f32[128]{0:T(128)}, u32[]{:S(2)}) copy-start(f32[128]{0:T(128)} %copy-done.72) | copy-start | bytes 1540
  1021.4 52.4 %copy-start.36 = (f32[128,64]{0,1:T(8,128)}, f32[128,64]{0,1:T(8,128)S(1)}, u32[]{:S(2)}) copy-start(f32[128,64]{0,1:T(8,128)S(1)} %get-tuple-element.295) | copy-start | bytes 98308
  1083.0 13.9 all-to-all-start.8
  1087.2 132.0 %all-gather.18.cloned.1.call-start = ((), (), s32[]{:S(2)}) async-start(), calls=%async_computation.22 | async-start | bytes 2621440 | tf_op jit(solution)/shard_map/all_gather | solution.py:334
  1151.5 13.2 all-to-all-start.10
  1155.0 68.6 %all-gather.12.cloned.1.call-start = ((), (), s32[]{:S(2)}) async-start(), calls=%async_computation.18 | async-start | bytes 2621440 | tf_op jit(solution)/shard_map/all_gather | solution.py:331
  1164.6 13.2 all-to-all-start.11
  1177.8 13.9 all-to-all-start.9
  1182.0 137.4 %all-gather.14.cloned.1.call-start = ((), (), s32[]{:S(2)}) async-start(), calls=%async_computation.19 | async-start | bytes 7864320 | tf_op jit(solution)/shard_map/all_gather | solution.py:332
  1202.4 252.9 %reduce-scatter.13.cloned.1.call-start = ((), (), s32[]{:S(2)}) async-start(), calls=%async_computation.25 | async-start | bytes 1081344
  1219.0 277.9 %reduce-scatter.9.cloned.1.call-start = ((), (), s32[]{:S(2)}) async-start(), calls=%async_computation.23 | async-start | bytes 2359296 | tf_op jit(solution)/shard_map/reduce_scatter | solution.py:354
  1223.5 338.6 %reduce-scatter.7.cloned.1.call-start = ((), (), s32[]{:S(2)}) async-start(), calls=%async_computation.20 | async-start | bytes 7077888 | tf_op jit(solution)/shard_map/reduce_scatter | solution.py:351
  1327.5 372.7 %reduce-scatter.11.cloned.1.call-start = ((), (), s32[]{:S(2)}) async-start(), calls=%async_computation.24 | async-start | bytes 1081344 | tf_op jit(solution)/shard_map/reduce_scatter | solution.py:361
  1352.0 52.5 %copy-start.2 = (f32[128,64]{0,1:T(8,128)S(1)}, f32[128,64]{0,1:T(8,128)}, u32[]{:S(2)}) copy-start(f32[128,64]{0,1:T(8,128)} %copy-done) | copy-start | bytes 98308
  1352.0 52.5 %copy-start.17 = (bf16[128,2048]{1,0:T(8,128)(2,1)S(1)}, bf16[128,2048]{1,0:T(8,128)(2,1)}, u32[]{:S(2)}) copy-start(bf16[128,2048]{1,0:T(8,128)(2,1)} %copy-done.16) | copy-start | bytes 1572868
  1352.0 52.5 %copy-start.37 = (f32[128,64]{0,1:T(8,128)S(1)}, f32[128,64]{0,1:T(8,128)}, u32[]{:S(2)}) copy-start(f32[128,64]{0,1:T(8,128)} %copy-done.36) | copy-start | bytes 98308
  1352.1 52.5 %copy-start.55 = (f32[128]{0:T(128)S(1)}, f32[128]{0:T(128)}, u32[]{:S(2)}) copy-start(f32[128]{0:T(128)} %copy-done.53) | copy-start | bytes 1540
  1352.1 52.5 %copy-start.60 = (f32[64]{0:T(128)S(1)}, f32[64]{0:T(128)}, u32[]{:S(2)}) copy-start(f32[64]{0:T(128)} %copy-done.59) | copy-start | bytes 772
  1352.1 52.5 %copy-start.69 = (f32[128]{0:T(128)S(1)}, f32[128]{0:T(128)}, u32[]{:S(2)}) copy-start(f32[128]{0:T(128)} %copy-done.68) | copy-start | bytes 1540
  1352.1 54.3 %copy-start.74 = (f32[64]{0:T(128)S(1)}, f32[64]{0:T(128)}, u32[]{:S(2)}) copy-start(f32[64]{0:T(128)} %get-tuple-element.333) | copy-start | bytes 772
  1352.1 55.5 %copy-start.82 = (f32[128]{0:T(128)S(1)}, f32[128]{0:T(128)}, u32[]{:S(2)}) copy-start(f32[128]{0:T(128)} %copy-done.81) | copy-start | bytes 1540
  1352.1 55.5 %copy-start.84 = (f32[128]{0:T(128)S(1)}, f32[128]{0:T(128)}, u32[]{:S(2)}) copy-start(f32[128]{0:T(128)} %get-tuple-element.291) | copy-start | bytes 1540
  1352.1 55.5 %copy-start.13 = (bf16[1,128,2048]{2,1,0:T(8,128)(2,1)S(1)}, bf16[1,128,2048]{2,1,0:T(8,128)(2,1)}, u32[]{:S(2)}) copy-start(bf16[1,128,2048]{2,1,0:T(8,128)(2,1)} %param.14) | copy-start | bytes 1572868
  1352.1 55.5 %copy-start.24 = (f32[128,2048]{1,0:T(8,128)S(1)}, f32[128,2048]{1,0:T(8,128)}, u32[]{:S(2)}) copy-start(f32[128,2048]{1,0:T(8,128)} %get-tuple-element.331) | copy-start | bytes 3145732
  1352.1 55.5 %copy-start.25 = (f32[128,2048]{1,0:T(8,128)S(1)}, f32[128,2048]{1,0:T(8,128)}, u32[]{:S(2)}) copy-start(f32[128,2048]{1,0:T(8,128)} %get-tuple-element.371) | copy-start | bytes 3145732
  1352.1 55.5 %copy-start.42 = (f32[1,2048]{1,0:T(1,128)S(1)}, f32[1,2048]{1,0:T(1,128)}, u32[]{:S(2)}) copy-start(f32[1,2048]{1,0:T(1,128)} %copy-done.40) | copy-start | bytes 24580
  1352.2 55.5 %copy-start.63 = (f32[128]{0:T(128)S(1)}, f32[128]{0:T(128)}, u32[]{:S(2)}) copy-start(f32[128]{0:T(128)} %copy-done.61) | copy-start | bytes 1540
  (62 other events, 915.9 us)
Sparse Core Ops, SparseCore 0:
  10.9 157.6 all-gather.7
  171.5 81.1 all-gather.9
  828.8 99.5 all-gather.15
  1089.3 45.5 all-gather.17
  1157.6 45.6 all-gather.11
  1205.3 114.0 all-gather.13
  1321.6 133.6 reduce-scatter.12
  1459.0 37.8 reduce-scatter.8
  1500.3 61.7 reduce-scatter.6
  1564.9 135.2 reduce-scatter.10
where the time goes:
time: 1720 us; the launch traced here: 1710 us
  waiting for transfers between devices  888 us (52%)
  blocking collectives  348 us (20%)
  matrix products  210 us (12%)
  local copies, waits for them, and re-layouts  102 us (6%)
  other arithmetic  87.4 us (5%)
  starting transfers between devices  53.8 us (3%)
  between operations  18.5 us (1%)
    all_gather x1, blocking collectives, local(): lax.all_gather(router_weight, ('seq', 'fsdp'), axis=0, tiled=True)  194 us
    all_to_all x1, waiting for transfers between devices, local(): lax.all_to_all(rows_grad.reshape(-1, capacity, model_width), ('seq', 'fsd...  143 us
    reduce_scatter x1, waiting for transfers between devices, local(): lax.psum_scatter(router_term, ('seq', 'fsdp'), scatter_dimension=0, tiled...  136 us
    all_to_all x1, waiting for transfers between devices, local(): lax.all_to_all(send_grad, ('seq', 'fsdp'), split_axis=0, concat_axis=0, t...  116 us
    all_to_all x1, waiting for transfers between devices, local(): lax.all_to_all(piece_out.reshape(-1, capacity, model_width), ('seq', 'fsd...  111 us
    all_gather x1, waiting for transfers between devices, local(): lax.all_gather(raw_grad_low, 'fsdp', axis=0, tiled=True)  92.9 us
    all_gather x1, waiting for transfers between devices, local(): lax.all_gather(qkv_weight, ('seq', 'fsdp'), axis=0, tiled=True)  84.7 us
    psum x2, blocking collectives, local(): count_total, prob_total = lax.psum((count_part, prob_part), ('seq', 'fsdp'))  82.9 us
  transfers between devices with their start and end apart: 22, of which 16 were waited for; matrix products, arithmetic and copies ran while one was open for 21% of the time, Pallas kernels for 0%

commit v1 on v0

v1 whole, which is shorter than its diff:
```python
import functools

import jax
import jax.numpy as jnp
from jax import lax
from jax.experimental import pallas as pl
from jax.experimental.pallas import tpu as pltpu
from jax.sharding import PartitionSpec as P

HEADS = 16
FF = 1024

epsilon = 1e-06
rope_base = 10000.0
MESH = pl.DeviceIdType.MESH
BF = jnp.bfloat16
F32 = jnp.float32


def dot(a, b, ca, cb):
    return lax.dot_general(a, b, (((ca,), (cb,)), ((), ())), preferred_element_type=F32)


def push_kernel(n_seq, n_fsdp, scope, gather, src, dst, send_sem, recv_sem, own_sem):
    me_s, me_f = lax.axis_index("seq"), lax.axis_index("fsdp")
    n = n_seq * n_fsdp if scope == "all" else n_seq
    me = me_s * n_fsdp + me_f if scope == "all" else me_s

    def where(index):
        if scope == "all":
            return (index // n_fsdp, index % n_fsdp)
        return (index, me_f)

    barrier = pltpu.get_barrier_semaphore()

    def greet(i, carry):
        pl.semaphore_signal(barrier, inc=1, device_id=where((me + i) % n), device_id_type=MESH)
        return carry

    lax.fori_loop(1, n, greet, 0)
    own = pltpu.make_async_copy(src if gather else src.at[me], dst.at[me], own_sem)
    own.start()
    pl.semaphore_wait(barrier, n - 1)

    def copy_to(other):
        return pltpu.make_async_remote_copy(
            src_ref=src if gather else src.at[other],
            dst_ref=dst.at[me],
            send_sem=send_sem.at[other],
            recv_sem=recv_sem.at[me],
            device_id=where(other),
            device_id_type=MESH,
        )

    def copy_from(other):
        return pltpu.make_async_remote_copy(
            src_ref=src if gather else src.at[other],
            dst_ref=dst.at[other],
            send_sem=send_sem.at[other],
            recv_sem=recv_sem.at[other],
            device_id=where(other),
            device_id_type=MESH,
        )

    def send(i, carry):
        copy_to((me + i) % n).start()
        return carry

    lax.fori_loop(1, n, send, 0)

    def finish(i, carry):
        other = (me + i) % n
        copy_from(other).wait_recv()
        copy_to(other).wait_send()
        return carry

    lax.fori_loop(1, n, finish, 0)
    own.wait()


def push(block, n_seq, n_fsdp, scope, gather, collective_id):
    n = n_seq * n_fsdp if scope == "all" else n_seq
    shape = (n,) + (block.shape if gather else block.shape[1:])
    return pl.pallas_call(
        functools.partial(push_kernel, n_seq, n_fsdp, scope, gather),
        out_shape=jax.ShapeDtypeStruct(shape, block.dtype),
        in_specs=[pl.BlockSpec(memory_space=pltpu.VMEM)],
        out_specs=pl.BlockSpec(memory_space=pltpu.VMEM),
        scratch_shapes=[
            pltpu.SemaphoreType.DMA((n,)),
            pltpu.SemaphoreType.DMA((n,)),
            pltpu.SemaphoreType.DMA,
        ],
        compiler_params=pltpu.CompilerParams(collective_id=collective_id, has_side_effects=True),
        name="push_" + scope,
    )(block)


def rows_of(flat, multiple):
    size = flat.shape[0]
    whole = -(-size // (multiple * 128)) * multiple * 128
    return jnp.pad(flat, (0, whole - size)).reshape(-1, 128)


def softmax_columns(k, q, length, scaling):
    scores = dot(k, q, 1, 1) * scaling
    key = lax.broadcasted_iota(jnp.int32, scores.shape, 0)
    scores = jnp.where(key < length, scores, -1e30)
    weights = jnp.exp(scores - jnp.max(scores, axis=0, keepdims=True))
    return weights / jnp.sum(weights, axis=0, keepdims=True)


def attend_kernel(scaling, length, q_ref, k_ref, v_ref, o_ref):
    probs = softmax_columns(k_ref[...], q_ref[...], length[0], scaling).astype(BF)
    o_ref[...] = dot(v_ref[...], probs, 0, 0).T.astype(BF)


def attend(query, key, value, length, block):
    slot_len, width = query.shape
    hd = 128
    return pl.pallas_call(
        functools.partial(attend_kernel, hd ** (-0.5)),
        out_shape=jax.ShapeDtypeStruct(query.shape, BF),
        grid_spec=pltpu.PrefetchScalarGridSpec(
            num_scalar_prefetch=1,
            grid=(width // hd, slot_len // block),
            in_specs=[
                pl.BlockSpec((block, hd), lambda h, i, n: (i, h)),
                pl.BlockSpec((slot_len, hd), lambda h, i, n: (0, h)),
                pl.BlockSpec((slot_len, hd), lambda h, i, n: (0, h)),
            ],
            out_specs=pl.BlockSpec((block, hd), lambda h, i, n: (i, h)),
        ),
        name="attend",
    )(length, query, key, value)


def attend_back_kernel(
    scaling, length, q_ref, k_ref, v_ref, g_ref, dq_ref, dk_ref, dv_ref, dk_sum, dv_sum
):
    step = pl.program_id(1)

    @pl.when(step == 0)
    def _():
        dk_sum[...] = jnp.zeros_like(dk_sum)
        dv_sum[...] = jnp.zeros_like(dv_sum)

    q, k, v, g = q_ref[...], k_ref[...], v_ref[...], g_ref[...]
    probs = softmax_columns(k, q, length[0], scaling)
    dv_sum[...] += dot(probs.astype(BF), g, 1, 0)
    weights_grad = dot(v, g, 1, 1)
    inner = jnp.sum(probs * weights_grad, axis=0, keepdims=True)
    score_grad = (probs * (weights_grad - inner) * scaling).astype(BF)
    dk_sum[...] += dot(score_grad, q, 1, 0)
    dq_ref[...] = dot(k, score_grad, 0, 0).T.astype(BF)

    @pl.when(step == pl.num_programs(1) - 1)
    def _():
        dk_ref[...] = dk_sum[...].astype(BF)
        dv_ref[...] = dv_sum[...].astype(BF)


def attend_back(query, key, value, grad, length, block):
    slot_len, width = query.shape
    hd = 128
    rows = pl.BlockSpec((block, hd), lambda h, i, n: (i, h))
    full = pl.BlockSpec((slot_len, hd), lambda h, i, n: (0, h))
    return pl.pallas_call(
        functools.partial(attend_back_kernel, hd ** (-0.5)),
        out_shape=[jax.ShapeDtypeStruct(query.shape, BF)] * 3,
        grid_spec=pltpu.PrefetchScalarGridSpec(
            num_scalar_prefetch=1,
            grid=(width // hd, slot_len // block),
            in_specs=[rows, full, full, rows],
            out_specs=[rows, full, full],
            scratch_shapes=[pltpu.VMEM((slot_len, hd), F32), pltpu.VMEM((slot_len, hd), F32)],
        ),
        name="attend_back",
    )(length, query, key, value, grad)


def rope_tables(positions, head_dim):
    half = head_dim // 2
    frequency = rope_base ** (-jnp.arange(half, dtype=F32) * 2.0 / head_dim)
    angles = positions.astype(F32)[:, None] * frequency[None, :]
    return jnp.cos(angles)[:, None, :], jnp.sin(angles)[:, None, :]


def rotate(values, cosine, sine):
    half = values.shape[-1] // 2
    a, b = values[..., :half], values[..., half:]
    return jnp.concatenate([a * cosine - b * sine, b * cosine + a * sine], axis=-1)


def rotate_back(values, cosine, sine):
    return rotate(values, cosine, -sine)


def places(block_routes, experts, capacity):
    count = block_routes.shape[0]
    match = (block_routes[:, :, None] == experts[None, None, :]).astype(F32).sum(axis=1)
    lower = jnp.tril(jnp.ones((count, count), BF), -1)
    rank = dot(lower, match.astype(BF), 1, 0)
    place = jnp.arange(capacity, dtype=F32)
    return match[:, :, None] * (rank[:, :, None] == place[None, None, :]).astype(F32)


def local(
    tokens,
    cotangent,
    lengths,
    routes,
    norm_gains,
    qkv_weight,
    proj_weight,
    router_weight,
    expert_up,
    expert_down,
):
    n_seq, n_fsdp = lax.axis_size("seq"), lax.axis_size("fsdp")
    n_dev = n_seq * n_fsdp
    me_s, me_f = lax.axis_index("seq"), lax.axis_index("fsdp")
    shard_len, width = tokens.shape[1], tokens.shape[2]
    slot_len = shard_len * n_seq
    experts = router_weight.shape[1]
    top_count = routes.shape[2]
    capacity = 3 * shard_len * top_count // (2 * experts)
    piece_ff = expert_down.shape[1]
    pieces_dev = expert_up.shape[0]
    split = FF // piece_ff
    head_dim = width // HEADS
    head_width = width // n_seq
    heads_dev = HEADS // n_seq
    owned = qkv_weight.shape[0]
    block = min(512, slot_len)
    length = lax.dynamic_slice_in_dim(lengths, me_f, 1)
    valid_total = jnp.sum(lengths).astype(F32).reshape(1)
    positions = me_s * shard_len + jnp.arange(shard_len, dtype=jnp.int32)
    row_valid = (positions < length[0]).astype(F32)
    local_routes = routes[0]
    push_all = functools.partial(push, n_seq=n_seq, n_fsdp=n_fsdp, scope="all")
    push_seq = functools.partial(push, n_seq=n_seq, n_fsdp=n_fsdp, scope="seq")

    gain_size, router_size = norm_gains.size, router_weight.size
    pieces = [norm_gains.reshape(-1), router_weight.reshape(-1), local_routes.astype(BF).reshape(-1)]
    small = push_all(rows_of(jnp.concatenate(pieces), 16), gather=True, collective_id=0)
    small = small.reshape(n_dev, -1)
    gains = small[:, :gain_size].reshape(n_dev, 4, owned).swapaxes(0, 1).reshape(4, width).astype(F32)
    router = small[:, gain_size : gain_size + router_size].reshape(width, experts)
    all_routes = small[:, gain_size + router_size :][:, : shard_len * top_count]
    all_routes = all_routes.reshape(n_seq, n_fsdp, shard_len, top_count).astype(jnp.int32)

    slot_tokens = lax.all_gather(tokens[0], "seq", axis=0, tiled=True)
    qkv_parts = qkv_weight.reshape(owned, 3, n_seq, head_width)
    qkv_parts = lax.all_to_all(qkv_parts, "seq", split_axis=2, concat_axis=0, tiled=True)
    qkv_parts = qkv_parts.reshape(n_seq, owned, 3 * head_width)
    qkv_local = lax.all_gather(qkv_parts, "fsdp", axis=1).reshape(width, 3 * head_width)
    full_proj = lax.all_gather(proj_weight, ("seq", "fsdp"), axis=0, tiled=True)
    masked_low = jnp.where(row_valid[:, None] > 0, cotangent[0], jnp.zeros((), BF))
    plane_masked = lax.all_gather(masked_low, "fsdp", axis=0, tiled=True)

    plane_routes = lax.dynamic_index_in_dim(all_routes, me_s, 0, keepdims=False)
    piece_ids = (jnp.arange(n_seq)[:, None] * n_fsdp + me_f) * pieces_dev + jnp.arange(pieces_dev)
    plane_experts = (piece_ids // split).reshape(-1).astype(jnp.int32)
    plane_hot = jax.vmap(lambda r: places(r, plane_experts, capacity))(plane_routes)
    block_row = jnp.arange(n_fsdp * shard_len, dtype=F32).reshape(n_fsdp, shard_len)
    plane_index = jnp.einsum("ft,ftec->efc", block_row, plane_hot, precision=lax.Precision.HIGHEST)
    plane_index = plane_index.astype(jnp.int32).reshape(n_seq, pieces_dev, n_fsdp, capacity)
    gather_hot = plane_hot.reshape(n_fsdp, shard_len, n_seq, pieces_dev, capacity).astype(BF)

    def dispatch(plane_rows, piece):
        index = plane_index[:, piece].reshape(-1)
        rows = plane_rows[index].reshape(n_seq, n_fsdp * capacity, width)
        return lax.all_to_all(rows, "seq", split_axis=0, concat_axis=0, tiled=True).reshape(-1, width)

    def combine(pieces_rows):
        total = 0.0
        for piece, rows in enumerate(pieces_rows):
            back = lax.all_to_all(
                rows.reshape(n_seq, n_fsdp * capacity, width), "seq", split_axis=0, concat_axis=0, tiled=True
            )
            back = back.reshape(n_seq, n_fsdp, capacity, width)
            total = total + jnp.einsum(
                "ftsc,sfcd->ftd", gather_hot[:, :, :, piece], back, preferred_element_type=F32
            )
        parts = lax.all_to_all(total.astype(BF), "fsdp", split_axis=0, concat_axis=0, tiled=True)
        return jnp.sum(parts.astype(F32), axis=0)

    def rms(values):
        return lax.rsqrt(jnp.mean(values * values, axis=-1, keepdims=True) + epsilon)

    slot_f32 = slot_tokens.astype(F32)
    normed_one = (slot_f32 * rms(slot_f32) * gains[0]).astype(BF)
    raw = jnp.dot(normed_one, qkv_local, preferred_element_type=F32)
    raw_query, raw_key, raw_value = jnp.split(raw, 3, axis=1)

    def seq_sums(first, second, collective_id):
        sums = jnp.stack([jnp.sum(first, axis=-1), jnp.sum(second, axis=-1)])
        every = push_seq(sums.reshape(-1, 128), gather=True, collective_id=collective_id)
        total = jnp.sum(every, axis=0).reshape(2, slot_len)
        return total[0][:, None], total[1][:, None]

    query_square, key_square = seq_sums(raw_query * raw_query, raw_key * raw_key, 1)
    query_rms = lax.rsqrt(query_square / width + epsilon)
    key_rms = lax.rsqrt(key_square / width + epsilon)
    own_gains = lax.dynamic_slice_in_dim(gains, me_s * head_width, head_width, 1)
    cosine, sine = rope_tables(jnp.arange(slot_len, dtype=jnp.int32), head_dim)

    def heads(values):
        return values.reshape(slot_len, heads_dev, head_dim)

    query = rotate(heads(raw_query * query_rms * own_gains[1]), cosine, sine)
    key = rotate(heads(raw_key * key_rms * own_gains[2]), cosine, sine)
    query = query.astype(BF).reshape(slot_len, head_width)
    key = key.astype(BF).reshape(slot_len, head_width)
    value = raw_value.astype(BF)
    attended = attend(query, key, value, length, block)
    attended_tok = lax.all_to_all(attended, "seq", split_axis=0, concat_axis=1, tiled=True)

    resid_in = tokens[0].astype(F32)
    resid_mid = resid_in + jnp.dot(attended_tok, full_proj, preferred_element_type=F32)
    mid_rms = rms(resid_mid)
    normed_two = (resid_mid * mid_rms * gains[3]).astype(BF)
    plane_rows = lax.all_gather(normed_two, "fsdp", axis=0, tiled=True)
    router_probs = jax.nn.softmax(jnp.dot(normed_two, router, preferred_element_type=F32), axis=-1)

    own_hot = places(local_routes, jnp.arange(experts, dtype=jnp.int32), capacity)
    gate_slot = jnp.sum(own_hot * router_probs[:, :, None], axis=0)
    gate_send = jnp.broadcast_to(gate_slot[:, None], (experts, split, capacity))
    gate_send = gate_send.reshape(n_dev, pieces_dev * capacity)
    gate_pad = -pieces_dev * capacity % 1024
    gate_send = jnp.pad(gate_send, ((0, 0), (0, gate_pad))).reshape(n_dev, -1, 128)
    gate_recv = push_all(gate_send, gather=False, collective_id=2)
    gate_recv = gate_recv.reshape(n_dev, -1)[:, : pieces_dev * capacity]
    gate_recv = gate_recv.reshape(n_dev, pieces_dev, capacity)

    outs, backs, gate_backs, up_grads, down_grads = [], [], [], [], []
    for piece in range(pieces_dev):
        gate_rows = gate_recv[:, piece].reshape(-1, 1)
        cot_rows = dispatch(plane_masked, piece)
        rows = dispatch(plane_rows, piece)
        up, down = expert_up[piece], expert_down[piece]
        hidden = jnp.dot(rows, up, preferred_element_type=F32)
        gate_pre, up_pre = hidden[:, :piece_ff], hidden[:, piece_ff:]
        sigmoid = jax.nn.sigmoid(gate_pre)
        activation = (gate_pre * sigmoid * up_pre).astype(BF)
        piece_out = jnp.dot(activation, down, preferred_element_type=F32).astype(BF).astype(F32)
        outs.append((piece_out * gate_rows).astype(BF))
        cot_f32 = cot_rows.astype(F32)
        gate_backs.append(jnp.sum(piece_out * cot_f32, axis=-1).reshape(n_dev, capacity))
        out_grad = (cot_f32 * gate_rows).astype(BF)
        act_grad = dot(out_grad, down, 1, 1)
        down_grads.append(dot(activation, out_grad, 0, 0))
        gate_grad = act_grad * up_pre * sigmoid * (1.0 + gate_pre * (1.0 - sigmoid))
        up_part = act_grad * gate_pre * sigmoid
        hidden_grad = jnp.concatenate([gate_grad, up_part], axis=-1).astype(BF)
        up_grads.append(dot(rows, hidden_grad, 0, 0))
        backs.append(dot(hidden_grad, up, 1, 1).astype(BF))
    up_grad = jnp.stack(up_grads)
    down_grad = jnp.stack(down_grads)
    normed_two_grad = combine(backs)
    layer_out = (resid_mid + combine(outs)).astype(BF)[None]

    counts = jnp.sum(
        (all_routes[..., None] == jnp.arange(experts, dtype=jnp.int32))
        * (
            jnp.arange(slot_len, dtype=jnp.int32).reshape(n_seq, 1, shard_len)
            < lengths[None, :, None]
        )[..., None, None].astype(F32),
        axis=(0, 1, 2, 3),
    )
    fraction = counts / (top_count * valid_total)
    back_send = jnp.stack(gate_backs, axis=1).reshape(n_dev, pieces_dev * capacity)
    back_send = jnp.pad(back_send, ((0, 0), (0, gate_pad))).reshape(n_dev, -1, 128)
    back_recv = push_all(back_send, gather=False, collective_id=3).reshape(n_dev, -1)
    slot_gates_grad = back_recv[:, : pieces_dev * capacity].reshape(experts, split, capacity).sum(axis=1)
    probs_grad = (
        jnp.sum(own_hot * slot_gates_grad[None], axis=2)
        + (experts * fraction / valid_total)[None, :] * row_valid[:, None]
    )
    logits_grad = router_probs * (
        probs_grad - jnp.sum(router_probs * probs_grad, axis=-1, keepdims=True)
    )
    router_term = lax.dot_general(
        normed_two.astype(F32), logits_grad, (((0,), (0,)), ((), ())), precision=lax.Precision.HIGHEST
    )
    normed_two_grad = normed_two_grad + lax.dot_general(
        logits_grad, router.astype(F32), (((1,), (1,)), ((), ())), precision=lax.Precision.HIGHEST
    )

    def rms_back(values, scale, gain, grad):
        weighted = gain * grad
        mean = jnp.mean(weighted * values, axis=-1, keepdims=True)
        return scale * weighted - values * (scale * scale * scale) * mean, jnp.sum(
            grad * values * scale, axis=0
        )

    mid_part, gain_three = rms_back(resid_mid, mid_rms, gains[3], normed_two_grad)
    mid_grad = masked_low.astype(F32) + mid_part
    branch_grad = mid_grad.astype(BF)
    slot_branch = lax.all_gather(branch_grad, "seq", axis=0, tiled=True)
    attended_grad = dot(branch_grad, full_proj, 1, 1).astype(BF)
    heads_grad = lax.all_to_all(attended_grad, "seq", split_axis=1, concat_axis=0, tiled=True)
    query_grad, key_grad, value_grad = attend_back(query, key, value, heads_grad, length, block)

    query_in = rotate_back(heads(query_grad.astype(F32)), cosine, sine).reshape(slot_len, head_width)
    key_in = rotate_back(heads(key_grad.astype(F32)), cosine, sine).reshape(slot_len, head_width)
    query_weighted, key_weighted = query_in * own_gains[1], key_in * own_gains[2]
    query_dot, key_dot = seq_sums(query_weighted * raw_query, key_weighted * raw_key, 4)
    raw_query_grad = query_rms * query_weighted - raw_query * (query_rms**3) * (query_dot / width)
    raw_key_grad = key_rms * key_weighted - raw_key * (key_rms**3) * (key_dot / width)
    gain_one = jnp.sum(query_in * raw_query * query_rms, axis=0)
    gain_two = jnp.sum(key_in * raw_key * key_rms, axis=0)
    raw_grad = jnp.concatenate(
        [raw_query_grad.astype(BF), raw_key_grad.astype(BF), value_grad], axis=1
    )
    one_part = dot(raw_grad, qkv_local, 1, 1).astype(BF)
    one_grad = lax.psum_scatter(one_part, "seq", scatter_dimension=0, tiled=True).astype(F32)
    input_part, gain_zero = rms_back(resid_in, rms(resid_in), gains[0], one_grad)
    input_grad = (mid_grad + input_part).astype(BF)[None]

    qkv_part = dot(normed_one, raw_grad, 0, 0).astype(BF)
    qkv_part = qkv_part.reshape(n_seq, n_fsdp, owned, 3 * head_width)
    qkv_part = lax.psum_scatter(qkv_part, "fsdp", scatter_dimension=1, tiled=True)
    qkv_part = qkv_part.reshape(n_seq, owned, 3, head_width)
    qkv_part = lax.all_to_all(qkv_part, "seq", split_axis=0, concat_axis=0, tiled=True)
    qkv_grad = qkv_part.transpose(1, 2, 0, 3).reshape(owned, 3 * width).astype(F32)
    proj_part = dot(attended, slot_branch, 0, 0).astype(BF)
    proj_grad = lax.psum_scatter(proj_part, "fsdp", scatter_dimension=0, tiled=True).astype(F32)

    prob_part = jnp.sum(router_probs * row_valid[:, None], axis=0)
    heads_gain = jnp.stack([gain_one, gain_two]).reshape(2, n_fsdp, owned).swapaxes(0, 1)
    same_seq = (jnp.arange(n_seq) == me_s).astype(F32)[:, None, None, None]
    heads_gain = (same_seq * heads_gain[None]).reshape(n_dev, 2 * owned)
    last = jnp.concatenate(
        [
            router_term.reshape(n_dev, owned * experts),
            gain_zero.reshape(n_dev, owned),
            gain_three.reshape(n_dev, owned),
            heads_gain,
            jnp.broadcast_to(prob_part[None], (n_dev, experts)),
        ],
        axis=1,
    )
    last_size = last.shape[1]
    last = jnp.pad(last, ((0, 0), (0, -last_size % 1024))).reshape(n_dev, -1, 128)
    last = push_all(last, gather=False, collective_id=5)
    last = jnp.sum(last, axis=0).reshape(-1)
    cut = owned * experts
    router_grad = last[:cut].reshape(owned, experts)
    gains_grad = jnp.stack(
        [
            last[cut : cut + owned],
            last[cut + 2 * owned : cut + 3 * owned],
            last[cut + 3 * owned : cut + 4 * owned],
            last[cut + owned : cut + 2 * owned],
        ]
    )
    prob_total = last[cut + 4 * owned : cut + 4 * owned + experts]
    loss_value = (experts * jnp.sum(fraction * prob_total / valid_total)).reshape(1)
    return (
        layer_out,
        input_grad,
        gains_grad,
        qkv_grad,
        proj_grad,
        router_grad,
        up_grad,
        down_grad,
        loss_value,
    )


def solution(mesh):
    rows = P(("seq", "fsdp"), None)
    return jax.shard_map(
        local,
        mesh=mesh,
        in_specs=(
            P("fsdp", "seq", None),
            P("fsdp", "seq", None),
            P(),
            P("fsdp", "seq", None),
            P(None, ("seq", "fsdp")),
            rows,
            rows,
            rows,
            P(("seq", "fsdp"), None, None),
            P(("seq", "fsdp"), None, None),
        ),
        out_specs=(
            P("fsdp", "seq", None),
            P("fsdp", "seq", None),
            P(None, ("seq", "fsdp")),
            rows,
            rows,
            rows,
            P(("seq", "fsdp"), None, None),
            P(("seq", "fsdp"), None, None),
            P(),
        ),
        check_vma=False,
    )
```

time: 1720 us -> 1020 us (0.59)
  waiting for transfers between devices: 888 us -> 464 us
  blocking collectives: 348 us -> 17.7 us
  Pallas kernels: 0 us -> 119 us
  matrix products: 210 us -> 149 us
    all_gather x2 -> x0, blocking collectives: 265 us -> none  [the longest x1 194 us: local(): lax.all_gather(router_weight, ('seq', 'fsdp'), axis=0, tiled=True)]
    reduce_scatter x3, waiting for transfers between devices: 239 us -> 19.1 us  [the longest x1 9.86 us: local(): lax.psum_scatter(qkv_part, 'fsdp', scatter_dimension=1, tiled=True)]
    all_to_all x12 -> x13, waiting for transfers between devices: 422 us -> 279 us  [the longest x4 111 us: combine(): lax.all_to_all(rows.reshape(n_seq, n_fsdp * capacity, width), 'seq', spli...]
    pallas_call x0 -> x8, Pallas kernels: none -> 119 us  [the longest x6 99 us: push(): pl.pallas_call(functools.partial(push_kernel, n_seq, n_fsdp, scope, gathe...]
    psum x2 -> x0, blocking collectives: 82.9 us -> none  [local(): count_total, prob_total = lax.psum((count_part, prob_part), ('seq', 'fsdp'))]
    dot_general x29 -> x27, matrix products: 210 us -> 149 us  [the longest x13 85 us: dot(): lax.dot_general(a, b, (((ca,), (cb,)), ((), ())), preferred_element_type=...]
    unnamed x11 -> x9, waiting for transfers between devices: 49.1 us -> 1.49 us
    gather x8 -> x4, local copies, waits for them, and re-layouts: 49.8 us -> 31.3 us  [dispatch(): rows = plane_rows[index].reshape(n_seq, n_fsdp * capacity, width)]
  transfers between devices with their start and end apart: 22 -> 22, of which waited for: 16 -> 19; matrix products, arithmetic and copies ran while one was open for 21% -> 27% of each run, Pallas kernels for 0% -> 10%
where the time goes in v1:
time: 1020 us
  waiting for transfers between devices  464 us (45%)
  matrix products  149 us (15%)
  Pallas kernels  119 us (12%)
  other arithmetic  95.9 us (9%)
  local copies, waits for them, and re-layouts  94.1 us (9%)
  starting transfers between devices  57.1 us (6%)
  between operations  18.2 us (2%)
  blocking collectives  17.7 us (2%)
    all_to_all x4, waiting for transfers between devices, combine(): lax.all_to_all(rows.reshape(n_seq, n_fsdp * capacity, width), 'seq', spli...  111 us
    pallas_call x6, Pallas kernels, push(): pl.pallas_call(functools.partial(push_kernel, n_seq, n_fsdp, scope, gathe...  99 us
    dot_general x13, matrix products, dot(): lax.dot_general(a, b, (((ca,), (cb,)), ((), ())), preferred_element_type=...  85 us
    all_to_all x2, waiting for transfers between devices, combine(): lax.all_to_all(total.astype(BF), 'fsdp', split_axis=0, concat_axis=0, til...  81.6 us
    all_to_all x4, waiting for transfers between devices, dispatch(): lax.all_to_all(rows, 'seq', split_axis=0, concat_axis=0, tiled=True)  61.3 us
    all_gather x1, waiting for transfers between devices, local(): plane_masked = lax.all_gather(masked_low, 'fsdp', axis=0, tiled=True)  38.8 us
    all_gather x1, waiting for transfers between devices, local(): plane_rows = lax.all_gather(normed_two, 'fsdp', axis=0, tiled=True)  33.5 us
    all_gather x1, waiting for transfers between devices, local(): slot_tokens = lax.all_gather(tokens[0], 'seq', axis=0, tiled=True)  33.3 us
  transfers between devices with their start and end apart: 22, of which 19 were waited for; matrix products, arithmetic and copies ran while one was open for 27% of the time, Pallas kernels for 10%

profile of v1, /device:TPU:0, one launch (start us, length us, event | category | flops | bytes accessed | tf_op | source)
XLA Modules:
  0.0 1015.2 jit_solution(2046066390384978084)
XLA Ops:
  8.7 17.7 %all_to_all.108 = bf16[64,3,8,256]{3,0,1,2:T(8,128)(2,1)S(1)} all-to-all(bf16[64,3,8,256]{3,0,1,2:T(8,128)(2,1)S(1)} %copy.225), channel_id=1, replica_groups=mesh['seq'=8,'fsdp'=4] {'seq'}, dimensions={2} | all-to-all | bytes 1572864 | tf_op jit(solution)/shard_map/all_to_all | solution.py:255
  34.6 26.2 %push_all.4 = bf16[32,48,128]{2,1,0:T(8,128)(2,1)} custom-call(bf16[48,128]{1,0:T(8,128)(2,1)} %fusion.100.src), custom_call_target="tpu_custom_call" | custom-call | tf_op jit(solution)/shard_map/push_all/pallas_call | solution.py:84
  68.8 31.3 %all-gather.8.cloned.1.call-done = bf16[8,4,64,768]{3,2,0,1:T(8,128)(2,1)} async-done(((bf16[8,1,64,768]{3,2,0,1:T(8,128)(2,1)}), bf16[8,4,64,768]{3,2,0,1:T(8,128)(2,1)}) %all-gather.8.cloned.1.call-update) | async-done | bytes 3145744 | tf_op jit(solution)/shard_map/all_gather | solution.py:257
  103.9 33.3 %all-gather.18.cloned.1.call-done = bf16[1,1024,2048]{2,1,0:T(8,128)(2,1)} async-done(((bf16[1,128,2048]{2,1,0:T(8,128)(2,1)}), bf16[1,1024,2048]{2,1,0:T(8,128)(2,1)}) %all-gather.18.cloned.1.call-update) | async-done | bytes 4194320 | tf_op jit(solution)/shard_map/all_gather | solution.py:253
  148.2 6.5 push_seq.2
  169.0 7.4 attend.1
  186.8 5.5 all-to-all-done.1
  192.3 27.1 %all-gather.10.cloned.1.call-done = bf16[2048,2048]{1,0:T(8,128)(2,1)} async-done(((bf16[64,2048]{1,0:T(8,128)(2,1)}), bf16[2048,2048]{1,0:T(8,128)(2,1)}) %all-gather.10.cloned.1.call-update) | async-done | bytes 8388624 | tf_op jit(solution)/shard_map/all_gather | solution.py:258
  226.5 38.8 %all-gather.14.cloned.1.call-done = bf16[512,2048]{1,0:T(8,128)(2,1)} async-done(((bf16[128,2048]{1,0:T(8,128)(2,1)}), bf16[512,2048]{1,0:T(8,128)(2,1)}) %all-gather.14.cloned.1.call-update) | async-done | bytes 2097168 | tf_op jit(solution)/shard_map/all_gather | solution.py:260
  265.3 8.9 gather_fusion.3
  277.9 33.5 %all-gather.12.cloned.1.call-done = bf16[512,2048]{1,0:T(8,128)(2,1)} async-done(((bf16[128,2048]{1,0:T(8,128)(2,1)}), bf16[512,2048]{1,0:T(8,128)(2,1)}) %all-gather.12.cloned.1.call-update) | async-done | bytes 2097168 | tf_op jit(solution)/shard_map/all_gather | solution.py:324
  311.4 9.1 gather_fusion.1
  332.8 9.0 gather_fusion
  341.7 23.3 %all-to-all-done.4 = bf16[8,96,2048]{2,1,0:T(8,128)(2,1)} async-done(((bf16[8,96,2048]{2,1,0:T(8,128)(2,1)}), bf16[8,96,2048]{2,1,0:T(8,128)(2,1)}, u32[]{:S(2)}, u32[]{:S(2)}) %all-to-all-start.4) | async-done | bytes 3145760 | tf_op jit(solution)/shard_map/all_to_all | solution.py:274
  368.8 10.0 fusion.5
  383.7 22.8 %all-to-all-done.2 = bf16[8,96,2048]{2,1,0:T(8,128)(2,1)S(1)} async-done(((bf16[8,96,2048]{2,1,0:T(8,128)(2,1)}), bf16[8,96,2048]{2,1,0:T(8,128)(2,1)S(1)}, u32[]{:S(2)}, u32[]{:S(2)}) %all-to-all-start.2) | async-done | bytes 3145760 | tf_op jit(solution)/shard_map/all_to_all | solution.py:274
  413.1 7.7 fusion.18
  420.9 10.0 fusion.9
  435.8 15.1 %all-to-all-done.7 = bf16[8,96,2048]{2,1,0:T(8,128)(2,1)} async-done(((bf16[8,96,2048]{2,1,0:T(8,128)(2,1)}), bf16[8,96,2048]{2,1,0:T(8,128)(2,1)}, u32[]{:S(2)}, u32[]{:S(2)}) %all-to-all-start.7) | async-done | bytes 3145760 | tf_op jit(solution)/shard_map/all_to_all | solution.py:274
  451.0 8.7 fusion.16
  462.6 10.1 push_all.6
  475.5 11.2 %push_all.5 = f32[32,8,128]{2,1,0:T(8,128)} custom-call(f32[32,8,128]{2,1,0:T(8,128)} %bitcast.330), custom_call_target="tpu_custom_call" | custom-call | tf_op jit(solution)/shard_map/push_all/pallas_call | solution.py:84
  493.3 6.5 multiply_convert_fusion.3
  499.8 11.4 %fusion.43 = bf16[768,2048]{1,0:T(8,128)(2,1)} fusion(bf16[2,2048,2048]{2,1,0:T(8,128)(2,1)} %param.18, bf16[768,1024]{1,0:T(8,128)(2,1)S(1)} %get-tuple-element.40, bf16[768,1024]{1,0:T(8,128)(2,1)S(1)} %get-tuple-element.39), kind=kOutput, calls=%fused_computation.67 | convolution fusion | flops 6450315264 | bytes 14680064 | tf_op jit(solution)/shard_map/dot_general | solution.py:21
  516.8 7.9 multiply_convert_fusion.1
  526.3 8.1 fusion.46
  534.4 19.5 %all-to-all-done.8 = bf16[8,96,2048]{2,1,0:T(8,128)(2,1)} async-done(((bf16[8,96,2048]{2,1,0:T(8,128)(2,1)}), bf16[8,96,2048]{2,1,0:T(8,128)(2,1)}, u32[]{:S(2)}, u32[]{:S(2)}) %all-to-all-start.8) | async-done | bytes 3145760 | tf_op jit(solution)/shard_map/all_to_all | solution.py:279
  558.4 8.0 fusion.22
  566.5 29.8 %all-to-all-done.10 = bf16[8,96,2048]{2,1,0:T(8,128)(2,1)} async-done(((bf16[8,96,2048]{2,1,0:T(8,128)(2,1)}), bf16[8,96,2048]{2,1,0:T(8,128)(2,1)}, u32[]{:S(2)}, u32[]{:S(2)}) %all-to-all-start.10) | async-done | bytes 3145760 | tf_op jit(solution)/shard_map/all_to_all | solution.py:279
  600.8 6.8 fusion.20
  607.6 31.0 %all-to-all-done.3 = bf16[8,96,2048]{2,1,0:T(8,128)(2,1)} async-done(((bf16[8,96,2048]{2,1,0:T(8,128)(2,1)}), bf16[8,96,2048]{2,1,0:T(8,128)(2,1)}, u32[]{:S(2)}, u32[]{:S(2)}) %all-to-all-start.3) | async-done | bytes 3145760 | tf_op jit(solution)/shard_map/all_to_all | solution.py:279
  649.2 31.0 %all-to-all-done.5 = bf16[8,96,2048]{2,1,0:T(8,128)(2,1)S(1)} async-done(((bf16[8,96,2048]{2,1,0:T(8,128)(2,1)}), bf16[8,96,2048]{2,1,0:T(8,128)(2,1)S(1)}, u32[]{:S(2)}, u32[]{:S(2)}) %all-to-all-start.5) | async-done | bytes 3145760 | tf_op jit(solution)/shard_map/all_to_all | solution.py:279
  689.6 40.9 %all-to-all-done.11 = bf16[4,128,2048]{2,1,0:T(8,128)(2,1)} async-done(((bf16[4,128,2048]{2,1,0:T(8,128)(2,1)}), bf16[4,128,2048]{2,1,0:T(8,128)(2,1)}, u32[]{:S(2)}, u32[]{:S(2)}) %all-to-all-start.11) | async-done | bytes 2097184 | tf_op jit(solution)/shard_map/all_to_all | solution.py:286
  742.0 40.7 %all-to-all-done.6 = bf16[4,128,2048]{2,1,0:T(8,128)(2,1)} async-done(((bf16[4,128,2048]{2,1,0:T(8,128)(2,1)}), bf16[4,128,2048]{2,1,0:T(8,128)(2,1)}, u32[]{:S(2)}, u32[]{:S(2)}) %all-to-all-start.6) | async-done | bytes 2097184 | tf_op jit(solution)/shard_map/all_to_all | solution.py:286
  786.7 6.5 convolution_convert_fusion.3
  799.3 10.4 %all-to-all-done.12 = bf16[128,8,256]{2,0,1:T(8,128)(2,1)S(1)} async-done(((bf16[128,8,256]{2,0,1:T(8,128)(2,1)}), bf16[128,8,256]{2,0,1:T(8,128)(2,1)S(1)}, u32[]{:S(2)}, u32[]{:S(2)}) %all-to-all-start.12) | async-done | bytes 524320 | tf_op jit(solution)/shard_map/all_to_all | solution.py:403
  810.5 12.9 %attend_back.1 = (bf16[1024,256]{1,0:T(8,128)(2,1)}, bf16[1024,256]{1,0:T(8,128)(2,1)}, bf16[1024,256]{1,0:T(8,128)(2,1)}) custom-call(s32[1]{0:T(128)} %dynamic_slice.10.length, bf16[1024,256]{1,0:T(8,128)(2,1)} %bitcast.300, bf16[1024,256]{1,0:T(8,128)(2,1)} %bitcast.302, bf16[1024,256]{1,0:T(8,128)(2,1)} %split.27.v_ref, bf16[1024,256]{1,0:T(8,128)(2,1)} %bitcast.317), custom_call_target="tpu_custom_call" | custom-call | tf_op jit(solution)/shard_map/attend_back/pallas_call | solution.py:168
  833.9 6.0 push_seq.3
  851.1 6.1 convolution_convert_fusion.1
  860.6 5.8 convolution_bitcast_fusion.2
  870.0 6.4 pad_maximum_fusion.1
  876.4 9.1 convolution_bitcast_fusion
  885.5 10.6 %convolution_bitcast_fusion.1 = f32[1,2048,2048]{2,1,0:T(8,128)} fusion(bf16[768,2048]{1,0:T(8,128)(2,1)S(1)} %bitcast.308, bf16[768,1024]{1,0:T(8,128)(2,1)S(1)} %copy-done.88, bf16[768,1024]{1,0:T(8,128)(2,1)S(1)} %copy-done.86), kind=kOutput, calls=%fused_computation.9 | convolution fusion | flops 6448742400 | bytes 23068672 | tf_op jit(solution)/shard_map/dot_general | solution.py:21
  896.1 18.9 %pad_maximum_fusion = f32[2,2048,2048]{2,1,0:T(8,128)} fusion(f32[1,2048,2048]{2,1,0:T(8,128)S(1)} %convolution_bitcast_fusion, f32[1,2048,2048]{2,1,0:T(8,128)} %convolution_bitcast_fusion.1), kind=kLoop, calls=%fused_computation.4 | loop fusion | flops 8388608 | bytes 67108864 | tf_op jit(solution)/shard_map/stack | solution.py:359
  923.7 39.0 %push_all.7 = f32[32,40,128]{2,1,0:T(8,128)} custom-call(f32[32,40,128]{2,1,0:T(8,128)} %bitcast.315), custom_call_target="tpu_custom_call" | custom-call | tf_op jit(solution)/shard_map/push_all/pallas_call | solution.py:84
  963.9 9.9 reduce-scatter.6.cloned.1.call-done
  984.8 8.8 all-to-all-done.13
  996.3 9.2 reduce-scatter.8.cloned.1.call-done
  (401 shorter events, 222.6 us)
Async XLA Ops:
  7.2 92.9 %all-gather.8.cloned.1.call-start = ((), (), s32[]{:S(2)}) async-start(), calls=%async_computation.17 | async-start | bytes 3932160 | tf_op jit(solution)/shard_map/all_gather | solution.py:257
  8.7 21.6 %copy-start.77 = (s32[4]{0:T(128)S(1)}, s32[4]{0:T(128)}, u32[]{:S(2)}) copy-start(s32[4]{0:T(128)} %param.12) | copy-start | bytes 52
  8.7 23.9 %copy-start.33 = (bf16[1,128,2048]{2,1,0:T(8,128)(2,1)S(1)}, bf16[1,128,2048]{2,1,0:T(8,128)(2,1)}, u32[]{:S(2)}) copy-start(bf16[1,128,2048]{2,1,0:T(8,128)(2,1)} %param.11) | copy-start | bytes 1572868
  28.8 108.4 %all-gather.18.cloned.1.call-start = ((), (), s32[]{:S(2)}) async-start(), calls=%async_computation.25 | async-start | bytes 4718592 | tf_op jit(solution)/shard_map/all_gather | solution.py:253
  29.5 189.9 %all-gather.10.cloned.1.call-start = ((), (), s32[]{:S(2)}) async-start(), calls=%async_computation.18 | async-start | bytes 8650752 | tf_op jit(solution)/shard_map/all_gather | solution.py:258
  30.2 235.1 %all-gather.14.cloned.1.call-start = ((), (), s32[]{:S(2)}) async-start(), calls=%async_computation.20 | async-start | bytes 2621440 | tf_op jit(solution)/shard_map/all_gather | solution.py:260
  63.4 77.1 %copy-start.50 = (f32[2048]{0:T(1024)}, f32[2048]{0:T(1024)S(1)}, u32[]{:S(2)}) copy-start(f32[2048]{0:T(1024)S(1)} %mul.765) | copy-start | bytes 24580
  64.6 39.4 %copy-start.9 = (s32[8,4,128,8]{3,2,1,0:T(8,128)}, s32[8,4,128,8]{3,2,1,0:T(8,128)S(1)}, u32[]{:S(2)}) copy-start(s32[8,4,128,8]{3,2,1,0:T(8,128)S(1)} %reshape.635) | copy-start | bytes 393220
  68.8 86.8 %copy-start.65 = (f32[1,256]{1,0:T(1,128)}, f32[1,256]{1,0:T(1,128)S(1)}, u32[]{:S(2)}) copy-start(f32[1,256]{1,0:T(1,128)S(1)} %get-tuple-element.62) | copy-start | bytes 3076
  68.8 86.8 %copy-start.67 = (f32[1,256]{1,0:T(1,128)}, f32[1,256]{1,0:T(1,128)S(1)}, u32[]{:S(2)}) copy-start(f32[1,256]{1,0:T(1,128)S(1)} %get-tuple-element.63) | copy-start | bytes 3076
  168.1 51.3 %copy-start.7 = (bf16[1,128,2048]{2,1,0:T(8,128)(2,1)S(1)}, bf16[1,128,2048]{2,1,0:T(8,128)(2,1)}, u32[]{:S(2)}) copy-start(bf16[1,128,2048]{2,1,0:T(8,128)(2,1)} %param.10) | copy-start | bytes 1572868
  178.5 13.8 %all-to-all-start.1 = ((bf16[8,128,256]{1,2,0:T(8,128)(2,1)}), bf16[8,128,256]{1,2,0:T(8,128)(2,1)S(1)}, u32[]{:S(2)}, u32[]{:S(2)}) async-start(bf16[8,128,256]{1,2,0:T(8,128)(2,1)} %copy.231), calls=%async_computation.1 | async-start | bytes 1048576 | tf_op jit(solution)/shard_map/all_to_all | solution.py:318
  182.0 129.4 %all-gather.12.cloned.1.call-start = ((), (), s32[]{:S(2)}) async-start(), calls=%async_computation.19 | async-start | bytes 2621440 | tf_op jit(solution)/shard_map/all_gather | solution.py:324
  182.4 42.4 %copy-start.48 = (f32[2048]{0:T(1024)}, f32[2048]{0:T(1024)S(1)}, u32[]{:S(2)}) copy-start(f32[2048]{0:T(1024)S(1)} %mul.802) | copy-start | bytes 24580
  182.6 41.6 %copy-start.60 = (f32[128,64]{0,1}, f32[128,64]{0,1:S(1)}, u32[]{:S(2)}) copy-start(f32[128,64]{0,1:S(1)} %fusion.84) | copy-start | bytes 98308
  224.8 49.5 %copy-start.70 = (f32[128]{0:T(128)}, f32[128]{0:T(128)S(1)}, u32[]{:S(2)}) copy-start(f32[128]{0:T(128)S(1)} %get-tuple-element.87) | copy-start | bytes 1540
  226.5 47.8 %copy-start.59 = (s32[1024]{0:T(1024)}, s32[1024]{0:T(1024)S(1)}, u32[]{:S(2)}) copy-start(s32[1024]{0:T(1024)S(1)} %pad_clamp_fusion) | copy-start | bytes 12292
  274.3 46.2 %all-to-all-start.9 = ((bf16[8,96,2048]{2,1,0:T(8,128)(2,1)}), bf16[8,96,2048]{2,1,0:T(8,128)(2,1)S(1)}, u32[]{:S(2)}, u32[]{:S(2)}) async-start(bf16[8,96,2048]{2,1,0:T(8,128)(2,1)} %bitcast.293), calls=%async_computation.9 | async-start | bytes 6291456 | tf_op jit(solution)/shard_map/all_to_all | solution.py:274
  322.1 42.9 %all-to-all-start.4 = ((bf16[8,96,2048]{2,1,0:T(8,128)(2,1)}), bf16[8,96,2048]{2,1,0:T(8,128)(2,1)}, u32[]{:S(2)}, u32[]{:S(2)}) async-start(bf16[8,96,2048]{2,1,0:T(8,128)(2,1)} %bitcast.292), calls=%async_computation.4 | async-start | bytes 6291456 | tf_op jit(solution)/shard_map/all_to_all | solution.py:274
  332.8 36.0 %copy-start.44 = (f32[128,64]{0,1:T(8,128)}, f32[128,64]{0,1:T(8,128)S(1)}, u32[]{:S(2)}) copy-start(f32[128,64]{0,1:T(8,128)S(1)} %get-tuple-element.95) | copy-start | bytes 98308
  365.0 41.5 %all-to-all-start.2 = ((bf16[8,96,2048]{2,1,0:T(8,128)(2,1)}), bf16[8,96,2048]{2,1,0:T(8,128)(2,1)S(1)}, u32[]{:S(2)}, u32[]{:S(2)}) async-start(bf16[8,96,2048]{2,1,0:T(8,128)(2,1)} %bitcast.32), calls=%async_computation.2 | async-start | bytes 6291456 | tf_op jit(solution)/shard_map/all_to_all | solution.py:274
  368.8 104.9 %copy-start.41 = (f32[128,64]{0,1:T(8,128)}, f32[128,64]{0,1:T(8,128)S(1)}, u32[]{:S(2)}) copy-start(f32[128,64]{0,1:T(8,128)S(1)} %fusion.88) | copy-start | bytes 98308
  408.2 42.8 %all-to-all-start.7 = ((bf16[8,96,2048]{2,1,0:T(8,128)(2,1)}), bf16[8,96,2048]{2,1,0:T(8,128)(2,1)}, u32[]{:S(2)}, u32[]{:S(2)}) async-start(bf16[8,96,2048]{2,1,0:T(8,128)(2,1)} %bitcast.291), calls=%async_computation.7 | async-start | bytes 6291456 | tf_op jit(solution)/shard_map/all_to_all | solution.py:274
  511.1 42.8 %all-to-all-start.8 = ((bf16[8,96,2048]{2,1,0:T(8,128)(2,1)}), bf16[8,96,2048]{2,1,0:T(8,128)(2,1)}, u32[]{:S(2)}, u32[]{:S(2)}) async-start(bf16[8,96,2048]{2,1,0:T(8,128)(2,1)} %bitcast.310), calls=%async_computation.8 | async-start | bytes 6291456 | tf_op jit(solution)/shard_map/all_to_all | solution.py:279
  553.9 42.4 %all-to-all-start.10 = ((bf16[8,96,2048]{2,1,0:T(8,128)(2,1)}), bf16[8,96,2048]{2,1,0:T(8,128)(2,1)}, u32[]{:S(2)}, u32[]{:S(2)}) async-start(bf16[8,96,2048]{2,1,0:T(8,128)(2,1)} %bitcast.309), calls=%async_computation.10 | async-start | bytes 6291456 | tf_op jit(solution)/shard_map/all_to_all | solution.py:279
  596.2 42.3 %all-to-all-start.3 = ((bf16[8,96,2048]{2,1,0:T(8,128)(2,1)}), bf16[8,96,2048]{2,1,0:T(8,128)(2,1)}, u32[]{:S(2)}, u32[]{:S(2)}) async-start(bf16[8,96,2048]{2,1,0:T(8,128)(2,1)} %bitcast.290), calls=%async_computation.3 | async-start | bytes 6291456 | tf_op jit(solution)/shard_map/all_to_all | solution.py:279
  638.6 41.6 %all-to-all-start.5 = ((bf16[8,96,2048]{2,1,0:T(8,128)(2,1)}), bf16[8,96,2048]{2,1,0:T(8,128)(2,1)S(1)}, u32[]{:S(2)}, u32[]{:S(2)}) async-start(bf16[8,96,2048]{2,1,0:T(8,128)(2,1)} %bitcast.289), calls=%async_computation.5 | async-start | bytes 6291456 | tf_op jit(solution)/shard_map/all_to_all | solution.py:279
  680.2 50.3 %all-to-all-start.11 = ((bf16[4,128,2048]{2,1,0:T(8,128)(2,1)}), bf16[4,128,2048]{2,1,0:T(8,128)(2,1)}, u32[]{:S(2)}, u32[]{:S(2)}) async-start(bf16[4,128,2048]{2,1,0:T(8,128)(2,1)} %fusion.23), calls=%async_computation.11 | async-start | bytes 4194304 | tf_op jit(solution)/shard_map/all_to_all | solution.py:286
  689.6 45.5 %copy-start.78 = (s32[4]{0:T(128)S(1)}, s32[4]{0:T(128)}, u32[]{:S(2)}) copy-start(s32[4]{0:T(128)} %param.12) | copy-start | bytes 52
  689.6 46.1 %copy-start.10 = (s32[8,4,128,8]{3,2,1,0:T(8,128)S(1)}, s32[8,4,128,8]{3,2,1,0:T(8,128)}, u32[]{:S(2)}) copy-start(s32[8,4,128,8]{3,2,1,0:T(8,128)} %copy-done.9) | copy-start | bytes 393220
  689.6 49.1 %copy-start.43 = (f32[128,64]{0,1:T(8,128)S(1)}, f32[128,64]{0,1:T(8,128)}, u32[]{:S(2)}) copy-start(f32[128,64]{0,1:T(8,128)} %get-tuple-element.27) | copy-start | bytes 98308
  689.6 49.1 %copy-start.45 = (f32[128,64]{0,1:T(8,128)S(1)}, f32[128,64]{0,1:T(8,128)}, u32[]{:S(2)}) copy-start(f32[128,64]{0,1:T(8,128)} %copy-done.44) | copy-start | bytes 98308
  689.6 49.1 %copy-start.69 = (f32[128]{0:T(128)S(1)}, f32[128]{0:T(128)}, u32[]{:S(2)}) copy-start(f32[128]{0:T(128)} %get-tuple-element.36) | copy-start | bytes 1540
  730.5 52.2 %all-to-all-start.6 = ((bf16[4,128,2048]{2,1,0:T(8,128)(2,1)}), bf16[4,128,2048]{2,1,0:T(8,128)(2,1)}, u32[]{:S(2)}, u32[]{:S(2)}) async-start(bf16[4,128,2048]{2,1,0:T(8,128)(2,1)} %fusion.24), calls=%async_computation.6 | async-start | bytes 4194304 | tf_op jit(solution)/shard_map/all_to_all | solution.py:286
  735.0 179.9 %all-gather.16.cloned.1.call-start = ((), (), s32[]{:S(2)}) async-start(), calls=%async_computation.23 | async-start | bytes 4718592 | tf_op jit(solution)/shard_map/all_gather | solution.py:401
  741.0 43.9 %copy-start.34 = (bf16[1,128,2048]{2,1,0:T(8,128)(2,1)S(1)}, bf16[1,128,2048]{2,1,0:T(8,128)(2,1)}, u32[]{:S(2)}) copy-start(bf16[1,128,2048]{2,1,0:T(8,128)(2,1)} %param.11) | copy-start | bytes 1572868
  741.0 43.9 %copy-start.73 = (pred[128]{0:T(512)(128)(4,1)S(1)}, pred[128]{0:T(512)(128)(4,1)}, u32[]{:S(2)}) copy-start(pred[128]{0:T(512)(128)(4,1)} %copy-done.72) | copy-start | bytes 388
  741.0 43.9 %copy-start.79 = (f32[128]{0:T(128)S(1)}, f32[128]{0:T(128)}, u32[]{:S(2)}) copy-start(f32[128]{0:T(128)} %get-tuple-element.86) | copy-start | bytes 1540
  794.0 32.5 %copy-start.19 = (f32[1024,64]{1,0:T(8,128)S(1)}, f32[1024,64]{1,0:T(8,128)}, u32[]{:S(2)}) copy-start(f32[1024,64]{1,0:T(8,128)} %get-tuple-element.79) | copy-start | bytes 786436
  794.0 32.5 %copy-start.30 = (f32[1024,64]{1,0:T(8,128)S(1)}, f32[1024,64]{1,0:T(8,128)}, u32[]{:S(2)}) copy-start(f32[1024,64]{1,0:T(8,128)} %get-tuple-element.77) | copy-start | bytes 786436
  794.0 15.7 %all-to-all-start.12 = ((bf16[128,8,256]{2,0,1:T(8,128)(2,1)}), bf16[128,8,256]{2,0,1:T(8,128)(2,1)S(1)}, u32[]{:S(2)}, u32[]{:S(2)}) async-start(bf16[128,8,256]{2,0,1:T(8,128)(2,1)} %bitcast.284), calls=%async_computation.12 | async-start | bytes 1048576 | tf_op jit(solution)/shard_map/all_to_all | solution.py:403
  799.2 121.9 %reduce-scatter.4.cloned.1.call-start = ((), (), s32[]{:S(2)}) async-start(), calls=%async_computation.21 | async-start | bytes 4718592 | tf_op jit(solution)/shard_map/reduce_scatter | solution.py:418
  849.6 124.1 %reduce-scatter.6.cloned.1.call-start = ((), (), s32[]{:S(2)}) async-start(), calls=%async_computation.22 | async-start | bytes 3932160 | tf_op jit(solution)/shard_map/reduce_scatter | solution.py:424
  859.0 146.5 %reduce-scatter.8.cloned.1.call-start = ((), (), s32[]{:S(2)}) async-start(), calls=%async_computation.24 | async-start | bytes 1310720 | tf_op jit(solution)/shard_map/reduce_scatter | solution.py:429
  896.1 18.9 %copy-start.29 = (bf16[1024,256]{1,0:T(8,128)(2,1)S(1)}, bf16[1024,256]{1,0:T(8,128)(2,1)}, u32[]{:S(2)}) copy-start(bf16[1024,256]{1,0:T(8,128)(2,1)} %attend.1) | copy-start | bytes 1572868
  962.6 20.9 %copy-start.23 = (f32[128,2048]{1,0:T(8,128)S(1)}, f32[128,2048]{1,0:T(8,128)}, u32[]{:S(2)}) copy-start(f32[128,2048]{1,0:T(8,128)} %get-tuple-element.32) | copy-start | bytes 3145732
  962.6 20.9 %copy-start.32 = (bf16[128,2048]{1,0:T(8,128)(2,1)S(1)}, bf16[128,2048]{1,0:T(8,128)(2,1)}, u32[]{:S(2)}) copy-start(bf16[128,2048]{1,0:T(8,128)(2,1)} %reduce-scatter.4.cloned.1.call-done) | copy-start | bytes 1572868
  977.3 16.2 %all-to-all-start.13 = ((bf16[8,64,3,256]{3,1,2,0:T(8,128)(2,1)}), bf16[8,64,3,256]{3,1,2,0:T(8,128)(2,1)S(1)}, u32[]{:S(2)}, u32[]{:S(2)}) async-start(bf16[8,64,3,256]{3,1,2,0:T(8,128)(2,1)} %copy.252), calls=%async_computation.15 | async-start | bytes 1572864 | tf_op jit(solution)/shard_map/all_to_all | solution.py:426
  (71 other events, 352.3 us)
Sparse Core Ops, SparseCore 0:
  28.9 71.1 all-gather.7
  102.0 35.1 all-gather.17
  140.1 79.2 all-gather.9
  221.4 43.8 all-gather.13
  266.7 44.6 all-gather.11
  786.8 42.7 all-gather.15
  849.7 50.8 reduce-scatter.3
  903.0 70.6 reduce-scatter.5
  976.2 29.3 reduce-scatter.7

commit v2 on v1

v2 whole, which is shorter than its diff:
```python
import functools

import jax
import jax.numpy as jnp
from jax import lax
from jax.experimental import pallas as pl
from jax.experimental.pallas import tpu as pltpu
from jax.sharding import PartitionSpec as P

HEADS = 16
FF = 1024

epsilon = 1e-06
rope_base = 10000.0
MESH = pl.DeviceIdType.MESH
BF = jnp.bfloat16
F32 = jnp.float32


def dot(a, b, ca, cb):
    return lax.dot_general(a, b, (((ca,), (cb,)), ((), ())), preferred_element_type=F32)


def push_kernel(n_seq, n_fsdp, scope, gather, src, dst, send_sem, recv_sem, own_sem):
    me_s, me_f = lax.axis_index("seq"), lax.axis_index("fsdp")
    n = n_seq * n_fsdp if scope == "all" else n_seq
    me = me_s * n_fsdp + me_f if scope == "all" else me_s

    def where(index):
        if scope == "all":
            return (index // n_fsdp, index % n_fsdp)
        return (index, me_f)

    barrier = pltpu.get_barrier_semaphore()

    def greet(i, carry):
        pl.semaphore_signal(barrier, inc=1, device_id=where((me + i) % n), device_id_type=MESH)
        return carry

    lax.fori_loop(1, n, greet, 0)
    own = pltpu.make_async_copy(src if gather else src.at[me], dst.at[me], own_sem)
    own.start()
    pl.semaphore_wait(barrier, n - 1)

    def copy_to(other):
        return pltpu.make_async_remote_copy(
            src_ref=src if gather else src.at[other],
            dst_ref=dst.at[me],
            send_sem=send_sem.at[other],
            recv_sem=recv_sem.at[me],
            device_id=where(other),
            device_id_type=MESH,
        )

    def copy_from(other):
        return pltpu.make_async_remote_copy(
            src_ref=src if gather else src.at[other],
            dst_ref=dst.at[other],
            send_sem=send_sem.at[other],
            recv_sem=recv_sem.at[other],
            device_id=where(other),
            device_id_type=MESH,
        )

    def send(i, carry):
        copy_to((me + i) % n).start()
        return carry

    lax.fori_loop(1, n, send, 0)

    def finish(i, carry):
        other = (me + i) % n
        copy_from(other).wait_recv()
        copy_to(other).wait_send()
        return carry

    lax.fori_loop(1, n, finish, 0)
    own.wait()


def push(block, n_seq, n_fsdp, scope, gather, collective_id):
    n = n_seq * n_fsdp if scope == "all" else n_seq
    shape = (n,) + (block.shape if gather else block.shape[1:])
    return pl.pallas_call(
        functools.partial(push_kernel, n_seq, n_fsdp, scope, gather),
        out_shape=jax.ShapeDtypeStruct(shape, block.dtype),
        in_specs=[pl.BlockSpec(memory_space=pltpu.VMEM)],
        out_specs=pl.BlockSpec(memory_space=pltpu.VMEM),
        scratch_shapes=[
            pltpu.SemaphoreType.DMA((n,)),
            pltpu.SemaphoreType.DMA((n,)),
            pltpu.SemaphoreType.DMA,
        ],
        compiler_params=pltpu.CompilerParams(collective_id=collective_id, has_side_effects=True),
        name="push_" + scope,
    )(block)


def rows_of(flat, multiple):
    size = flat.shape[0]
    whole = -(-size // (multiple * 128)) * multiple * 128
    return jnp.pad(flat, (0, whole - size)).reshape(-1, 128)


def remote(src, dst, send_sem, recv_sem, device):
    return pltpu.make_async_remote_copy(
        src_ref=src,
        dst_ref=dst,
        send_sem=send_sem,
        recv_sem=recv_sem,
        device_id=device,
        device_id_type=MESH,
    )


def greet_all(n_seq, n_fsdp):
    me_s, me_f = lax.axis_index("seq"), lax.axis_index("fsdp")
    n = n_seq * n_fsdp
    me = me_s * n_fsdp + me_f
    barrier = pltpu.get_barrier_semaphore()

    def greet(i, carry):
        other = (me + i) % n
        pl.semaphore_signal(
            barrier, inc=1, device_id=(other // n_fsdp, other % n_fsdp), device_id_type=MESH
        )
        return carry

    lax.fori_loop(1, n, greet, 0)
    pl.semaphore_wait(barrier, n - 1)


def greet_lines(n_seq, n_fsdp):
    me_s, me_f = lax.axis_index("seq"), lax.axis_index("fsdp")
    barrier = pltpu.get_barrier_semaphore()
    for i in range(1, n_seq):
        pl.semaphore_signal(
            barrier, inc=1, device_id=((me_s + i) % n_seq, me_f), device_id_type=MESH
        )
    for i in range(1, n_fsdp):
        pl.semaphore_signal(
            barrier, inc=1, device_id=(me_s, (me_f + i) % n_fsdp), device_id_type=MESH
        )
    pl.semaphore_wait(barrier, n_seq + n_fsdp - 2)


class Exchange:
    def __init__(self, n_seq, n_fsdp, src, dst, sems):
        self.n, self.n_fsdp, self.src, self.dst = n_seq * n_fsdp, n_fsdp, src, dst
        self.send_sem, self.recv_sem, self.own_sem = sems
        self.me = lax.axis_index("seq") * n_fsdp + lax.axis_index("fsdp")

    def copy(self, i, place):
        other = (self.me + i) % self.n
        return remote(
            self.src.at[other],
            self.dst.at[self.me if place is None else place],
            self.send_sem.at[i],
            self.recv_sem.at[self.me if place is None else place],
            (other // self.n_fsdp, other % self.n_fsdp),
        )

    def own(self):
        return pltpu.make_async_copy(
            self.src.at[self.me], self.dst.at[self.me], self.own_sem
        )

    def start(self):
        self.own().start()

        def one(i, carry):
            self.copy(i, None).start()
            return carry

        lax.fori_loop(1, self.n, one, 0)

    def finish(self):
        def one(i, carry):
            self.copy(i, None).wait_send()
            self.copy(i, (self.me + i) % self.n).wait_recv()
            return carry

        lax.fori_loop(1, self.n, one, 0)
        self.own().wait()


def exchange_sems(n):
    return [
        pltpu.SemaphoreType.DMA((n,)),
        pltpu.SemaphoreType.DMA((n,)),
        pltpu.SemaphoreType.DMA,
    ]


def line_step(n_fsdp, step, arrived, forward):
    me_f = lax.axis_index("fsdp")

    @pl.when(me_f - step >= 0)
    def _():
        arrived(me_f - step)

        @pl.when(me_f + 1 < n_fsdp)
        def _():
            forward(me_f - step, 0, me_f + 1)

    @pl.when(me_f + step < n_fsdp)
    def _():
        arrived(me_f + step)

        @pl.when(me_f >= 1)
        def _():
            forward(me_f + step, 1, me_f - 1)


def line_sent(n_fsdp, step, sent):
    me_f = lax.axis_index("fsdp")

    @pl.when((me_f - step >= 0) & (me_f + 1 < n_fsdp))
    def _():
        sent(me_f - step, 0, me_f + 1)

    @pl.when((me_f + step < n_fsdp) & (me_f >= 1))
    def _():
        sent(me_f + step, 1, me_f - 1)


def flipped(index, bit):
    return index + bit * (1 - 2 * ((index // bit) % 2))


class SeqGather:
    def __init__(self, order, own, block, send_sem, recv_sem):
        self.order, self.own, self.block = order, own, block
        self.send_sem, self.recv_sem = send_sem, recv_sem
        self.me_s, self.me_f = lax.axis_index("seq"), lax.axis_index("fsdp")

    def held(self, stage):
        indices = [self.me_s]
        for bit in self.order[:stage]:
            indices = indices + [flipped(i, bit) for i in indices]
        return indices

    def copies(self, stage):
        partner = flipped(self.me_s, self.order[stage])
        result = []
        for count, index in enumerate(self.held(stage)):
            src = self.own if count == 0 else self.block(index)
            sem = self.send_sem.at[(1 << stage) - 1 + count]
            result.append(
                remote(src, self.block(index), sem, self.recv_sem.at[index], (partner, self.me_f))
            )
        return result

    def start(self, stage):
        for copy in self.copies(stage):
            copy.start()

    def wait(self, stage):
        for index in self.held(stage):
            index = flipped(index, self.order[stage])
            remote(
                self.block(index),
                self.block(index),
                self.send_sem.at[0],
                self.recv_sem.at[index],
                (self.me_s, self.me_f),
            ).wait_recv()

    def sent(self):
        for stage in range(len(self.order)):
            for copy in self.copies(stage):
                copy.wait_send()


def gather_orders(n_seq):
    bits = [1 << b for b in range(n_seq.bit_length() - 1)]
    return bits[1:] + bits[:1], bits[:0:-1] + bits[:1]


def first_kernel(
    n_seq,
    n_fsdp,
    small,
    tokens,
    qkv,
    small_all,
    slot,
    qkv_all,
    own_sem,
    small_send,
    small_recv,
    qkv_send,
    qkv_recv,
    line_send,
    line_recv,
    token_send,
    token_recv,
):
    me_s, me_f = lax.axis_index("seq"), lax.axis_index("fsdp")
    n = n_seq * n_fsdp
    me = me_s * n_fsdp + me_f
    head_width = qkv_all.shape[3] // 3
    width = head_width * n_seq
    half = tokens.shape[0] // 2
    orders = gather_orders(n_seq)
    stages = len(orders[0])

    def columns(owner, part):
        start = pl.multiple_of(part * width + owner * head_width, 128)
        return qkv.at[:, pl.ds(start, head_width)]

    def column_place(source, part):
        return qkv_all.at[source, me_f, :, pl.ds(part * head_width, head_width)]

    own = [
        pltpu.make_async_copy(small, small_all.at[me], own_sem.at[0]),
        pltpu.make_async_copy(tokens, slot.at[me_s], own_sem.at[1]),
    ] + [
        pltpu.make_async_copy(columns(me_s, part), column_place(me_s, part), own_sem.at[2 + part])
        for part in range(3)
    ]
    for copy in own:
        copy.start()
    greet_all(n_seq, n_fsdp)

    def column_copy(i, part):
        other = (me_s + i) % n_seq
        return remote(
            columns(other, part),
            column_place(me_s, part),
            qkv_send.at[i, part],
            qkv_recv.at[me_s, part],
            (other, me_f),
        )

    for i in range(1, n_seq):
        for part in range(3):
            column_copy(i, part).start()
    for copy in own:
        copy.wait()

    def line_copy(part, step, block, way, to):
        place = qkv_all.at[part, block]
        return remote(
            place, place, line_send.at[part, way, step], line_recv.at[part, block], (me_s, to)
        )

    def line_first(part):
        @pl.when(me_f + 1 < n_fsdp)
        def _():
            line_copy(part, 0, me_f, 0, me_f + 1).start()

        @pl.when(me_f >= 1)
        def _():
            line_copy(part, 0, me_f, 1, me_f - 1).start()

    def column_arrived(i, carry):
        source = (me_s + i) % n_seq

        @pl.when(i > 0)
        def _():
            for part in range(3):
                remote(
                    columns(source, part),
                    column_place(source, part),
                    qkv_send.at[i, part],
                    qkv_recv.at[source, part],
                    (source, me_f),
                ).wait_recv()

        line_first(source)
        return carry

    lax.fori_loop(0, n_seq, column_arrived, 0)

    flows = []
    for side in range(2):
        rows = pl.ds(side * half, half)
        flows.append(
            SeqGather(
                orders[side],
                tokens.at[rows],
                lambda index, rows=rows: slot.at[index, rows],
                token_send.at[side],
                token_recv.at[side],
            )
        )

    def point(stage):
        for flow in flows:
            if 0 < stage <= stages:
                flow.wait(stage - 1)
            if stage < stages:
                flow.start(stage)

    def small_copy(i):
        other = (me + i) % n
        return remote(
            small,
            small_all.at[me],
            small_send.at[i],
            small_recv.at[me],
            (other // n_fsdp, other % n_fsdp),
        )

    def small_start(i, carry):
        small_copy(i).start()
        return carry

    point(0)
    lax.fori_loop(1, n, small_start, 0)
    count = 1
    for step in range(1, n_fsdp):

        def column_next(i, carry, step=step):
            part = (me_s + i) % n_seq
            line_step(
                n_fsdp,
                step,
                lambda block: line_copy(part, 0, block, 0, me_f).wait_recv(),
                lambda block, way, to: line_copy(part, step, block, way, to).start(),
            )
            return carry

        for part in range(2):
            lax.fori_loop(part * n_seq // 2, (part + 1) * n_seq // 2, column_next, 0)
            point(count)
            count += 1
    while count <= stages:
        point(count)
        count += 1
    for flow in flows:
        flow.sent()

    def column_sent(i, carry):
        for part in range(3):
            column_copy(i, part).wait_send()
        return carry

    lax.fori_loop(1, n_seq, column_sent, 0)

    def small_wait(i, carry):
        other = (me + i) % n
        small_copy(i).wait_send()
        remote(
            small,
            small_all.at[other],
            small_send.at[i],
            small_recv.at[other],
            (other // n_fsdp, other % n_fsdp),
        ).wait_recv()
        return carry

    lax.fori_loop(1, n, small_wait, 0)

    def line_done(part, carry):
        for step in range(n_fsdp):
            line_sent(
                n_fsdp,
                step,
                lambda block, way, to: line_copy(part, step, block, way, to).wait_send(),
            )
        return carry

    lax.fori_loop(0, n_seq, line_done, 0)


def first_gather(small, tokens, qkv, n_seq, n_fsdp, collective_id):
    owned = qkv.shape[0]
    head_width = qkv.shape[1] // (3 * n_seq)
    n = n_seq * n_fsdp
    vmem = pl.BlockSpec(memory_space=pltpu.VMEM)
    any_space = pl.BlockSpec(memory_space=pl.ANY)
    dma = pltpu.SemaphoreType.DMA
    return pl.pallas_call(
        functools.partial(first_kernel, n_seq, n_fsdp),
        out_shape=[
            jax.ShapeDtypeStruct((n,) + small.shape, BF),
            jax.ShapeDtypeStruct((n_seq,) + tokens.shape, BF),
            jax.ShapeDtypeStruct((n_seq, n_fsdp, owned, 3 * head_width), BF),
        ],
        in_specs=[vmem] * 3,
        out_specs=[vmem, any_space, any_space],
        scratch_shapes=[
            dma((5,)),
            dma((n,)),
            dma((n,)),
            dma((n_seq, 3)),
            dma((n_seq, 3)),
            dma((n_seq, 2, n_fsdp)),
            dma((n_seq, n_fsdp)),
            dma((2, n_seq - 1)),
            dma((2, n_seq)),
        ],
        compiler_params=pltpu.CompilerParams(collective_id=collective_id, has_side_effects=True),
        name="first_gather",
    )(small, tokens, qkv)


def greet_seq(n_seq):
    me_s, me_f = lax.axis_index("seq"), lax.axis_index("fsdp")
    barrier = pltpu.get_barrier_semaphore()
    for i in range(1, n_seq):
        pl.semaphore_signal(
            barrier, inc=1, device_id=((me_s + i) % n_seq, me_f), device_id_type=MESH
        )
    pl.semaphore_wait(barrier, n_seq - 1)


class TermSum:
    def __init__(
        self, n_seq, n_fsdp, terms, seq_terms, fsdp_terms, seq_send, seq_recv, fsdp_send, fsdp_recv
    ):
        self.n_seq, self.n_fsdp, self.terms = n_seq, n_fsdp, terms
        self.seq_terms, self.fsdp_terms = seq_terms, fsdp_terms
        self.seq_send, self.seq_recv = seq_send, seq_recv
        self.fsdp_send, self.fsdp_recv = fsdp_send, fsdp_recv
        self.me_s, self.me_f = lax.axis_index("seq"), lax.axis_index("fsdp")

    def part(self, owner):
        columns = self.seq_terms.shape[2]
        return self.terms.at[:, pl.ds(pl.multiple_of(owner * columns, 128), columns)]

    def seq_copy(self, i, place):
        other = (self.me_s + i) % self.n_seq
        return remote(
            self.part(other),
            self.seq_terms.at[place],
            self.seq_send.at[i],
            self.seq_recv.at[place],
            (other, self.me_f),
        )

    def fsdp_copy(self, i, place):
        other = (self.me_f + i) % self.n_fsdp
        return remote(
            self.seq_terms.at[self.me_s],
            self.fsdp_terms.at[place],
            self.fsdp_send.at[i],
            self.fsdp_recv.at[place],
            (self.me_s, other),
        )

    def start_seq(self):
        for i in range(1, self.n_seq):
            self.seq_copy(i, self.me_s).start()

    def over_seq(self):
        result = self.part(self.me_s)[...]
        for i in range(1, self.n_seq):
            place = (self.me_s + i) % self.n_seq
            self.seq_copy(i, place).wait_recv()
            result = result + self.seq_terms[place]
        for i in range(1, self.n_seq):
            self.seq_copy(i, self.me_s).wait_send()
        return result

    def start_fsdp(self, more):
        self.seq_terms[self.me_s] = more + (self.over_seq() if self.terms is not None else 0.0)
        for i in range(1, self.n_fsdp):
            self.fsdp_copy(i, self.me_f).start()

    def finish(self):
        result = self.seq_terms[self.me_s]
        for i in range(1, self.n_fsdp):
            place = (self.me_f + i) % self.n_fsdp
            self.fsdp_copy(i, place).wait_recv()
            result = result + self.fsdp_terms[place]
        for i in range(1, self.n_fsdp):
            self.fsdp_copy(i, self.me_f).wait_send()
        return result


def term_scratch(n_seq, n_fsdp, shape):
    dma = pltpu.SemaphoreType.DMA
    return [
        pltpu.VMEM((n_seq,) + shape, F32),
        pltpu.VMEM((n_fsdp,) + shape, F32),
        dma((n_seq,)),
        dma((n_seq,)),
        dma((n_fsdp,)),
        dma((n_fsdp,)),
    ]


def gather_kernel(n_seq, n_fsdp, x, terms, out, total, own_sem, send_sem, recv_sem, *scratch):
    me_s = lax.axis_index("seq")
    half = x.shape[0] // 2
    own = pltpu.make_async_copy(x, out.at[me_s], own_sem)
    own.start()
    term_sum = TermSum(n_seq, n_fsdp, terms, scratch[0], None, *scratch[1:], None, None)
    greet_seq(n_seq)
    flows = []
    for side, order in enumerate(gather_orders(n_seq)):
        rows = pl.ds(side * half, half)
        flows.append(
            SeqGather(
                order,
                x.at[rows],
                lambda index, rows=rows: out.at[index, rows],
                send_sem.at[side],
                recv_sem.at[side],
            )
        )
    for stage in range(len(flows[0].order)):
        for flow in flows:
            flow.start(stage)
        if stage == 0:
            term_sum.start_seq()
        if stage == 1:
            total[...] = term_sum.over_seq()
        for flow in flows:
            flow.wait(stage)
    for flow in flows:
        flow.sent()
    own.wait()


def gather_seq(x, terms, n_seq, n_fsdp, collective_id):
    vmem = pl.BlockSpec(memory_space=pltpu.VMEM)
    dma = pltpu.SemaphoreType.DMA
    part = (terms.shape[0], terms.shape[1] // n_seq)
    return pl.pallas_call(
        functools.partial(gather_kernel, n_seq, n_fsdp),
        out_shape=[
            jax.ShapeDtypeStruct((n_seq,) + x.shape, x.dtype),
            jax.ShapeDtypeStruct(part, terms.dtype),
        ],
        in_specs=[vmem] * 2,
        out_specs=[vmem] * 2,
        scratch_shapes=[
            dma,
            dma((2, n_seq - 1)),
            dma((2, n_seq)),
            pltpu.VMEM((n_seq,) + part, F32),
            dma((n_seq,)),
            dma((n_seq,)),
        ],
        compiler_params=pltpu.CompilerParams(collective_id=collective_id, has_side_effects=True),
        cost_estimate=pl.CostEstimate(flops=0, bytes_accessed=1 << 26, transcendentals=0),
        name="gather_seq",
    )(x, terms)


class SeqReduce:
    def __init__(self, n_seq, a, w, w_dim, sums, got, send_sem, recv_sem):
        self.a, self.w, self.w_dim, self.sums, self.got = a, w, w_dim, sums, got
        self.send_sem, self.recv_sem = send_sem, recv_sem
        self.me_s, self.me_f = lax.axis_index("seq"), lax.axis_index("fsdp")
        self.orders = [order[-1:] + order[-2::-1] for order in gather_orders(n_seq)]
        self.stages = len(self.orders[0])
        self.half = sums.shape[1] // 2
        self.width = sums.shape[2]

    def combined(self, index, bits):
        indices = [index]
        for bit in bits:
            indices = indices + [flipped(i, bit) for i in indices]
        return indices

    def product(self, index):
        def some(columns):
            w = self.w[:, columns] if self.w_dim == 0 else self.w[columns, :]
            self.sums[index, :, columns] = dot(self.a[index], w, 1, self.w_dim).astype(BF)

        chunked(self.width, 512, some)

    def copy(self, stage, side, count, index):
        order = self.orders[side]
        slot = sum(1 << (self.stages - 1 - s) for s in range(stage)) + count
        rows = pl.ds(side * self.half, self.half)
        return remote(
            self.sums.at[index, rows],
            self.got.at[slot, rows],
            self.send_sem.at[side, slot],
            self.recv_sem.at[side, slot],
            (flipped(self.me_s, order[stage]), self.me_f),
        )

    def leaving(self, stage, side):
        order = self.orders[side]
        return self.combined(flipped(self.me_s, order[stage]), order[stage + 1 :])

    def start(self, stage):
        if stage == 0:
            for count, index in enumerate(self.leaving(0, 0)):
                self.product(index)
                for side in range(2):
                    self.copy(0, side, self.twin(count) if side == 1 else count, index).start()
            for index in self.combined(self.me_s, self.orders[0][1:]):
                self.product(index)
        else:
            for side in range(2):
                for count, index in enumerate(self.leaving(stage, side)):
                    self.copy(stage, side, count, index).start()

    def twin(self, count):
        first, second = self.orders[0][1:], self.orders[1][1:]
        place = 0
        for position, bit in enumerate(first):
            if (count >> position) & 1:
                place += 1 << second.index(bit)
        return place

    def finish(self, stage, last=None):
        for side in range(2):
            order = self.orders[side]
            rows = pl.ds(side * self.half, self.half)
            for count, index in enumerate(self.combined(self.me_s, order[stage + 1 :])):
                copy = self.copy(stage, side, count, index)
                copy.wait_recv()
                slot = sum(1 << (self.stages - 1 - s) for s in range(stage)) + count

                def some(columns):
                    total = self.sums[index, rows, columns].astype(F32)
                    total = total + self.got[slot, rows, columns].astype(F32)
                    if last is None:
                        self.sums[index, rows, columns] = total.astype(BF)
                    else:
                        last[rows, columns] = total

                chunked(self.width, 1024, some)

    def events(self, last):
        def leave(count, index):
            self.product(index)
            for side in range(2):
                self.copy(0, side, self.twin(count) if side == 1 else count, index).start()

        result = [
            (1, functools.partial(leave, count, index))
            for count, index in enumerate(self.leaving(0, 0))
        ]
        for index in self.combined(self.me_s, self.orders[0][1:]):
            result.append((1, functools.partial(self.product, index)))
        result.append((1, functools.partial(self.finish, 0, last if self.stages == 1 else None)))
        for stage in range(1, self.stages):
            result.append((0, functools.partial(self.start, stage)))
            result.append(
                (7, functools.partial(self.finish, stage, last if stage == self.stages - 1 else None))
            )
        return result

    def sent(self):
        for stage in range(self.stages):
            for side in range(2):
                for count, index in enumerate(self.leaving(stage, side)):
                    self.copy(stage, side, count, index).wait_send()


def reduce_scratch(n_seq, rows, width):
    dma = pltpu.SemaphoreType.DMA
    return [
        pltpu.VMEM((n_seq, rows, width), BF),
        pltpu.VMEM((n_seq - 1, rows, width), BF),
        dma((2, n_seq - 1)),
        dma((2, n_seq - 1)),
    ]


def reduce_kernel(n_seq, w_dim, a, w, out, *scratch):
    greet_seq(n_seq)
    reduce = SeqReduce(n_seq, a, w, w_dim, *scratch)
    for stage in range(reduce.stages):
        reduce.start(stage)
        reduce.finish(stage, out if stage == reduce.stages - 1 else None)
    reduce.sent()


def product_reduced(a, w, w_dim, n_seq, collective_id):
    rows = a.shape[0] // n_seq
    width = w.shape[1 - w_dim]
    return pl.pallas_call(
        functools.partial(reduce_kernel, n_seq, w_dim),
        out_shape=jax.ShapeDtypeStruct((rows, width), F32),
        in_specs=[pl.BlockSpec(memory_space=pltpu.VMEM)] * 2,
        out_specs=pl.BlockSpec(memory_space=pltpu.VMEM),
        scratch_shapes=reduce_scratch(n_seq, rows, width),
        compiler_params=pltpu.CompilerParams(
            collective_id=collective_id, has_side_effects=True, vmem_limit_bytes=40 << 20
        ),
        name="product_reduced",
    )(a.reshape(n_seq, rows, -1), w)


def last_kernel(
    n_seq,
    n_fsdp,
    a,
    w,
    part,
    x,
    mid,
    gains,
    terms_in,
    heads,
    input_out,
    qkv_out,
    total,
    *scratch,
):
    up, down, done, got, up_send, up_recv, down_send, down_recv, done_send, done_recv = scratch[:10]
    one, terms, seq_terms, fsdp_terms, seq_send, seq_recv, fsdp_send, fsdp_recv = scratch[10:18]
    me_s, me_f = lax.axis_index("seq"), lax.axis_index("fsdp")
    head_width = part.shape[3] // 3
    width = n_seq * head_width
    greet_lines(n_seq, n_fsdp)
    reduce = SeqReduce(n_seq, a, w, 1, *scratch[18:])
    term_sum = TermSum(
        n_seq,
        n_fsdp,
        terms,
        seq_terms,
        fsdp_terms,
        seq_send,
        seq_recv,
        fsdp_send,
        fsdp_recv,
    )

    def input_rows():
        tile = 32
        terms[...] = terms_in[...]

        def some(i, carry):
            rows = pl.ds(pl.multiple_of(i * tile, tile), tile)
            values = x[rows, :].astype(F32)
            scale = lax.rsqrt(jnp.mean(values * values, axis=-1, keepdims=True) + epsilon)
            grad = one[rows, :]
            weighted = grad * gains[0:1, :]
            mean = jnp.mean(weighted * values, axis=-1, keepdims=True)
            result = scale * weighted - values * (scale * scale * scale * mean)
            input_out[rows, :] = (mid[rows, :] + result).astype(BF)
            terms[0:1, :] += jnp.sum(grad * values * scale, axis=0, keepdims=True)
            return carry

        lax.fori_loop(0, x.shape[0] // tile, some, 0)
        term_sum.start_seq()

    def line_copy(src, way, s, block):
        buffer, send, recv = (up, up_send, up_recv) if way == 0 else (down, down_send, down_recv)
        to = me_f + 1 if way == 0 else me_f - 1
        place = buffer.at[block, s]
        return remote(
            place if src is None else src, place, send.at[block, s], recv.at[block, s], (me_s, to)
        )

    def done_copy(i):
        s = (me_s + i) % n_seq
        return remote(done.at[s], got.at[me_s], done_send.at[i], done_recv.at[me_s], (s, me_f))

    def stream(way, number):
        buffer = up if way == 0 else down
        behind = me_f if way == 0 else n_fsdp - 1 - me_f
        turn, i = number // n_seq, number % n_seq
        s = (me_s + i) % n_seq
        block = n_fsdp - 1 - turn if way == 0 else turn
        ahead = n_fsdp - 1 - behind
        on_time = (number >= 0) & (turn < ahead)
        finishes_up = (me_f == n_fsdp - 1) | ((n_fsdp - 1 > 2 * me_f) & (me_f > 0))

        @pl.when(on_time & (behind == 0))
        def _():
            line_copy(part.at[s, block], way, s, block).start()

        @pl.when(on_time & (behind > 0))
        def _():
            line_copy(None, way, s, block).wait_recv()
            total = buffer[block, s].astype(F32) + part[s, block].astype(F32)
            buffer[block, s] = total.astype(BF)
            line_copy(None, way, s, block).start()

        @pl.when((number >= 0) & (turn == ahead) & (behind > 0))
        def _():
            line_copy(None, way, s, me_f).wait_recv()
            done[s] = (done[s].astype(F32) + buffer[me_f, s].astype(F32)).astype(BF)

            @pl.when(finishes_up if way == 0 else jnp.logical_not(finishes_up))
            def _():
                @pl.when(i > 0)
                def _():
                    done_copy(i).start()

    lag = 2
    slots = n_seq * (n_fsdp - 1) + lag * (n_fsdp - 1)

    def run(first, last):
        def slot(number, carry):
            stream(0, number - lag * me_f)
            stream(1, number - lag * (n_fsdp - 1 - me_f))
            return carry

        lax.fori_loop(first, last, slot, 0)

    def begin(i, carry):
        done[i] = part[i, me_f]
        return carry

    lax.fori_loop(0, n_seq, begin, 0)
    reached = 0
    for number, event in enumerate(
        reduce.events(one)
        + [(0, input_rows), (3, functools.partial(term_sum.start_fsdp, heads[...]))]
    ):
        run(reached, min(slots, reached + event[0]))
        reached = min(slots, reached + event[0])
        event[1]()
    run(reached, slots)

    def place(s, rows):
        for third in range(3):
            columns = pl.ds(pl.multiple_of(third * width + s * head_width, 128), head_width)
            qkv_out[:, columns] = rows[:, third * head_width : (third + 1) * head_width].astype(F32)

    place(me_s, done[me_s])

    def arrived(i, carry):
        s = (me_s + i) % n_seq
        remote(done.at[s], got.at[s], done_send.at[i], done_recv.at[s], (s, me_f)).wait_recv()
        place(s, got[s])
        return carry

    lax.fori_loop(1, n_seq, arrived, 0)

    def all_sent(i, carry):
        s = (me_s + i) % n_seq

        @pl.when(i > 0)
        def _():
            done_copy(i).wait_send()

        for j in range(n_fsdp - 1):

            @pl.when(me_f + j < n_fsdp - 1)
            def _():
                line_copy(None, 0, s, n_fsdp - 1 - j).wait_send()

            @pl.when(j < me_f)
            def _():
                line_copy(None, 1, s, j).wait_send()

        return carry

    lax.fori_loop(0, n_seq, all_sent, 0)
    reduce.sent()
    total[...] = term_sum.finish()


def last_reduce(a, w, part, x, mid, gains, terms, heads, n_seq, n_fsdp, collective_id):
    rows, width = a.shape[0] // n_seq, w.shape[0]
    owned, columns = part.shape[2:]
    vmem = pl.BlockSpec(memory_space=pltpu.VMEM)
    dma = pltpu.SemaphoreType.DMA
    return pl.pallas_call(
        functools.partial(last_kernel, n_seq, n_fsdp),
        out_shape=[
            jax.ShapeDtypeStruct((rows, width), BF),
            jax.ShapeDtypeStruct((owned, n_seq * columns), F32),
            jax.ShapeDtypeStruct(heads.shape, F32),
        ],
        in_specs=[vmem] * 8,
        out_specs=[vmem] * 3,
        scratch_shapes=[
            pltpu.VMEM((n_fsdp, n_seq, owned, columns), BF),
            pltpu.VMEM((n_fsdp, n_seq, owned, columns), BF),
            pltpu.VMEM((n_seq, owned, columns), BF),
            pltpu.VMEM((n_seq, owned, columns), BF),
            dma((n_fsdp, n_seq)),
            dma((n_fsdp, n_seq)),
            dma((n_fsdp, n_seq)),
            dma((n_fsdp, n_seq)),
            dma((n_seq,)),
            dma((n_seq,)),
            pltpu.VMEM((rows, width), F32),
            pltpu.VMEM(terms.shape, F32),
        ]
        + term_scratch(n_seq, n_fsdp, heads.shape)
        + reduce_scratch(n_seq, rows, width),
        compiler_params=pltpu.CompilerParams(
            collective_id=collective_id, has_side_effects=True, vmem_limit_bytes=50 << 20
        ),
        cost_estimate=pl.CostEstimate(flops=0, bytes_accessed=1 << 27, transcendentals=0),
        name="last_reduce",
    )(a.reshape(n_seq, rows, -1), w, part, x, mid, gains, terms, heads)


def chunked(total, size, body):
    def step(i, carry):
        body(pl.ds(pl.multiple_of(i * size, size), size))
        return carry

    lax.fori_loop(0, total // size, step, 0)


def dispatch_kernel(n_seq, n_fsdp, pieces, x, hot, gates, masked, gates_out, masked_out, *refs):
    outs = refs[:pieces]
    (
        gathered,
        send,
        own_sem,
        line_send,
        line_recv,
        row_send,
        row_recv,
        masked_rows,
        masked_sem,
    ) = refs[pieces : pieces + 9]
    gate_exchange = Exchange(n_seq, n_fsdp, gates, gates_out, refs[pieces + 9 :])
    me_s, me_f = lax.axis_index("seq"), lax.axis_index("fsdp")
    width = x.shape[1]
    capacity = outs[0].shape[2]
    greet_all(n_seq, n_fsdp)

    def line_copy(step, block, way, to):
        src = x if step == 0 else gathered.at[block]
        return remote(
            src, gathered.at[block], line_send.at[way, step], line_recv.at[block], (me_s, to)
        )

    def row_copy(block, i, piece):
        other = (me_s + i) % n_seq
        return remote(
            send.at[block, other, piece],
            outs[piece].at[me_s, block],
            row_send.at[block, i, piece],
            row_recv.at[me_s, block, piece],
            (other, me_f),
        )

    def own_copy(block, piece):
        return pltpu.make_async_copy(
            send.at[block, me_s, piece], outs[piece].at[me_s, block], own_sem.at[block, piece]
        )

    def scatter(block, rows):
        def some(columns):
            picked = dot(hot[block], rows[:, columns], 1, 0).astype(BF)
            send[block, :, :, :, columns] = picked.reshape(n_seq, pieces, capacity, -1)

        chunked(width, 512, some)
        for i in range(1, n_seq):
            for piece in range(pieces):
                row_copy(block, i, piece).start()
        for piece in range(pieces):
            own_copy(block, piece).start()

    def masked_copy(block):
        return pltpu.make_async_copy(
            masked_rows.at[block % 2], masked_out.at[:, :, block], masked_sem.at[block % 2]
        )

    def lay_masked(block):
        if block >= 2:
            masked_copy(block - 2).wait()

        def some(columns):
            picked = dot(hot[block], masked[block, :, columns], 1, 0).astype(BF)
            masked_rows[block % 2, :, :, :, columns] = picked.reshape(n_seq, pieces, capacity, -1)

        chunked(width, 512, some)
        masked_copy(block).start()

    @pl.when(me_f + 1 < n_fsdp)
    def _():
        line_copy(0, me_f, 0, me_f + 1).start()

    @pl.when(me_f >= 1)
    def _():
        line_copy(0, me_f, 1, me_f - 1).start()

    scatter(me_f, x)
    gate_exchange.start()
    lay_masked(0)
    for step in range(1, n_fsdp):
        line_step(
            n_fsdp,
            step,
            lambda block: line_copy(1, block, 0, me_f).wait_recv(),
            lambda block, way, to: line_copy(step, block, way, to).start(),
        )

        @pl.when(me_f - step >= 0)
        def _():
            scatter(me_f - step, gathered.at[me_f - step])

        @pl.when(me_f + step < n_fsdp)
        def _():
            scatter(me_f + step, gathered.at[me_f + step])

        lay_masked(step)

    for step in range(n_fsdp):
        line_sent(
            n_fsdp, step, lambda block, way, to: line_copy(step, block, way, to).wait_send()
        )
    for block in range(n_fsdp):
        for piece in range(pieces):
            own_copy(block, piece).wait()
            for i in range(1, n_seq):
                source = (me_s + i) % n_seq
                row_copy(block, i, piece).wait_send()
                remote(
                    send.at[block, source, piece],
                    outs[piece].at[source, block],
                    row_send.at[block, i, piece],
                    row_recv.at[source, block, piece],
                    (source, me_f),
                ).wait_recv()
    gate_exchange.finish()
    for block in range(max(0, n_fsdp - 2), n_fsdp):
        masked_copy(block).wait()


def dispatch_rows(x, hot, gates, masked, n_seq, n_fsdp, pieces, capacity, collective_id):
    rows, width = x.shape
    vmem = pl.BlockSpec(memory_space=pltpu.VMEM)
    dma = pltpu.SemaphoreType.DMA
    return pl.pallas_call(
        functools.partial(dispatch_kernel, n_seq, n_fsdp, pieces),
        out_shape=[
            jax.ShapeDtypeStruct(gates.shape, F32),
            jax.ShapeDtypeStruct((n_seq, pieces, n_fsdp, capacity, width), BF),
        ]
        + [jax.ShapeDtypeStruct((n_seq, n_fsdp, capacity, width), BF)] * pieces,
        in_specs=[vmem] * 4,
        out_specs=[vmem] + [pl.BlockSpec(memory_space=pl.ANY)] * (pieces + 1),
        scratch_shapes=[
            pltpu.VMEM((n_fsdp, rows, width), BF),
            pltpu.VMEM((n_fsdp, n_seq, pieces, capacity, width), BF),
            dma((n_fsdp, pieces)),
            dma((2, n_fsdp)),
            dma((n_fsdp,)),
            dma((n_fsdp, n_seq, pieces)),
            dma((n_seq, n_fsdp, pieces)),
            pltpu.VMEM((2, n_seq, pieces, capacity, width), BF),
            dma((2,)),
        ]
        + exchange_sems(n_seq * n_fsdp),
        compiler_params=pltpu.CompilerParams(
            collective_id=collective_id, has_side_effects=True, vmem_limit_bytes=40 << 20
        ),
        name="dispatch_rows",
    )(x, hot, gates, masked)


def return_kernel(n_seq, n_fsdp, pieces, hot, gates, *refs):
    rows = refs[:pieces]
    out, gates_out, got, parts, sums, own_sem, row_send, row_recv, part_send, part_recv = refs[
        pieces : pieces + 10
    ]
    gate_exchange = Exchange(n_seq, n_fsdp, gates, gates_out, refs[pieces + 10 :])
    me_s, me_f = lax.axis_index("seq"), lax.axis_index("fsdp")
    width = out.shape[1]
    capacity = rows[0].shape[2]
    greet_all(n_seq, n_fsdp)

    def row_copy(j, i, piece):
        other, block = (me_s + i) % n_seq, (me_f + j) % n_fsdp
        return remote(
            rows[piece].at[other, block],
            got.at[block, me_s, piece],
            row_send.at[j % n_fsdp, i, piece],
            row_recv.at[block, me_s, piece],
            (other, me_f),
        )

    def own_copy(j, piece):
        block = (me_f + j) % n_fsdp
        return pltpu.make_async_copy(
            rows[piece].at[me_s, block], got.at[block, me_s, piece], own_sem.at[j % n_fsdp, piece]
        )

    def part_copy(j):
        block = (me_f + j) % n_fsdp
        return remote(
            parts.at[block], sums.at[me_f], part_send.at[j], part_recv.at[me_f], (me_s, block)
        )

    for j in range(1, n_fsdp + 1):
        for piece in range(pieces):
            for i in range(1, n_seq):
                row_copy(j, i, piece).start()
            own_copy(j, piece).start()
    gate_exchange.start()
    for j in range(1, n_fsdp + 1):
        block = (me_f + j) % n_fsdp
        for piece in range(pieces):
            own_copy(j, piece).wait()
            for i in range(1, n_seq):
                source = (me_s + i) % n_seq
                remote(
                    rows[piece].at[source, block],
                    got.at[block, source, piece],
                    row_send.at[0, i, piece],
                    row_recv.at[block, source, piece],
                    (source, me_f),
                ).wait_recv()

        def some(columns):
            arrived = got[block, :, :, :, columns].reshape(n_seq * pieces * capacity, -1)
            total = dot(hot[block], arrived, 1, 0)
            if j < n_fsdp:
                parts[block, :, columns] = total.astype(BF)
            else:
                out[:, columns] = total

        chunked(width, 512, some)
        if j < n_fsdp:
            part_copy(j).start()
    for j in range(1, n_fsdp):
        source = (me_f + n_fsdp - j) % n_fsdp
        remote(
            parts.at[source], sums.at[source], part_send.at[j], part_recv.at[source], (me_s, source)
        ).wait_recv()

    def add(columns):
        total = out[:, columns]
        for j in range(1, n_fsdp):
            total = total + sums[(me_f + j) % n_fsdp, :, columns].astype(F32)
        out[:, columns] = total

    chunked(width, 512, add)
    for j in range(1, n_fsdp):
        part_copy(j).wait_send()
    for j in range(1, n_fsdp + 1):
        for piece in range(pieces):
            for i in range(1, n_seq):
                row_copy(j, i, piece).wait_send()
    gate_exchange.finish()


def return_rows(piece_rows, hot, gates, n_seq, n_fsdp, collective_id):
    pieces = len(piece_rows)
    capacity, width = piece_rows[0].shape[2:]
    count = hot.shape[1]
    vmem = pl.BlockSpec(memory_space=pltpu.VMEM)
    dma = pltpu.SemaphoreType.DMA
    return pl.pallas_call(
        functools.partial(return_kernel, n_seq, n_fsdp, pieces),
        out_shape=[
            jax.ShapeDtypeStruct((count, width), F32),
            jax.ShapeDtypeStruct(gates.shape, F32),
        ],
        in_specs=[vmem, vmem] + [pl.BlockSpec(memory_space=pl.ANY)] * pieces,
        out_specs=[vmem, vmem],
        scratch_shapes=[
            pltpu.VMEM((n_fsdp, n_seq, pieces, capacity, width), BF),
            pltpu.VMEM((n_fsdp, count, width), BF),
            pltpu.VMEM((n_fsdp, count, width), BF),
            dma((n_fsdp, pieces)),
            dma((n_fsdp, n_seq, pieces)),
            dma((n_fsdp, n_seq, pieces)),
            dma((n_fsdp,)),
            dma((n_fsdp,)),
        ]
        + exchange_sems(n_seq * n_fsdp),
        compiler_params=pltpu.CompilerParams(
            collective_id=collective_id, has_side_effects=True, vmem_limit_bytes=40 << 20
        ),
        name="return_rows",
    )(hot, gates, *piece_rows)


def weight_grad_kernel(a, b, *refs):
    refs[-1][0] = dot(a[...], b[0], 0, 0)


def weight_grad(a, b, whole, piece, pieces, part):
    rows, m = a.shape
    parts, _, n = b.shape
    tile = min(256, m)
    more = [] if whole is None else [whole]
    return pl.pallas_call(
        weight_grad_kernel,
        out_shape=jax.ShapeDtypeStruct((pieces, m, n * parts), F32),
        grid=(m // tile,),
        in_specs=[
            pl.BlockSpec((rows, tile), lambda i: (0, i)),
            pl.BlockSpec((1, rows, n), lambda i: (part, 0, 0)),
        ]
        + [pl.BlockSpec(memory_space=pl.ANY)] * len(more),
        out_specs=pl.BlockSpec((1, tile, n), lambda i: (piece, i, part)),
        input_output_aliases={2: 0} if more else {},
        cost_estimate=pl.CostEstimate(
            flops=2 * rows * m * n,
            bytes_accessed=2 * rows * (m + n) + 4 * m * n,
            transcendentals=0,
        ),
        name="weight_grad",
    )(a, b, *more)


def seq_tile(n_seq, rows_each):
    tile = n_seq
    while tile > 1 and (tile * rows_each > 1024 or n_seq % tile):
        tile -= 1
    return tile


def expert_forward_kernel(x, gates, w_gate, w_up, w_down, *refs):
    hidden, activation, out, scaled, total = refs[-5:]
    step = pl.program_id(1)
    gate = dot(x[...], w_gate[0], 1, 0)
    up = dot(x[...], w_up[0], 1, 0)
    hidden[0] = gate
    hidden[1] = up
    act = (gate * jax.nn.sigmoid(gate) * up).astype(BF)
    activation[...] = act
    product = dot(act, w_down[0], 1, 0)

    @pl.when(step == 0)
    def _():
        total[...] = product

    @pl.when(step > 0)
    def _():
        total[...] += product

    @pl.when(step == pl.num_programs(1) - 1)
    def _():
        low = total[...].astype(BF)
        out[...] = low
        scaled[...] = (low.astype(F32) * gates[...]).astype(BF).reshape(scaled.shape)


def expert_forward(x, gates, w_up, w_down, whole, piece, n_seq, n_fsdp):
    rows, width = x.shape
    pieces, ff = w_down.shape[:2]
    capacity = rows // (n_seq * n_fsdp)
    tile = min(256, ff)
    steps = ff // tile
    spans = seq_tile(n_seq, n_fsdp * capacity)
    count = spans * n_fsdp * capacity
    more = [] if whole is None else [whole]
    fixed = lambda r, i: (r, 0)
    return pl.pallas_call(
        expert_forward_kernel,
        out_shape=[
            jax.ShapeDtypeStruct((2, rows, ff), F32),
            jax.ShapeDtypeStruct((rows, ff), BF),
            jax.ShapeDtypeStruct((rows, width), BF),
            jax.ShapeDtypeStruct((n_seq, pieces, n_fsdp, capacity, width), BF),
        ],
        grid=(rows // count, steps),
        in_specs=[
            pl.BlockSpec((count, width), fixed),
            pl.BlockSpec((count, 1), fixed),
            pl.BlockSpec((1, width, tile), lambda r, i: (piece, 0, i)),
            pl.BlockSpec((1, width, tile), lambda r, i: (piece, 0, steps + i)),
            pl.BlockSpec((1, tile, width), lambda r, i: (piece, i, 0)),
        ]
        + [pl.BlockSpec(memory_space=pl.ANY)] * len(more),
        out_specs=[
            pl.BlockSpec((2, count, tile), lambda r, i: (0, r, i)),
            pl.BlockSpec((count, tile), lambda r, i: (r, i)),
            pl.BlockSpec((count, width), fixed),
            pl.BlockSpec((spans, 1, n_fsdp, capacity, width), lambda r, i: (r, piece, 0, 0, 0)),
        ],
        scratch_shapes=[pltpu.VMEM((count, width), F32)],
        input_output_aliases={5: 3} if more else {},
        compiler_params=pltpu.CompilerParams(vmem_limit_bytes=56 << 20),
        cost_estimate=pl.CostEstimate(
            flops=6 * rows * width * ff, bytes_accessed=6 * width * ff, transcendentals=rows * ff
        ),
        name="expert_forward",
    )(x, gates, w_up, w_up, w_down, *more)


def expert_backward_kernel(masked, gates, piece_out, hidden, w_down, out, grad, inner, partial):
    @pl.when(pl.program_id(1) == 0)
    def _():
        partial[...] = jnp.zeros_like(partial)

        def some(columns):
            low = masked[:, 0, :, :, columns].reshape(grad.shape[0], -1).astype(F32)
            grad[:, columns] = (low * gates[...]).astype(BF)
            product = low * piece_out[:, columns].astype(F32)
            for i in range(product.shape[1] // 128):
                partial[...] += product[:, i * 128 : (i + 1) * 128]

        chunked(grad.shape[1], 512, some)
        sums = jnp.sum(partial[...].T, axis=0, keepdims=True)
        inner[...] = jnp.broadcast_to(sums, inner.shape)

    act_grad = dot(grad[...], w_down[0], 1, 1)
    gate, up = hidden[0], hidden[1]
    sigmoid = jax.nn.sigmoid(gate)
    out[0] = (act_grad * up * sigmoid * (1.0 + gate * (1.0 - sigmoid))).astype(BF)
    out[1] = (act_grad * gate * sigmoid).astype(BF)


def expert_backward(masked, gates, piece_out, hidden, w_down, piece):
    rows, width = piece_out.shape
    ff = w_down.shape[1]
    n_seq, _, n_fsdp, capacity, _ = masked.shape
    tile = min(256, ff)
    spans = seq_tile(n_seq, n_fsdp * capacity)
    count = spans * n_fsdp * capacity
    part = pl.BlockSpec((2, count, tile), lambda r, i: (0, r, i))
    fixed = lambda r, i: (r, 0)
    return pl.pallas_call(
        expert_backward_kernel,
        out_shape=[
            jax.ShapeDtypeStruct((2, rows, ff), BF),
            jax.ShapeDtypeStruct((rows, width), BF),
            jax.ShapeDtypeStruct((8, rows), F32),
        ],
        grid=(rows // count, ff // tile),
        in_specs=[
            pl.BlockSpec((spans, 1, n_fsdp, capacity, width), lambda r, i: (r, piece, 0, 0, 0)),
            pl.BlockSpec((count, 1), fixed),
            pl.BlockSpec((count, width), fixed),
            part,
            pl.BlockSpec((1, tile, width), lambda r, i: (piece, i, 0)),
        ],
        out_specs=[
            part,
            pl.BlockSpec((count, width), fixed),
            pl.BlockSpec((8, count), lambda r, i: (0, r)),
        ],
        scratch_shapes=[pltpu.VMEM((count, 128), F32)],
        compiler_params=pltpu.CompilerParams(vmem_limit_bytes=48 << 20),
        cost_estimate=pl.CostEstimate(
            flops=2 * rows * width * ff, bytes_accessed=12 * rows * ff, transcendentals=rows * ff
        ),
        name="expert_backward",
    )(masked, gates, piece_out, hidden, w_down)


def expert_input_kernel(grad, w_up, out):
    ff = grad.shape[2]
    total = dot(grad[0], w_up[0, :, :ff], 1, 1) + dot(grad[1], w_up[0, :, ff:], 1, 1)
    out[...] = total.astype(BF)


def expert_input(grad, w_up, piece):
    rows, ff = grad.shape[1:]
    width = w_up.shape[1]
    tile = min(256, width)
    return pl.pallas_call(
        expert_input_kernel,
        out_shape=jax.ShapeDtypeStruct((rows, width), BF),
        grid=(width // tile,),
        in_specs=[
            pl.BlockSpec((2, rows, ff), lambda i: (0, 0, 0)),
            pl.BlockSpec((1, tile, 2 * ff), lambda i: (piece, i, 0)),
        ],
        out_specs=pl.BlockSpec((rows, tile), lambda i: (0, i)),
        cost_estimate=pl.CostEstimate(
            flops=4 * rows * width * ff, bytes_accessed=4 * width * ff, transcendentals=0
        ),
        name="expert_input",
    )(grad, w_up)


class SeqShare:
    def __init__(self, n_seq, own, every, send_sem, recv_sem):
        self.n_seq, self.own, self.every = n_seq, own, every
        self.send_sem, self.recv_sem = send_sem, recv_sem
        self.me_s, self.me_f = lax.axis_index("seq"), lax.axis_index("fsdp")

    def copy(self, i, place):
        other = (self.me_s + i) % self.n_seq
        return remote(
            self.own,
            self.every.at[place],
            self.send_sem.at[i],
            self.recv_sem.at[place],
            (other, self.me_f),
        )

    def total(self):
        for i in range(1, self.n_seq):
            self.copy(i, self.me_s).start()
        total = self.own[...]
        for i in range(1, self.n_seq):
            place = (self.me_s + i) % self.n_seq
            self.copy(i, place).wait_recv()
            total = total + self.every[place]
        for i in range(1, self.n_seq):
            self.copy(i, self.me_s).wait_send()
        return total


def share_scratch(n_seq, shape):
    dma = pltpu.SemaphoreType.DMA
    return [pltpu.VMEM(shape, F32), pltpu.VMEM((n_seq,) + shape, F32), dma((n_seq,)), dma((n_seq,))]


def row_sums(values):
    ones = jnp.ones((8, values.shape[1]), F32)
    return lax.dot_general(
        ones,
        values,
        (((1,), (1,)), ((), ())),
        preferred_element_type=F32,
        precision=lax.Precision.HIGHEST,
    )


def front_kernel(n_seq, x, gain, w, normed, raw, totals, *scratch):
    greet_seq(n_seq)
    share = SeqShare(n_seq, *scratch)
    head_width = w.shape[1] // 3
    tile = 256

    def some(i, carry):
        rows = pl.ds(pl.multiple_of(i * tile, tile), tile)
        values = x[rows, :].astype(F32)
        scale = lax.rsqrt(jnp.mean(values * values, axis=-1, keepdims=True) + epsilon)
        low = (values * scale * gain[0:1, :]).astype(BF)
        normed[rows, :] = low
        result = dot(low, w[...], 1, 0)
        raw[rows, :] = result
        for part in range(2):
            piece = result[:, part * head_width : (part + 1) * head_width]
            share.own[part : part + 1, rows] = row_sums(piece * piece)[0:1]
        return carry

    share.own[...] = jnp.zeros_like(share.own)
    lax.fori_loop(0, x.shape[0] // tile, some, 0)
    totals[...] = share.total()


def front(x, gains, w, n_seq, collective_id):
    rows, width = x.shape
    vmem = pl.BlockSpec(memory_space=pltpu.VMEM)
    return pl.pallas_call(
        functools.partial(front_kernel, n_seq),
        out_shape=[
            jax.ShapeDtypeStruct((rows, width), BF),
            jax.ShapeDtypeStruct((rows, w.shape[1]), F32),
            jax.ShapeDtypeStruct((8, rows), F32),
        ],
        in_specs=[vmem] * 3,
        out_specs=[vmem] * 3,
        scratch_shapes=share_scratch(n_seq, (8, rows)),
        compiler_params=pltpu.CompilerParams(
            collective_id=collective_id, has_side_effects=True, vmem_limit_bytes=40 << 20
        ),
        name="front",
    )(x, gains, w)


def column_rms(sums, part, width):
    return lax.rsqrt(sums.T[:, part : part + 1] / width + epsilon)


def turned(values, cosine, sine):
    return values * cosine + pltpu.roll(values, values.shape[1] // 2, 1) * sine


def softmax_columns(k, q, length, scaling):
    scores = dot(k, q, 1, 1) * scaling
    key = lax.broadcasted_iota(jnp.int32, scores.shape, 0)
    scores = jnp.where(key < length, scores, -1e30)
    weights = jnp.exp(scores - jnp.max(scores, axis=0, keepdims=True))
    return weights / jnp.sum(weights, axis=0, keepdims=True)


def attend_kernel(
    width,
    length,
    raw_q,
    raw_k,
    raw_v,
    q_sums,
    k_sums,
    gain,
    q_cos,
    q_sin,
    k_cos,
    k_sin,
    o_ref,
    q_ref,
    k_ref,
    v_ref,
):
    scaling = raw_q.shape[1] ** (-0.5)

    @pl.when(pl.program_id(1) == 0)
    def _():
        key = raw_k[...] * column_rms(k_sums[...], 1, width) * gain[2:3, :]
        k_ref[...] = turned(key, k_cos[...], k_sin[...]).astype(BF)
        v_ref[...] = raw_v[...].astype(BF)

    query = raw_q[...] * column_rms(q_sums[...], 0, width) * gain[1:2, :]
    query = turned(query, q_cos[...], q_sin[...]).astype(BF)
    q_ref[...] = query
    probs = softmax_columns(k_ref[...], query, length[0], scaling).astype(BF)
    o_ref[...] = dot(v_ref[...], probs, 0, 0).T.astype(BF)


def attend(raw, totals, gains, cosine, sine, length, block, width):
    slot_len, head_width = raw.shape[0], raw.shape[1] // 3
    hd = cosine.shape[1]
    heads = head_width // hd
    rows = lambda shift: pl.BlockSpec((block, hd), lambda h, i, n: (i, shift + h))
    full = lambda shift: pl.BlockSpec((slot_len, hd), lambda h, i, n: (0, shift + h))
    table = pl.BlockSpec((block, hd), lambda h, i, n: (i, 0))
    whole_table = pl.BlockSpec((slot_len, hd), lambda h, i, n: (0, 0))
    return pl.pallas_call(
        functools.partial(attend_kernel, width),
        out_shape=[jax.ShapeDtypeStruct((slot_len, head_width), BF)] * 4,
        grid_spec=pltpu.PrefetchScalarGridSpec(
            num_scalar_prefetch=1,
            grid=(heads, slot_len // block),
            in_specs=[
                rows(0),
                full(heads),
                full(2 * heads),
                pl.BlockSpec((8, block), lambda h, i, n: (0, i)),
                pl.BlockSpec((8, slot_len), lambda h, i, n: (0, 0)),
                pl.BlockSpec((4, hd), lambda h, i, n: (0, h)),
                table,
                table,
                whole_table,
                whole_table,
            ],
            out_specs=[rows(0), rows(0), full(0), full(0)],
        ),
        cost_estimate=pl.CostEstimate(
            flops=4 * heads * slot_len * slot_len * hd, bytes_accessed=1 << 23, transcendentals=0
        ),
        name="attend",
    )(length, raw, raw, raw, totals, totals, gains, cosine, sine, cosine, sine)


def attend_back_kernel(
    width,
    length,
    q_ref,
    k_ref,
    v_ref,
    g_ref,
    raw_q,
    raw_k,
    q_sums,
    k_sums,
    gain,
    q_cos,
    q_sin,
    k_cos,
    k_sin,
    dq_ref,
    dk_ref,
    dv_ref,
    dots,
    gain_out,
    dk_sum,
    dv_sum,
):
    head, step = pl.program_id(0), pl.program_id(1)
    last = step == pl.num_programs(1) - 1
    block, hd = q_ref.shape
    scaling = hd ** (-0.5)

    @pl.when(step == 0)
    def _():
        dk_sum[...] = jnp.zeros_like(dk_sum)
        dv_sum[...] = jnp.zeros_like(dv_sum)
        gain_out[...] = jnp.zeros_like(gain_out)

        @pl.when(head == 0)
        def _():
            dots[...] = jnp.zeros_like(dots)

    q, k, v, g = q_ref[...], k_ref[...], v_ref[...], g_ref[...]
    probs = softmax_columns(k, q, length[0], scaling)
    dv_sum[...] += dot(probs.astype(BF), g, 1, 0)
    weights_grad = dot(v, g, 1, 1)
    inner = jnp.sum(probs * weights_grad, axis=0, keepdims=True)
    score_grad = (probs * (weights_grad - inner) * scaling).astype(BF)
    dk_sum[...] += dot(score_grad, q, 1, 0)
    query_grad = dot(k, score_grad, 0, 0).T.astype(BF).astype(F32)
    query_in = turned(query_grad, q_cos[...], -q_sin[...])
    dq_ref[...] = query_in
    product = query_in * raw_q[...]
    rows = pl.ds(pl.multiple_of(step * block, block), block)
    dots[0:1, rows] += row_sums(product * gain[1:2, :])[0:1]
    gain_out[0:1, :] += jnp.sum(
        product * column_rms(q_sums[...], 0, width), axis=0, keepdims=True
    )

    @pl.when(last)
    def _():
        key_in = turned(dk_sum[...].astype(BF).astype(F32), k_cos[...], -k_sin[...])
        dk_ref[...] = key_in
        dv_ref[...] = dv_sum[...].astype(BF)
        product = key_in * raw_k[...]
        dots[1:2, :] += row_sums(product * gain[2:3, :])[0:1]
        gain_out[1:2, :] = jnp.sum(
            product * column_rms(k_sums[...], 1, width), axis=0, keepdims=True
        )


def attend_back(query, key, value, grad, raw, totals, gains, cosine, sine, length, block, width):
    slot_len, head_width = query.shape
    hd = cosine.shape[1]
    heads = head_width // hd
    rows = pl.BlockSpec((block, hd), lambda h, i, n: (i, h))
    full = lambda shift: pl.BlockSpec((slot_len, hd), lambda h, i, n: (0, shift + h))
    table = pl.BlockSpec((block, hd), lambda h, i, n: (i, 0))
    whole_table = pl.BlockSpec((slot_len, hd), lambda h, i, n: (0, 0))
    return pl.pallas_call(
        functools.partial(attend_back_kernel, width),
        out_shape=[
            jax.ShapeDtypeStruct(query.shape, F32),
            jax.ShapeDtypeStruct(query.shape, F32),
            jax.ShapeDtypeStruct(query.shape, BF),
            jax.ShapeDtypeStruct((8, slot_len), F32),
            jax.ShapeDtypeStruct((8, head_width), F32),
        ],
        grid_spec=pltpu.PrefetchScalarGridSpec(
            num_scalar_prefetch=1,
            grid=(heads, slot_len // block),
            in_specs=[
                rows,
                full(0),
                full(0),
                rows,
                rows,
                full(heads),
                pl.BlockSpec((8, block), lambda h, i, n: (0, i)),
                pl.BlockSpec((8, slot_len), lambda h, i, n: (0, 0)),
                pl.BlockSpec((4, hd), lambda h, i, n: (0, h)),
                table,
                table,
                whole_table,
                whole_table,
            ],
            out_specs=[
                rows,
                full(0),
                full(0),
                pl.BlockSpec((8, slot_len), lambda h, i, n: (0, 0)),
                pl.BlockSpec((8, hd), lambda h, i, n: (0, h)),
            ],
            scratch_shapes=[pltpu.VMEM((slot_len, hd), F32), pltpu.VMEM((slot_len, hd), F32)],
        ),
        cost_estimate=pl.CostEstimate(
            flops=20 * heads * slot_len * slot_len * hd, bytes_accessed=1 << 24, transcendentals=0
        ),
        name="attend_back",
    )(
        length,
        query,
        key,
        value,
        grad,
        raw,
        raw,
        totals,
        totals,
        gains,
        cosine,
        sine,
        cosine,
        sine,
    )


def raw_back_kernel(
    n_seq, n_fsdp, width, dq, dk, dv, raw, totals, gain, dots, terms, out, terms_out, *scratch
):
    greet_lines(n_seq, n_fsdp)
    share = SeqShare(n_seq, *scratch[:4])
    term_sum = TermSum(n_seq, n_fsdp, None, *scratch[4:6], None, None, *scratch[6:])
    term_sum.start_fsdp(terms[...])
    head_width = dq.shape[1]
    share.own[...] = dots[...]
    share.own[...] = share.total()
    tile = 256

    def some(i, carry):
        rows = pl.ds(pl.multiple_of(i * tile, tile), tile)
        inner = share.own[:, rows].T / width
        for part, grad in enumerate((dq, dk)):
            columns = slice(part * head_width, (part + 1) * head_width)
            scale = column_rms(totals[:, rows], part, width)
            weighted = grad[rows, :] * gain[part + 1 : part + 2, :]
            cube = scale * scale * scale
            result = scale * weighted - raw[rows, columns] * (cube * inner[:, part : part + 1])
            out[rows, columns] = result.astype(BF)
        out[rows, 2 * head_width :] = dv[rows, :]
        return carry

    lax.fori_loop(0, dq.shape[0] // tile, some, 0)
    terms_out[...] = term_sum.finish()


def raw_back(dq, dk, dv, raw, totals, gains, dots, terms, n_seq, n_fsdp, width, collective_id):
    vmem = pl.BlockSpec(memory_space=pltpu.VMEM)
    dma = pltpu.SemaphoreType.DMA
    return pl.pallas_call(
        functools.partial(raw_back_kernel, n_seq, n_fsdp, width),
        out_shape=[
            jax.ShapeDtypeStruct(raw.shape, BF),
            jax.ShapeDtypeStruct(terms.shape, F32),
        ],
        in_specs=[vmem] * 8,
        out_specs=[vmem] * 2,
        scratch_shapes=share_scratch(n_seq, dots.shape)
        + [
            pltpu.VMEM((n_seq,) + terms.shape, F32),
            pltpu.VMEM((n_fsdp,) + terms.shape, F32),
            dma((n_fsdp,)),
            dma((n_fsdp,)),
        ],
        compiler_params=pltpu.CompilerParams(
            collective_id=collective_id, has_side_effects=True, vmem_limit_bytes=40 << 20
        ),
        name="raw_back",
    )(dq, dk, dv, raw, totals, gains, dots, terms)


def rope_tables(positions, head_dim):
    half = head_dim // 2
    frequency = rope_base ** (-jnp.arange(half, dtype=F32) * 2.0 / head_dim)
    angles = positions.astype(F32)[:, None] * frequency[None, :]
    cosine, sine = jnp.cos(angles), jnp.sin(angles)
    return jnp.concatenate([cosine, cosine], axis=1), jnp.concatenate([-sine, sine], axis=1)


def places(block_routes, experts, capacity):
    count = block_routes.shape[0]
    match = (block_routes[:, :, None] == experts[None, None, :]).astype(F32).sum(axis=1)
    lower = jnp.tril(jnp.ones((count, count), BF), -1)
    rank = dot(lower, match.astype(BF), 1, 0)
    place = jnp.arange(capacity, dtype=F32)
    return match[:, :, None] * (rank[:, :, None] == place[None, None, :]).astype(F32)


def local(
    tokens,
    cotangent,
    lengths,
    routes,
    norm_gains,
    qkv_weight,
    proj_weight,
    router_weight,
    expert_up,
    expert_down,
):
    n_seq, n_fsdp = lax.axis_size("seq"), lax.axis_size("fsdp")
    n_dev = n_seq * n_fsdp
    me_s, me_f = lax.axis_index("seq"), lax.axis_index("fsdp")
    shard_len, width = tokens.shape[1], tokens.shape[2]
    slot_len = shard_len * n_seq
    experts = router_weight.shape[1]
    top_count = routes.shape[2]
    capacity = 3 * shard_len * top_count // (2 * experts)
    piece_ff = expert_down.shape[1]
    pieces_dev = expert_up.shape[0]
    split = FF // piece_ff
    head_dim = width // HEADS
    head_width = width // n_seq
    heads_dev = HEADS // n_seq
    owned = qkv_weight.shape[0]
    block = min(512, slot_len)
    length = lax.dynamic_slice_in_dim(lengths, me_f, 1)
    valid_total = jnp.sum(lengths).astype(F32).reshape(1)
    positions = me_s * shard_len + jnp.arange(shard_len, dtype=jnp.int32)
    row_valid = (positions < length[0]).astype(F32)
    local_routes = routes[0]
    push_all = functools.partial(push, n_seq=n_seq, n_fsdp=n_fsdp, scope="all")
    push_seq = functools.partial(push, n_seq=n_seq, n_fsdp=n_fsdp, scope="seq")

    gain_size, router_size = norm_gains.size, router_weight.size
    pieces = [norm_gains.reshape(-1), router_weight.reshape(-1), local_routes.astype(BF).reshape(-1)]
    small, slot_tokens, qkv_local = first_gather(
        rows_of(jnp.concatenate(pieces), 16),
        tokens[0],
        qkv_weight,
        n_seq,
        n_fsdp,
        collective_id=0,
    )
    slot_tokens = slot_tokens.reshape(slot_len, width)
    qkv_local = qkv_local.reshape(width, 3 * head_width)
    small = small.reshape(n_dev, -1)
    gains = small[:, :gain_size].reshape(n_dev, 4, owned).swapaxes(0, 1).reshape(4, width).astype(F32)
    router = small[:, gain_size : gain_size + router_size].reshape(width, experts)
    all_routes = small[:, gain_size + router_size :][:, : shard_len * top_count]
    all_routes = all_routes.reshape(n_seq, n_fsdp, shard_len, top_count).astype(jnp.int32)

    masked_low = jnp.where(row_valid[:, None] > 0, cotangent[0], jnp.zeros((), BF))
    proj_later = lax.optimization_barrier((proj_weight, slot_tokens))[0]
    proj_rows = lax.all_gather(proj_later, "fsdp", axis=0, tiled=True)

    plane_routes = lax.dynamic_index_in_dim(all_routes, me_s, 0, keepdims=False)
    piece_ids = (jnp.arange(n_seq)[:, None] * n_fsdp + me_f) * pieces_dev + jnp.arange(pieces_dev)
    plane_experts = (piece_ids // split).reshape(-1).astype(jnp.int32)
    plane_hot = jax.vmap(lambda r: places(r, plane_experts, capacity))(plane_routes)
    to_rows = plane_hot.reshape(n_fsdp, shard_len, -1).astype(BF)
    to_places = to_rows.swapaxes(1, 2)

    def exchange(rows):
        return lax.all_to_all(rows, "seq", split_axis=0, concat_axis=0, tiled=True)

    normed_one, raw, totals = front(slot_tokens, gains, qkv_local, n_seq, collective_id=1)
    masked_later = lax.optimization_barrier((masked_low, raw))[0]
    plane_masked = lax.all_gather(masked_later, "fsdp", axis=0)

    def combine(pieces_back):
        total = 0.0
        for piece in range(pieces_dev):
            back = pieces_back[:, piece]
            hot = to_rows.reshape(n_fsdp, shard_len, n_seq, pieces_dev, capacity)[:, :, :, piece]
            total = total + jnp.einsum("ftsc,sfcd->ftd", hot, back, preferred_element_type=F32)
        return total.astype(BF)

    def rms(values):
        return lax.rsqrt(jnp.mean(values * values, axis=-1, keepdims=True) + epsilon)

    own_gains = lax.dynamic_slice_in_dim(gains, me_s * head_width, head_width, 1)
    cosine, sine = rope_tables(jnp.arange(slot_len, dtype=jnp.int32), head_dim)
    attended, query, key, value = attend(
        raw, totals, own_gains, cosine, sine, length, block, width
    )

    resid_in = tokens[0].astype(F32)
    resid_mid = resid_in + product_reduced(attended, proj_rows, 0, n_seq, collective_id=8)
    mid_rms = rms(resid_mid)
    normed_two = (resid_mid * mid_rms * gains[3]).astype(BF)
    router_probs = jax.nn.softmax(jnp.dot(normed_two, router, preferred_element_type=F32), axis=-1)

    own_hot = places(local_routes, jnp.arange(experts, dtype=jnp.int32), capacity)
    gate_slot = jnp.sum(own_hot * router_probs[:, :, None], axis=0)
    gate_send = jnp.broadcast_to(gate_slot[:, None], (experts, split, capacity))
    gate_send = gate_send.reshape(n_dev, pieces_dev * capacity)
    gate_pad = -pieces_dev * capacity % 1024
    gate_send = jnp.pad(gate_send, ((0, 0), (0, gate_pad))).reshape(n_dev, -1, 128)
    gate_recv, cot_rows, *piece_rows = dispatch_rows(
        normed_two,
        to_places,
        gate_send,
        plane_masked,
        n_seq,
        n_fsdp,
        pieces_dev,
        capacity,
        collective_id=6,
    )
    cot_all = exchange(cot_rows)
    gate_recv = gate_recv.reshape(n_dev, -1)[:, : pieces_dev * capacity]
    gate_recv = gate_recv.reshape(n_dev, pieces_dev, capacity)

    forward = []
    outs = None
    for piece in range(pieces_dev):
        gate_rows = gate_recv[:, piece].reshape(-1, 1)
        rows = piece_rows[piece].reshape(-1, width)
        result = expert_forward(rows, gate_rows, expert_up, expert_down, outs, piece, n_seq, n_fsdp)
        outs = result[-1]
        forward.append((gate_rows, rows) + tuple(result[:-1]))
    outs_back = exchange(outs)
    cot_all, forward = lax.optimization_barrier((cot_all, forward))
    backs, gate_backs = [], []
    up_grad = down_grad = None
    for piece in range(pieces_dev):
        gate_rows, rows, hidden, activation, piece_out = forward[piece]
        hidden_grad, out_grad, gate_back = expert_backward(
            cot_all, gate_rows, piece_out, hidden, expert_down, piece
        )
        gate_backs.append(gate_back[0].reshape(n_dev, capacity))
        backs.append(expert_input(hidden_grad, expert_up, piece))
        down_grad = weight_grad(activation, out_grad[None], down_grad, piece, pieces_dev, 0)
        for part in range(2):
            up_grad = weight_grad(rows, hidden_grad, up_grad, piece, pieces_dev, part)
    back_send = jnp.stack(gate_backs, axis=1).reshape(n_dev, pieces_dev * capacity)
    back_send = jnp.pad(back_send, ((0, 0), (0, gate_pad))).reshape(n_dev, -1, 128)
    backs, outs_back, up_grad, down_grad = lax.optimization_barrier(
        (backs, outs_back, up_grad, down_grad)
    )
    backs = [rows.reshape(n_seq, n_fsdp, capacity, width) for rows in backs]
    normed_two_grad, back_recv = return_rows(
        backs, to_rows, back_send, n_seq, n_fsdp, collective_id=7
    )
    outs_back = lax.optimization_barrier((outs_back, normed_two_grad))[0]
    outs_sums = combine(outs_back)

    seen = (all_routes[..., None] == jnp.arange(experts, dtype=jnp.int32)).astype(BF)
    live = jnp.arange(slot_len, dtype=jnp.int32).reshape(n_seq, 1, shard_len) < lengths[None, :, None]
    live = jnp.broadcast_to(live[..., None], all_routes.shape).astype(BF)
    counts = dot(live.reshape(1, -1), seen.reshape(-1, experts), 1, 0)[0]
    fraction = counts / (top_count * valid_total)
    back_recv = back_recv.reshape(n_dev, -1)
    slot_gates_grad = back_recv[:, : pieces_dev * capacity].reshape(experts, split, capacity).sum(axis=1)
    probs_grad = (
        jnp.sum(own_hot * slot_gates_grad[None], axis=2)
        + (experts * fraction / valid_total)[None, :] * row_valid[:, None]
    )
    logits_grad = router_probs * (
        probs_grad - jnp.sum(router_probs * probs_grad, axis=-1, keepdims=True)
    )
    router_term = lax.dot_general(
        logits_grad, normed_two.astype(F32), (((0,), (0,)), ((), ())), precision=lax.Precision.HIGHEST
    )
    normed_two_grad = normed_two_grad + lax.dot_general(
        logits_grad, router.astype(F32), (((1,), (1,)), ((), ())), precision=lax.Precision.HIGHEST
    )

    def rms_back(values, scale, gain, grad):
        weighted = gain * grad
        mean = jnp.mean(weighted * values, axis=-1, keepdims=True)
        return scale * weighted - values * (scale * scale * scale) * mean, jnp.sum(
            grad * values * scale, axis=0
        )

    mid_part, gain_three = rms_back(resid_mid, mid_rms, gains[3], normed_two_grad)
    mid_grad = masked_low.astype(F32) + mid_part
    branch_grad = mid_grad.astype(BF)
    branch_later, outs_sums = lax.optimization_barrier((branch_grad, outs_sums))
    outs_parts = lax.all_to_all(outs_sums, "fsdp", split_axis=0, concat_axis=0, tiled=True)
    slot_branch, router_parts = gather_seq(
        branch_later, router_term, n_seq, n_fsdp, collective_id=9
    )
    slot_branch = slot_branch.reshape(slot_len, width)
    heads_grad = dot(slot_branch, proj_rows, 1, 1).astype(BF)
    query_in, key_in, value_grad, dots, heads_gain = attend_back(
        query,
        key,
        value,
        heads_grad,
        raw,
        totals,
        own_gains,
        cosine,
        sine,
        length,
        block,
        width,
    )
    raw_grad, router_parts = raw_back(
        query_in,
        key_in,
        value_grad,
        raw,
        totals,
        own_gains,
        dots,
        router_parts,
        n_seq,
        n_fsdp,
        width,
        collective_id=4,
    )
    raw_grad, outs_parts = lax.optimization_barrier((raw_grad, outs_parts))
    layer_out = (resid_mid + jnp.sum(outs_parts.astype(F32), axis=0)).astype(BF)[None]

    qkv_part = dot(normed_one, raw_grad, 0, 0).astype(BF)
    qkv_part = qkv_part.reshape(n_seq, n_fsdp, owned, 3 * head_width)
    prob_part = jnp.sum(router_probs * row_valid[:, None], axis=0)
    prob_row = jnp.tile(jnp.pad(prob_part, (0, head_width - experts)), n_seq)
    terms = jnp.pad(jnp.stack([gain_three, prob_row]), ((1, 5), (0, 0)))
    heads_terms = jnp.pad(heads_gain[:2], ((3, 3), (0, 0)))
    input_grad, qkv_grad, last = last_reduce(
        raw_grad,
        qkv_local,
        qkv_part,
        tokens[0],
        mid_grad,
        gains,
        terms,
        heads_terms,
        n_seq,
        n_fsdp,
        collective_id=10,
    )
    input_grad = input_grad[None]

    proj_part = dot(attended, slot_branch, 0, 0).astype(BF)
    proj_grad = lax.psum_scatter(proj_part, "fsdp", scatter_dimension=0, tiled=True).astype(F32)

    router_grad = lax.dynamic_slice_in_dim(router_parts, me_f * owned, owned, 1).T
    prob_total = last[2, :experts]
    last = lax.dynamic_slice_in_dim(last, me_f * owned, owned, 1)
    gains_grad = jnp.stack([last[0], last[3], last[4], last[1]])
    loss_value = (experts * jnp.sum(fraction * prob_total / valid_total)).reshape(1)
    return (
        layer_out,
        input_grad,
        gains_grad,
        qkv_grad,
        proj_grad,
        router_grad,
        up_grad,
        down_grad,
        loss_value,
    )


def solution(mesh):
    rows = P(("seq", "fsdp"), None)
    return jax.shard_map(
        local,
        mesh=mesh,
        in_specs=(
            P("fsdp", "seq", None),
            P("fsdp", "seq", None),
            P(),
            P("fsdp", "seq", None),
            P(None, ("seq", "fsdp")),
            rows,
            rows,
            rows,
            P(("seq", "fsdp"), None, None),
            P(("seq", "fsdp"), None, None),
        ),
        out_specs=(
            P("fsdp", "seq", None),
            P("fsdp", "seq", None),
            P(None, ("seq", "fsdp")),
            rows,
            rows,
            rows,
            P(("seq", "fsdp"), None, None),
            P(("seq", "fsdp"), None, None),
            P(),
        ),
        check_vma=False,
    )
```

time: 1020 us -> 725 us (0.71)
  Pallas kernels: 119 us -> 559 us
  waiting for transfers between devices: 464 us -> 28.9 us
  matrix products: 149 us -> 25.6 us
  other arithmetic: 95.9 us -> 18.7 us
  local copies, waits for them, and re-layouts: 94.1 us -> 48.4 us
  starting transfers between devices: 57.1 us -> 14.7 us
  blocking collectives: 17.7 us -> 0 us
    pallas_call x8 -> x22, Pallas kernels: 119 us -> 559 us  [the longest x1 79.9 us: return_rows(): pl.pallas_call(functools.partial(return_kernel, n_seq, n_fsdp, pieces), o...]
    all_to_all x13 -> x3, waiting for transfers between devices: 279 us -> 28.8 us  [the longest x2 28.8 us: exchange(): return lax.all_to_all(rows, 'seq', split_axis=0, concat_axis=0, tiled=True)]
    all_gather x6 -> x2, waiting for transfers between devices: 164 us -> 0.02 us  [the longest x1 0.02 us: local(): plane_masked = lax.all_gather(masked_later, 'fsdp', axis=0)]
    dot_general x13 -> x5, matrix products: 85 us -> 18.9 us  [dot(): lax.dot_general(a, b, (((ca,), (cb,)), ((), ())), preferred_element_type=...]
    dot_general x12 -> x3, matrix products: 62.7 us -> 4.13 us  [the longest x2 2.91 us: combine(): jnp.einsum('ftsc,sfcd->ftd', hot, back, preferred_element_type=F32)]
    all_to_all x13 -> x3, starting transfers between devices: 56.1 us -> 14.6 us  [the longest x2 10 us: exchange(): return lax.all_to_all(rows, 'seq', split_axis=0, concat_axis=0, tiled=True)]
    gather x4 -> x0, local copies, waits for them, and re-layouts: 31.3 us -> none  [dispatch(): rows = plane_rows[index].reshape(n_seq, n_fsdp * capacity, width)]
    another operation x6 -> x2, other arithmetic: 29.2 us -> 0.61 us  [the longest x1 0.59 us: local(): gains_grad = jnp.stack([last[0], last[3], last[4], last[1]])]
  transfers between devices with their start and end apart: 22 -> 6, of which waited for: 19 -> 1; matrix products, arithmetic and copies ran while one was open for 27% -> 5% of each run, Pallas kernels for 10% -> 37%
where the time goes in v2:
time: 725 us; the launch traced here: 712 us
  Pallas kernels  559 us (77%)
  local copies, waits for them, and re-layouts  48.4 us (7%)
  waiting for transfers between devices  28.9 us (4%)
  matrix products  25.6 us (4%)
  other arithmetic  18.7 us (3%)
  between operations  17.3 us (2%)
  starting transfers between devices  14.7 us (2%)
    pallas_call x1, Pallas kernels, return_rows(): pl.pallas_call(functools.partial(return_kernel, n_seq, n_fsdp, pieces), o...  79.9 us
    pallas_call x1, Pallas kernels, dispatch_rows(): pl.pallas_call(functools.partial(dispatch_kernel, n_seq, n_fsdp, pieces),...  75.2 us
    pallas_call x1, Pallas kernels, first_gather(): pl.pallas_call(functools.partial(first_kernel, n_seq, n_fsdp), out_shape=...  75 us
    pallas_call x1, Pallas kernels, last_reduce(): pl.pallas_call(functools.partial(last_kernel, n_seq, n_fsdp), out_shape=[...  64 us
    pallas_call x6, Pallas kernels, weight_grad(): pl.pallas_call(weight_grad_kernel, out_shape=jax.ShapeDtypeStruct((pieces...  55.1 us
    pallas_call x2, Pallas kernels, expert_forward(): pl.pallas_call(expert_forward_kernel, out_shape=[jax.ShapeDtypeStruct((2,...  40.5 us
    pallas_call x1, Pallas kernels, gather_seq(): pl.pallas_call(functools.partial(gather_kernel, n_seq, n_fsdp), out_shape...  33.9 us
    unnamed x126, local copies, waits for them, and re-layouts  32 us
  transfers between devices with their start and end apart: 6, of which 1 were waited for; matrix products, arithmetic and copies ran while one was open for 5% of the time, Pallas kernels for 37%

profile of v2, /device:TPU:0, one launch (start us, length us, event | category | flops | bytes accessed | tf_op | source)
XLA Modules:
  0.0 712.5 jit_solution(16036855502158810802)
XLA Ops:
  10.3 75.0 %first_gather.1 = (bf16[32,48,128]{2,1,0:T(8,128)(2,1)}, bf16[8,128,2048]{2,1,0:T(8,128)(2,1)}, bf16[8,4,64,768]{3,2,1,0:T(8,128)(2,1)}) custom-call(bf16[48,128]{1,0:T(8,128)(2,1)} %fusion.33.small, bf16[128,2048]{1,0:T(8,128)(2,1)} %bitcast.121, bf16[64,6144]{1,0:T(8,128)(2,1)} %qkv.1), custom_call_target="tpu_custom_call" | custom-call | tf_op jit(solution)/shard_map/first_gather/pallas_call | solution.py:475
  88.0 1.9 copy-done.6
  89.9 17.0 %front.1 = (bf16[1024,2048]{1,0:T(8,128)(2,1)S(1)}, f32[1024,768]{1,0:T(8,128)S(1)}, f32[8,1024]{1,0:T(8,128)S(1)}) custom-call(bf16[1024,2048]{1,0:T(8,128)(2,1)} %bitcast.132, f32[4,2048]{1,0:T(4,128)S(1)} %convert_element_type.130.gain.gains, bf16[2048,768]{1,0:T(8,128)(2,1)S(1)} %bitcast.120), custom_call_target="tpu_custom_call" | custom-call | tf_op jit(solution)/shard_map/front/pallas_call | solution.py:1528
  106.9 1.7 copy-done
  109.2 2.1 copy-done.30
  117.7 1.9 fusion.11
  119.6 1.3 pad_maximum_fusion
  120.9 11.0 %attend.1 = (bf16[1024,256]{1,0:T(8,128)(2,1)}, bf16[1024,256]{1,0:T(8,128)(2,1)}, bf16[1024,256]{1,0:T(8,128)(2,1)}, bf16[1024,256]{1,0:T(8,128)(2,1)}) custom-call(s32[1]{0:T(128)} %dynamic_slice.16.length, f32[1024,768]{1,0:T(8,128)} %copy-done, f32[1024,768]{1,0:T(8,128)} %copy-done, f32[1024,768]{1,0:T(8,128)} %copy-done, f32[8,1024]{1,0:T(8,128)} %copy-done.25, ...), custom_call_target="tpu_custom_call" | custom-call | flops 1073741824 | bytes 8388608 | tf_op jit(solution)/shard_map/attend/pallas_call | solution.py:1602
  134.5 30.2 %product_reduced.1 = f32[128,2048]{1,0:T(8,128)S(1)} custom-call(bf16[8,128,256]{2,1,0:T(8,128)(2,1)S(1)} %bitcast.128, bf16[256,2048]{1,0:T(8,128)(2,1)S(1)} %copy-done.18), custom_call_target="tpu_custom_call" | custom-call | tf_op jit(solution)/shard_map/product_reduced/pallas_call | solution.py:773
  168.7 1.6 copy-done.14
  170.3 75.2 %dispatch_rows.1 = (f32[32,8,128]{2,1,0:T(8,128)S(1)}, bf16[8,2,4,24,2048]{4,3,2,1,0:T(8,128)(2,1)}, bf16[8,4,24,2048]{3,2,1,0:T(8,128)(2,1)S(1)}, bf16[8,4,24,2048]{3,2,1,0:T(8,128)(2,1)S(1)}) custom-call(bf16[128,2048]{1,0:T(8,128)(2,1)S(1)} %multiply_convert_fusion.x, bf16[4,384,128]{2,1,0:T(8,128)(2,1)S(1)} %copy.82.hot, f32[32,8,128]{2,1,0:T(8,128)S(1)} %bitcast.129, ...), custom_call_target="tpu_custom_call" | custom-call | tf_op jit(solution)/shard_map/dispatch_rows/pallas_call | solution.py:1118
  245.5 1.6 copy-done.2
  247.1 1.7 copy-done.3
  248.8 4.7 all-to-all-start
  256.0 20.2 %expert_forward.2 = (f32[2,768,1024]{2,1,0:T(8,128)}, bf16[768,1024]{1,0:T(8,128)(2,1)}, bf16[768,2048]{1,0:T(8,128)(2,1)}, bf16[8,2,4,24,2048]{4,3,2,1,0:T(8,128)(2,1)}) custom-call(bf16[768,2048]{1,0:T(8,128)(2,1)} %bitcast.116, f32[768,1]{1,0:T(8,128)} %copy.85.gates, bf16[2,2048,2048]{2,1,0:T(8,128)(2,1)} %w_up.7, bf16[2,2048,2048]{2,1,0:T(8,128)(2,1)} %w_up.7, ...), custom_call_target="tpu_custom_call" | custom-call | flops 9663676416 | bytes 12582912 | tf_op jit(solution)/shard_map/expert_forward/pallas_call | solution.py:1336
  276.2 20.3 %expert_forward.3 = (f32[2,768,1024]{2,1,0:T(8,128)}, bf16[768,1024]{1,0:T(8,128)(2,1)}, bf16[768,2048]{1,0:T(8,128)(2,1)}, bf16[8,2,4,24,2048]{4,3,2,1,0:T(8,128)(2,1)}) custom-call(bf16[768,2048]{1,0:T(8,128)(2,1)} %bitcast.113, f32[768,1]{1,0:T(8,128)} %copy.87.gates, bf16[2,2048,2048]{2,1,0:T(8,128)(2,1)} %w_up.7, ...), custom_call_target="tpu_custom_call", output_to_operand_aliasing={{3}: (5, {})} | custom-call | flops 9663676416 | bytes 12582912 | tf_op jit(solution)/shard_map/expert_forward/pallas_call | solution.py:1336
  296.5 28.8 %all-to-all-done.masked = bf16[8,2,4,24,2048]{4,3,2,1,0:T(8,128)(2,1)} async-done(((bf16[8,2,4,24,2048]{4,3,2,1,0:T(8,128)(2,1)}), bf16[8,2,4,24,2048]{4,3,2,1,0:T(8,128)(2,1)}, u32[]{:S(2)}, u32[]{:S(2)}) %all-to-all-start) | async-done | bytes 6291488 | tf_op jit(solution)/shard_map/all_to_all | solution.py:1900
  325.3 5.3 all-to-all-start.1
  333.8 1.9 multiply_divide_fusion
  336.0 12.3 %expert_backward.3 = (bf16[2,768,1024]{2,1,0:T(8,128)(2,1)S(1)}, bf16[768,2048]{1,0:T(8,128)(2,1)}, f32[8,768]{1,0:T(8,128)S(1)}) custom-call(bf16[8,2,4,24,2048]{4,3,2,1,0:T(8,128)(2,1)} %all-to-all-done.masked, f32[768,1]{1,0:T(8,128)S(1)} %copy.89.gates, bf16[768,2048]{1,0:T(8,128)(2,1)} %get-tuple-element.102.piece_out, ...), custom_call_target="tpu_custom_call" | custom-call | flops 3221225472 | bytes 9437184 | tf_op jit(solution)/shard_map/expert_backward/pallas_call | solution.py:1401
  348.3 1.7 copy-done.4
  350.3 12.3 %expert_backward.2 = (bf16[2,768,1024]{2,1,0:T(8,128)(2,1)S(1)}, bf16[768,2048]{1,0:T(8,128)(2,1)}, f32[8,768]{1,0:T(8,128)S(1)}) custom-call(bf16[8,2,4,24,2048]{4,3,2,1,0:T(8,128)(2,1)} %all-to-all-done.masked, f32[768,1]{1,0:T(8,128)S(1)} %copy.88.gates, bf16[768,2048]{1,0:T(8,128)(2,1)} %get-tuple-element.98.piece_out, ...), custom_call_target="tpu_custom_call" | custom-call | flops 3221225472 | bytes 9437184 | tf_op jit(solution)/shard_map/expert_backward/pallas_call | solution.py:1401
  362.6 1.6 copy-done.5
  364.6 9.8 %weight_grad.6.refs_0_ = f32[2,2048,2048]{2,1,0:T(8,128)} custom-call(bf16[768,2048]{1,0:T(8,128)(2,1)} %bitcast.117, bf16[2,768,1024]{2,1,0:T(8,128)(2,1)} %copy-done.5), custom_call_target="tpu_custom_call" | custom-call | flops 3221225472 | bytes 13107200 | tf_op jit(solution)/shard_map/weight_grad/pallas_call | solution.py:1273
  374.4 9.8 %weight_grad.7.refs_0_ = f32[2,2048,2048]{2,1,0:T(8,128)} custom-call(bf16[768,2048]{1,0:T(8,128)(2,1)} %bitcast.118, bf16[2,768,1024]{2,1,0:T(8,128)(2,1)} %copy-done.5, f32[2,2048,2048]{2,1,0:T(8,128)} %weight_grad.6.refs_0_), custom_call_target="tpu_custom_call", output_to_operand_aliasing={{}: (2, {})} | custom-call | flops 3221225472 | bytes 13107200 | tf_op jit(solution)/shard_map/weight_grad/pallas_call | solution.py:1273
  384.2 9.8 %weight_grad.8.refs_0_ = f32[2,2048,2048]{2,1,0:T(8,128)} custom-call(bf16[768,2048]{1,0:T(8,128)(2,1)} %bitcast.114, bf16[2,768,1024]{2,1,0:T(8,128)(2,1)} %copy-done.4, f32[2,2048,2048]{2,1,0:T(8,128)} %weight_grad.7.refs_0_), custom_call_target="tpu_custom_call", output_to_operand_aliasing={{}: (2, {})} | custom-call | flops 3221225472 | bytes 13107200 | tf_op jit(solution)/shard_map/weight_grad/pallas_call | solution.py:1273
  394.0 9.8 %weight_grad.9 = f32[2,2048,2048]{2,1,0:T(8,128)} custom-call(bf16[768,2048]{1,0:T(8,128)(2,1)} %bitcast.115, bf16[2,768,1024]{2,1,0:T(8,128)(2,1)} %copy-done.4, f32[2,2048,2048]{2,1,0:T(8,128)} %weight_grad.8.refs_0_), custom_call_target="tpu_custom_call", output_to_operand_aliasing={{}: (2, {})} | custom-call | flops 3221225472 | bytes 13107200 | tf_op jit(solution)/shard_map/weight_grad/pallas_call | solution.py:1273
  403.7 8.0 %weight_grad.10.refs_0_ = f32[2,1024,2048]{2,1,0:T(8,128)} custom-call(bf16[768,1024]{1,0:T(8,128)(2,1)} %get-tuple-element.112.a, bf16[1,768,2048]{2,1,0:T(8,128)(2,1)} %bitcast.136), custom_call_target="tpu_custom_call" | custom-call | flops 3221225472 | bytes 13107200 | tf_op jit(solution)/shard_map/weight_grad/pallas_call | solution.py:1273
  411.7 8.0 %weight_grad.11 = f32[2,1024,2048]{2,1,0:T(8,128)} custom-call(bf16[768,1024]{1,0:T(8,128)(2,1)} %get-tuple-element.110.a, bf16[1,768,2048]{2,1,0:T(8,128)(2,1)} %bitcast.133, f32[2,1024,2048]{2,1,0:T(8,128)} %weight_grad.10.refs_0_), custom_call_target="tpu_custom_call", output_to_operand_aliasing={{}: (2, {})} | custom-call | flops 3221225472 | bytes 13107200 | tf_op jit(solution)/shard_map/weight_grad/pallas_call | solution.py:1273
  419.7 12.4 %expert_input.2 = bf16[768,2048]{1,0:T(8,128)(2,1)} custom-call(bf16[2,768,1024]{2,1,0:T(8,128)(2,1)} %copy-done.5, bf16[2,2048,2048]{2,1,0:T(8,128)(2,1)} %w_up.7), custom_call_target="tpu_custom_call" | custom-call | flops 6442450944 | bytes 8388608 | tf_op jit(solution)/shard_map/expert_input/pallas_call | solution.py:1440
  432.2 12.5 %expert_input.3 = bf16[768,2048]{1,0:T(8,128)(2,1)} custom-call(bf16[2,768,1024]{2,1,0:T(8,128)(2,1)} %copy-done.4, bf16[2,2048,2048]{2,1,0:T(8,128)(2,1)} %w_up.7), custom_call_target="tpu_custom_call" | custom-call | flops 6442450944 | bytes 8388608 | tf_op jit(solution)/shard_map/expert_input/pallas_call | solution.py:1440
  444.7 1.9 copy-done.12
  446.5 1.9 copy-done.13
  448.4 79.9 %return_rows.1 = (f32[128,2048]{1,0:T(8,128)S(1)}, f32[32,8,128]{2,1,0:T(8,128)S(1)}) custom-call(bf16[4,128,384]{2,1,0:T(8,128)(2,1)S(1)} %copy-done.11, f32[32,8,128]{2,1,0:T(8,128)S(1)} %copy.100.gates, bf16[8,4,24,2048]{3,2,1,0:T(8,128)(2,1)S(1)} %bitcast.124, bf16[8,4,24,2048]{3,2,1,0:T(8,128)(2,1)S(1)} %bitcast.125), custom_call_target="tpu_custom_call" | custom-call | tf_op jit(solution)/shard_map/return_rows/pallas_call | solution.py:1238
  530.5 2.0 multiply_reduce_fusion
  532.6 3.4 slice_bitcast_fusion
  536.8 2.2 fusion.1
  539.0 1.5 fusion.41
  540.5 4.6 all-to-all-start.2
  546.4 33.9 %gather_seq.1 = (bf16[8,128,2048]{2,1,0:T(8,128)(2,1)}, f32[64,256]{1,0:T(8,128)}) custom-call(bf16[128,2048]{1,0:T(8,128)(2,1)} %get-tuple-element.120.x, f32[64,2048]{1,0:T(8,128)} %fusion.36.terms), custom_call_target="tpu_custom_call" | custom-call | bytes 67108864 | tf_op jit(solution)/shard_map/gather_seq/pallas_call | solution.py:623
  580.3 4.5 convolution_convert_fusion.1
  584.9 4.3 convolution_convert_fusion.2.g_ref
  589.2 17.3 %attend_back.1 = (f32[1024,256]{1,0:T(8,128)}, f32[1024,256]{1,0:T(8,128)}, bf16[1024,256]{1,0:T(8,128)(2,1)}, f32[8,1024]{1,0:T(8,128)}, f32[8,256]{1,0:T(8,128)}) custom-call(s32[1]{0:T(128)} %dynamic_slice.16.length, bf16[1024,256]{1,0:T(8,128)(2,1)} %get-tuple-element.81.q_ref, bf16[1024,256]{1,0:T(8,128)(2,1)} %get-tuple-element.82.k_ref, ...), custom_call_target="tpu_custom_call" | custom-call | flops 5368709120 | bytes 16777216 | tf_op jit(solution)/shard_map/attend_back/pallas_call | solution.py:1705
  611.5 10.3 %raw_back.1 = (bf16[1024,768]{1,0:T(8,128)(2,1)S(1)}, f32[64,256]{1,0:T(8,128)S(1)}) custom-call(f32[1024,256]{1,0:T(8,128)S(1)} %copy-done.16, f32[1024,256]{1,0:T(8,128)S(1)} %copy-done.17, bf16[1024,256]{1,0:T(8,128)(2,1)S(1)} %copy-done.22, f32[1024,768]{1,0:T(8,128)S(1)} %copy-done.1, f32[8,1024]{1,0:T(8,128)S(1)} %copy-done.26, ...), custom_call_target="tpu_custom_call" | custom-call | tf_op jit(solution)/shard_map/raw_back/pallas_call | solution.py:1795
  623.7 1.8 convert_element_type.153
  625.5 8.0 %convolution_convert_fusion = bf16[2048,768]{1,0:T(8,128)(2,1)} fusion(bf16[1024,2048]{1,0:T(8,128)(2,1)} %copy-done.30, bf16[1024,768]{1,0:T(8,128)(2,1)} %copy-done.15), kind=kOutput, calls=%fused_computation.6 | convolution fusion | flops 3222798336 | bytes 8912896 | tf_op jit(solution)/shard_map/dot_general | solution.py:21
  633.5 64.0 %last_reduce.1 = (bf16[128,2048]{1,0:T(8,128)(2,1)S(1)}, f32[64,6144]{1,0:T(8,128)S(1)}, f32[8,256]{1,0:T(8,128)S(1)}) custom-call(bf16[8,128,768]{2,1,0:T(8,128)(2,1)} %bitcast.127, bf16[2048,768]{1,0:T(8,128)(2,1)} %bitcast.119, bf16[8,4,64,768]{3,2,1,0:T(8,128)(2,1)} %bitcast.135, bf16[128,2048]{1,0:T(8,128)(2,1)S(1)} %bitcast.122, ...), custom_call_target="tpu_custom_call" | custom-call | bytes 134217728 | tf_op jit(solution)/shard_map/last_reduce/pallas_call | solution.py:954
  697.7 2.2 convert_reduce_fusion
  (220 shorter events, 40.4 us)
Async XLA Ops:
  7.2 125.0 %all-gather.4.cloned.1.call-start = ((), (), s32[]{:S(2)}) async-start(), calls=%async_computation.4 | async-start | bytes 1310720 | tf_op jit(solution)/shard_map/all_gather | solution.py:1890
  85.3 83.3 %all-gather.6.cloned.1.call-start = ((), (), s32[]{:S(2)}) async-start(), calls=%async_computation.6 | async-start | bytes 2621440 | tf_op jit(solution)/shard_map/all_gather | solution.py:1904
  86.7 30.3 %copy-start.23 = (f32[4,2048]{1,0:T(4,128)}, f32[4,2048]{1,0:T(4,128)S(1)}, u32[]{:S(2)}) copy-start(f32[4,2048]{1,0:T(4,128)S(1)} %convert_element_type.130.gain.gains) | copy-start | bytes 98308
  88.0 1.9 copy-start.6
  89.9 22.6 %copy-start.35 = (bf16[1,128,2048]{2,1,0:T(8,128)(2,1)S(1)}, bf16[1,128,2048]{2,1,0:T(8,128)(2,1)}, u32[]{:S(2)}) copy-start(bf16[1,128,2048]{2,1,0:T(8,128)(2,1)} %param.11) | copy-start | bytes 1572868
  106.9 1.7 copy-start
  109.2 2.1 copy-start.30
  116.0 4.8 copy-start.10
  116.2 49.3 %copy-start.41 = (f32[2048]{0:T(1024)}, f32[2048]{0:T(1024)S(1)}, u32[]{:S(2)}) copy-start(f32[2048]{0:T(1024)S(1)} %mul.229) | copy-start | bytes 24580
  117.0 49.1 %copy-start.34 = (bf16[2048,64]{1,0:T(8,128)(2,1)}, bf16[2048,64]{1,0:T(8,128)(2,1)S(1)}, u32[]{:S(2)}) copy-start(bf16[2048,64]{1,0:T(8,128)(2,1)S(1)} %reshape.243) | copy-start | bytes 786436
  120.9 11.0 %copy-start.44 = (s32[1,128,8]{1,2,0:T(8,128)S(1)}, s32[1,128,8]{1,2,0:T(8,128)}, u32[]{:S(2)}) copy-start(s32[1,128,8]{1,2,0:T(8,128)} %param.13) | copy-start | bytes 12292
  120.9 43.8 %copy-start.7 = (bf16[1,128,2048]{2,1,0:T(8,128)(2,1)S(1)}, bf16[1,128,2048]{2,1,0:T(8,128)(2,1)}, u32[]{:S(2)}) copy-start(bf16[1,128,2048]{2,1,0:T(8,128)(2,1)} %param.10) | copy-start | bytes 1572868
  131.9 35.7 %copy-start.40 = (f32[128,64]{0,1:T(8,128)}, f32[128,64]{0,1:T(8,128)S(1)}, u32[]{:S(2)}) copy-start(f32[128,64]{0,1:T(8,128)S(1)} %convert_reduce_fusion.1) | copy-start | bytes 98308
  132.2 35.5 %copy-start.43 = (f32[128,64]{0,1:T(8,128)}, f32[128,64]{0,1:T(8,128)S(1)}, u32[]{:S(2)}) copy-start(f32[128,64]{0,1:T(8,128)S(1)} %fusion.14) | copy-start | bytes 98308
  245.5 1.6 copy-start.2
  247.1 1.7 copy-start.3
  248.8 76.6 %all-to-all-start = ((bf16[8,2,4,24,2048]{4,3,2,1,0:T(8,128)(2,1)}), bf16[8,2,4,24,2048]{4,3,2,1,0:T(8,128)(2,1)}, u32[]{:S(2)}, u32[]{:S(2)}) async-start(bf16[8,2,4,24,2048]{4,3,2,1,0:T(8,128)(2,1)} %get-tuple-element.85), calls=%async_computation | async-start | bytes 12582912 | tf_op jit(solution)/shard_map/all_to_all | solution.py:1900
  325.3 5.3 copy-start.55
  325.3 119.3 %all-to-all-start.1 = ((bf16[8,2,4,24,2048]{4,3,2,1,0:T(8,128)(2,1)}), bf16[8,2,4,24,2048]{4,3,2,1,0:T(8,128)(2,1)}, u32[]{:S(2)}, u32[]{:S(2)}) async-start(bf16[8,2,4,24,2048]{4,3,2,1,0:T(8,128)(2,1)} %get-tuple-element.107), calls=%async_computation.1 | async-start | bytes 12582912 | tf_op jit(solution)/shard_map/all_to_all | solution.py:1900
  348.3 1.7 copy-start.4
  362.6 1.6 copy-start.5
  432.2 12.5 %copy-start.11 = (bf16[4,128,384]{2,1,0:T(8,128)(2,1)S(1)}, bf16[4,128,384]{2,1,0:T(8,128)(2,1)}, u32[]{:S(2)}) copy-start(bf16[4,128,384]{2,1,0:T(8,128)(2,1)} %copy-done.10) | copy-start | bytes 1179652
  444.7 1.9 copy-start.12
  446.5 1.9 copy-start.13
  448.4 81.1 %copy-start.46 = (f32[128]{0:T(128)S(1)}, f32[128]{0:T(128)}, u32[]{:S(2)}) copy-start(f32[128]{0:T(128)} %copy-done.45) | copy-start | bytes 1540
  448.4 81.1 %copy-start.47 = (f32[128]{0:T(128)S(1)}, f32[128]{0:T(128)}, u32[]{:S(2)}) copy-start(f32[128]{0:T(128)} %get-tuple-element.184) | copy-start | bytes 1540
  448.4 82.1 %copy-start.32 = (f32[128,2048]{1,0:T(8,128)S(1)}, f32[128,2048]{1,0:T(8,128)}, u32[]{:S(2)}) copy-start(f32[128,2048]{1,0:T(8,128)} %copy-done.31) | copy-start | bytes 3145732
  448.4 82.1 %copy-start.42 = (f32[2048]{0:T(1024)S(1)}, f32[2048]{0:T(1024)}, u32[]{:S(2)}) copy-start(f32[2048]{0:T(1024)} %copy-done.41) | copy-start | bytes 24580
  536.8 2.2 copy-start.36
  536.8 2.2 copy-start.52
  536.8 2.2 copy-start.54
  536.8 2.2 copy-start.57
  540.5 4.7 copy-start.38
  540.5 4.7 copy-start.48
  540.5 4.7 copy-start.50
  540.5 39.8 %copy-start.21 = (bf16[1024,256]{1,0:T(8,128)(2,1)S(1)}, bf16[1024,256]{1,0:T(8,128)(2,1)}, u32[]{:S(2)}) copy-start(bf16[1024,256]{1,0:T(8,128)(2,1)} %get-tuple-element.79) | copy-start | bytes 1572868
  540.5 85.0 %all-to-all-start.2 = ((bf16[4,128,2048]{2,1,0:T(8,128)(2,1)}), bf16[4,128,2048]{2,1,0:T(8,128)(2,1)}, u32[]{:S(2)}, u32[]{:S(2)}) async-start(bf16[4,128,2048]{2,1,0:T(8,128)(2,1)} %fusion.1), calls=%async_computation.2 | async-start | bytes 4194304 | tf_op jit(solution)/shard_map/all_to_all | solution.py:2016
  545.1 78.6 %reduce-scatter.2.cloned.1.call-start = ((), (), s32[]{:S(2)}) async-start(), calls=%async_computation.5 | async-start | bytes 1310720 | tf_op jit(solution)/shard_map/reduce_scatter | solution.py:2075
  580.3 4.6 copy-start.19
  589.2 18.0 %copy-start.1 = (f32[1024,768]{1,0:T(8,128)S(1)}, f32[1024,768]{1,0:T(8,128)}, u32[]{:S(2)}) copy-start(f32[1024,768]{1,0:T(8,128)} %copy-done) | copy-start | bytes 9437188
  589.2 18.0 %copy-start.26 = (f32[8,1024]{1,0:T(8,128)S(1)}, f32[8,1024]{1,0:T(8,128)}, u32[]{:S(2)}) copy-start(f32[8,1024]{1,0:T(8,128)} %copy-done.25) | copy-start | bytes 98308
  589.2 18.0 %copy-start.27 = (f32[64,256]{1,0:T(8,128)S(1)}, f32[64,256]{1,0:T(8,128)}, u32[]{:S(2)}) copy-start(f32[64,256]{1,0:T(8,128)} %get-tuple-element.126.terms) | copy-start | bytes 196612
  589.2 18.0 %copy-start.28 = (f32[4,256]{1,0:T(4,128)S(1)}, f32[4,256]{1,0:T(4,128)}, u32[]{:S(2)}) copy-start(f32[4,256]{1,0:T(4,128)} %constant_dynamic-slice_fusion.2.gain) | copy-start | bytes 12292
  625.5 8.0 %copy-start.8 = (bf16[1,128,2048]{2,1,0:T(8,128)(2,1)S(1)}, bf16[1,128,2048]{2,1,0:T(8,128)(2,1)}, u32[]{:S(2)}) copy-start(bf16[1,128,2048]{2,1,0:T(8,128)(2,1)} %param.10) | copy-start | bytes 1572868
  625.5 8.0 %copy-start.9 = (f32[128,2048]{1,0:T(8,128)S(1)}, f32[128,2048]{1,0:T(8,128)}, u32[]{:S(2)}) copy-start(f32[128,2048]{1,0:T(8,128)} %get-tuple-element.180.mid) | copy-start | bytes 3145732
  625.5 8.0 %copy-start.24 = (f32[4,2048]{1,0:T(4,128)S(1)}, f32[4,2048]{1,0:T(4,128)}, u32[]{:S(2)}) copy-start(f32[4,2048]{1,0:T(4,128)} %copy-done.23) | copy-start | bytes 98308
  697.6 2.3 copy-start.33
  697.6 3.2 copy-start.56
  (16 other events, 15.3 us)
Sparse Core Ops, SparseCore 0:
  85.5 27.9 all-gather.3
  115.6 45.4 all-gather.5
  585.0 27.6 reduce-scatter.1

commit v3 on v2

--- a/solution.py
+++ b/solution.py
@@ -277,15 +277,39 @@
     return bits[1:] + bits[:1], bits[:0:-1] + bits[:1]
 
 
+def block_places(routes, ids, capacity):
+    count = routes.shape[1]
+    match = jnp.zeros((ids.shape[0], count), F32)
+    for k in range(routes.shape[0]):
+        match = match + (routes[k : k + 1, :] == ids).astype(F32)
+    row = lax.broadcasted_iota(jnp.int32, (count, count), 0)
+    column = lax.broadcasted_iota(jnp.int32, (count, count), 1)
+    rank = dot(match.astype(BF), (row < column).astype(BF), 1, 0)
+    place = lax.broadcasted_iota(jnp.int32, (ids.shape[0], capacity, count), 1).astype(F32)
+    hot = match[:, None, :] * (rank[:, None, :] == place).astype(F32)
+    return hot.reshape(ids.shape[0] * capacity, count)
+
+
 def first_kernel(
     n_seq,
     n_fsdp,
+    pieces,
+    split,
+    capacity,
+    owned,
+    top,
     small,
     tokens,
     qkv,
+    masked,
     small_all,
+    gains,
     slot,
     qkv_all,
+    masked_all,
+    to_places,
+    to_rows,
+    send,
     own_sem,
     small_send,
     small_recv,
@@ -295,6 +319,9 @@
     line_recv,
     token_send,
     token_recv,
+    row_send,
+    row_recv,
+    row_own,
 ):
     me_s, me_f = lax.axis_index("seq"), lax.axis_index("fsdp")
     n = n_seq * n_fsdp
@@ -323,6 +350,31 @@
         copy.start()
     greet_all(n_seq, n_fsdp)
 
+    def small_copy(i):
+        other = (me + i) % n
+        return remote(
+            small,
+            small_all.at[me],
+            small_send.at[i],
+            small_recv.at[me],
+            (other // n_fsdp, other % n_fsdp),
+        )
+
+    def small_arrived(other):
+        return remote(
+            small,
+            small_all.at[other],
+            small_send.at[0],
+            small_recv.at[other],
+            (other // n_fsdp, other % n_fsdp),
+        )
+
+    def small_start(i, carry):
+        small_copy(i).start()
+        return carry
+
+    lax.fori_loop(1, n, small_start, 0)
+
     def column_copy(i, part):
         other = (me_s + i) % n_seq
         return remote(
@@ -336,42 +388,6 @@
     for i in range(1, n_seq):
         for part in range(3):
             column_copy(i, part).start()
-    for copy in own:
-        copy.wait()
-
-    def line_copy(part, step, block, way, to):
-        place = qkv_all.at[part, block]
-        return remote(
-            place, place, line_send.at[part, way, step], line_recv.at[part, block], (me_s, to)
-        )
-
-    def line_first(part):
-        @pl.when(me_f + 1 < n_fsdp)
-        def _():
-            line_copy(part, 0, me_f, 0, me_f + 1).start()
-
-        @pl.when(me_f >= 1)
-        def _():
-            line_copy(part, 0, me_f, 1, me_f - 1).start()
-
-    def column_arrived(i, carry):
-        source = (me_s + i) % n_seq
-
-        @pl.when(i > 0)
-        def _():
-            for part in range(3):
-                remote(
-                    columns(source, part),
-                    column_place(source, part),
-                    qkv_send.at[i, part],
-                    qkv_recv.at[source, part],
-                    (source, me_f),
-                ).wait_recv()
-
-        line_first(source)
-        return carry
-
-    lax.fori_loop(0, n_seq, column_arrived, 0)
 
     flows = []
     for side in range(2):
@@ -393,26 +409,75 @@
             if stage < stages:
                 flow.start(stage)
 
-    def small_copy(i):
-        other = (me + i) % n
+    point(0)
+    for copy in own:
+        copy.wait()
+
+    piece = lax.broadcasted_iota(jnp.int32, (n_seq * pieces, 1), 0)
+    piece = ((piece // pieces) * n_fsdp + me_f) * pieces + piece % pieces
+    ids = piece // split
+
+    def row_copy(i, place):
+        other = (me_s + i) % n_seq
         return remote(
-            small,
-            small_all.at[me],
-            small_send.at[i],
-            small_recv.at[me],
-            (other // n_fsdp, other % n_fsdp),
-        )
-
-    def small_start(i, carry):
-        small_copy(i).start()
+            send.at[other], masked_all.at[place, :, me_f], row_send.at[i], row_recv.at[place], (other, me_f)
+        )
+
+    def own_row():
+        return pltpu.make_async_copy(send.at[me_s], masked_all.at[me_s, :, me_f], row_own)
+
+    def table(block):
+        routes = small_all[me_s * n_fsdp + block, 8 : 8 + top, :].astype(F32).astype(jnp.int32)
+        hot = block_places(routes, ids, capacity)
+        to_places[block] = hot.astype(BF)
+        to_rows[block] = hot.T.astype(BF)
+
+    def scatter():
+        def some(lanes):
+            picked = dot(to_places[me_f], masked[:, lanes], 1, 0).astype(BF)
+            send[:, :, :, lanes] = picked.reshape(n_seq, pieces, capacity, -1)
+
+        chunked(width, 512, some)
+        for i in range(1, n_seq):
+            row_copy(i, me_s).start()
+        own_row().start()
+
+    def line_copy(part, step, block, way, to):
+        place = qkv_all.at[part, block]
+        return remote(
+            place, place, line_send.at[part, way, step], line_recv.at[part, block], (me_s, to)
+        )
+
+    def line_first(part):
+        @pl.when(me_f + 1 < n_fsdp)
+        def _():
+            line_copy(part, 0, me_f, 0, me_f + 1).start()
+
+        @pl.when(me_f >= 1)
+        def _():
+            line_copy(part, 0, me_f, 1, me_f - 1).start()
+
+    def column_arrived(i, carry):
+        source = (me_s + i) % n_seq
+
+        @pl.when(i > 0)
+        def _():
+            for part in range(3):
+                remote(
+                    columns(source, part),
+                    column_place(source, part),
+                    qkv_send.at[i, part],
+                    qkv_recv.at[source, part],
+                    (source, me_f),
+                ).wait_recv()
+
+        line_first(source)
         return carry
 
-    point(0)
-    lax.fori_loop(1, n, small_start, 0)
-    count = 1
-    for step in range(1, n_fsdp):
-
-        def column_next(i, carry, step=step):
+    lax.fori_loop(0, n_seq, column_arrived, 0)
+
+    def column_step(step):
+        def column_next(i, carry):
             part = (me_s + i) % n_seq
             line_step(
                 n_fsdp,
@@ -422,15 +487,42 @@
             )
             return carry
 
-        for part in range(2):
-            lax.fori_loop(part * n_seq // 2, (part + 1) * n_seq // 2, column_next, 0)
-            point(count)
-            count += 1
-    while count <= stages:
-        point(count)
-        count += 1
+        lax.fori_loop(0, n_seq, column_next, 0)
+
+    point(1)
+    table(me_f)
+    for stage in range(2, stages + 1):
+        point(stage)
+    scatter()
+    for step in range(1, n_fsdp):
+        column_step(step)
+    for i in range(1, n_fsdp):
+        block = (me_f + i) % n_fsdp
+        small_arrived(me_s * n_fsdp + block).wait_recv()
+        table(block)
     for flow in flows:
         flow.sent()
+
+    def small_wait(i, carry):
+        other = (me + i) % n
+        small_copy(i).wait_send()
+
+        @pl.when(other // n_fsdp != me_s)
+        def _():
+            small_arrived(other).wait_recv()
+
+        return carry
+
+    lax.fori_loop(1, n, small_wait, 0)
+
+    lane = lax.broadcasted_iota(jnp.int32, (8, 128), 1)
+    each = 128 // owned
+    for j in range(width // 128):
+        total = jnp.zeros((8, 128), F32)
+        for k in range(each):
+            some = jnp.where(lane < owned, small_all[j * each + k, :8, :].astype(F32), 0.0)
+            total = total + (pltpu.roll(some, k * owned, 1) if k else some)
+        gains[:, j * 128 : (j + 1) * 128] = total
 
     def column_sent(i, carry):
         for part in range(3):
@@ -438,20 +530,6 @@
         return carry
 
     lax.fori_loop(1, n_seq, column_sent, 0)
-
-    def small_wait(i, carry):
-        other = (me + i) % n
-        small_copy(i).wait_send()
-        remote(
-            small,
-            small_all.at[other],
-            small_send.at[i],
-            small_recv.at[other],
-            (other // n_fsdp, other % n_fsdp),
-        ).wait_recv()
-        return carry
-
-    lax.fori_loop(1, n, small_wait, 0)
 
     def line_done(part, carry):
         for step in range(n_fsdp):
@@ -463,25 +541,38 @@
         return carry
 
     lax.fori_loop(0, n_seq, line_done, 0)
-
-
-def first_gather(small, tokens, qkv, n_seq, n_fsdp, collective_id):
+    own_row().wait()
+    for i in range(1, n_seq):
+        row_copy(i, me_s).wait_send()
+        row_copy(i, (me_s + i) % n_seq).wait_recv()
+
+
+def first_gather(
+    small, tokens, qkv, masked, n_seq, n_fsdp, pieces, split, capacity, top, collective_id
+):
     owned = qkv.shape[0]
-    head_width = qkv.shape[1] // (3 * n_seq)
+    rows, width = tokens.shape
+    head_width = width // n_seq
     n = n_seq * n_fsdp
+    places_all = n_seq * pieces * capacity
     vmem = pl.BlockSpec(memory_space=pltpu.VMEM)
     any_space = pl.BlockSpec(memory_space=pl.ANY)
     dma = pltpu.SemaphoreType.DMA
     return pl.pallas_call(
-        functools.partial(first_kernel, n_seq, n_fsdp),
+        functools.partial(first_kernel, n_seq, n_fsdp, pieces, split, capacity, owned, top),
         out_shape=[
             jax.ShapeDtypeStruct((n,) + small.shape, BF),
+            jax.ShapeDtypeStruct((8, width), F32),
             jax.ShapeDtypeStruct((n_seq,) + tokens.shape, BF),
             jax.ShapeDtypeStruct((n_seq, n_fsdp, owned, 3 * head_width), BF),
+            jax.ShapeDtypeStruct((n_seq, pieces, n_fsdp, capacity, width), BF),
+            jax.ShapeDtypeStruct((n_fsdp, places_all, rows), BF),
+            jax.ShapeDtypeStruct((n_fsdp, rows, places_all), BF),
         ],
-        in_specs=[vmem] * 3,
-        out_specs=[vmem, any_space, any_space],
+        in_specs=[vmem] * 4,
+        out_specs=[vmem, vmem, any_space, any_space, any_space, vmem, vmem],
         scratch_shapes=[
+            pltpu.VMEM((n_seq, pieces, capacity, width), BF),
             dma((5,)),
             dma((n,)),
             dma((n,)),
@@ -491,10 +582,15 @@
             dma((n_seq, n_fsdp)),
             dma((2, n_seq - 1)),
             dma((2, n_seq)),
+            dma((n_seq,)),
+            dma((n_seq,)),
+            dma,
         ],
-        compiler_params=pltpu.CompilerParams(collective_id=collective_id, has_side_effects=True),
+        compiler_params=pltpu.CompilerParams(
+            collective_id=collective_id, has_side_effects=True, vmem_limit_bytes=40 << 20
+        ),
         name="first_gather",
-    )(small, tokens, qkv)
+    )(small, tokens, qkv, masked)
 
 
 def greet_seq(n_seq):
@@ -992,20 +1088,13 @@
     lax.fori_loop(0, total // size, step, 0)
 
 
-def dispatch_kernel(n_seq, n_fsdp, pieces, x, hot, gates, masked, gates_out, masked_out, *refs):
-    outs = refs[:pieces]
-    (
-        gathered,
-        send,
-        own_sem,
-        line_send,
-        line_recv,
-        row_send,
-        row_recv,
-        masked_rows,
-        masked_sem,
-    ) = refs[pieces : pieces + 9]
-    gate_exchange = Exchange(n_seq, n_fsdp, gates, gates_out, refs[pieces + 9 :])
+def dispatch_kernel(n_seq, n_fsdp, pieces, x, hot, gates, masked, before, w_up, w_down, *refs):
+    masked_all, columns_out, scaled = refs[:3]
+    outs, hiddens, acts, results = (refs[3 + k * pieces : 3 + (k + 1) * pieces] for k in range(4))
+    rest = refs[3 + 4 * pieces :]
+    gates_out, gathered, send, total = rest[:4]
+    own_sem, line_send, line_recv, row_send, row_recv, own_two, send_two, recv_two = rest[4:12]
+    gate_exchange = Exchange(n_seq, n_fsdp, gates, gates_out, rest[12:])
     me_s, me_f = lax.axis_index("seq"), lax.axis_index("fsdp")
     width = x.shape[1]
     capacity = outs[0].shape[2]
@@ -1017,13 +1106,13 @@
             src, gathered.at[block], line_send.at[way, step], line_recv.at[block], (me_s, to)
         )
 
-    def row_copy(block, i, piece):
+    def row_copy(block, i, piece, place):
         other = (me_s + i) % n_seq
         return remote(
             send.at[block, other, piece],
-            outs[piece].at[me_s, block],
+            outs[piece].at[place, block],
             row_send.at[block, i, piece],
-            row_recv.at[me_s, block, piece],
+            row_recv.at[place, block, piece],
             (other, me_f),
         )
 
@@ -1032,33 +1121,54 @@
             send.at[block, me_s, piece], outs[piece].at[me_s, block], own_sem.at[block, piece]
         )
 
-    def scatter(block, rows):
+    def masked_copy(block, i, place):
+        other = (me_s + i) % n_seq
+        return remote(
+            send.at[block, other],
+            masked_all.at[place, :, block],
+            send_two.at[block, i],
+            recv_two.at[place, block],
+            (other, me_f),
+        )
+
+    def own_masked(block):
+        return pltpu.make_async_copy(
+            send.at[block, me_s], masked_all.at[me_s, :, block], own_two.at[block]
+        )
+
+    def pick(block, rows):
         def some(columns):
             picked = dot(hot[block], rows[:, columns], 1, 0).astype(BF)
             send[block, :, :, :, columns] = picked.reshape(n_seq, pieces, capacity, -1)
 
         chunked(width, 512, some)
+
+    def scatter(block, rows):
+        pick(block, rows)
         for i in range(1, n_seq):
             for piece in range(pieces):
-                row_copy(block, i, piece).start()
+                row_copy(block, i, piece, me_s).start()
         for piece in range(pieces):
             own_copy(block, piece).start()
 
-    def masked_copy(block):
-        return pltpu.make_async_copy(
-            masked_rows.at[block % 2], masked_out.at[:, :, block], masked_sem.at[block % 2]
-        )
-
-    def lay_masked(block):
-        if block >= 2:
-            masked_copy(block - 2).wait()
-
-        def some(columns):
-            picked = dot(hot[block], masked[block, :, columns], 1, 0).astype(BF)
-            masked_rows[block % 2, :, :, :, columns] = picked.reshape(n_seq, pieces, capacity, -1)
-
-        chunked(width, 512, some)
-        masked_copy(block).start()
+    def scatter_masked(block):
+        for piece in range(pieces):
+            own_copy(block, piece).wait()
+            for i in range(1, n_seq):
+                row_copy(block, i, piece, me_s).wait_send()
+        pick(block, masked.at[block])
+        for i in range(1, n_seq):
+            masked_copy(block, i, me_s).start()
+        own_masked(block).start()
+
+    def around(step, act):
+        @pl.when(me_f - step >= 0)
+        def _():
+            act(me_f - step)
+
+        @pl.when(me_f + step < n_fsdp)
+        def _():
+            act(me_f + step)
 
     @pl.when(me_f + 1 < n_fsdp)
     def _():
@@ -1070,7 +1180,6 @@
 
     scatter(me_f, x)
     gate_exchange.start()
-    lay_masked(0)
     for step in range(1, n_fsdp):
         line_step(
             n_fsdp,
@@ -1078,69 +1187,147 @@
             lambda block: line_copy(1, block, 0, me_f).wait_recv(),
             lambda block, way, to: line_copy(step, block, way, to).start(),
         )
-
-        @pl.when(me_f - step >= 0)
-        def _():
-            scatter(me_f - step, gathered.at[me_f - step])
-
-        @pl.when(me_f + step < n_fsdp)
-        def _():
-            scatter(me_f + step, gathered.at[me_f + step])
-
-        lay_masked(step)
-
+        around(step, lambda block: scatter(block, gathered.at[block]))
+    for step in range(1, n_fsdp):
+        around(step, scatter_masked)
     for step in range(n_fsdp):
         line_sent(
             n_fsdp, step, lambda block, way, to: line_copy(step, block, way, to).wait_send()
         )
-    for block in range(n_fsdp):
-        for piece in range(pieces):
-            own_copy(block, piece).wait()
+
+    gate_exchange.finish()
+    n = n_seq * n_fsdp
+    for piece in range(pieces):
+        lanes = lax.broadcasted_iota(jnp.int32, (n, capacity, 128), 2)
+        place = lax.broadcasted_iota(jnp.int32, (n, capacity, 128), 1)
+        values = jnp.broadcast_to(gates_out[:, piece : piece + 1, :], (n, capacity, 128))
+        column = jnp.sum(jnp.where(lanes == place, values, 0.0), axis=2, keepdims=True)
+        columns_out[piece] = column.reshape(n * capacity, 1)
+
+    for piece in range(pieces):
+        own_copy(me_f, piece).wait()
+        for i in range(1, n_seq):
+            row_copy(me_f, i, piece, me_s).wait_send()
+    for piece in range(pieces):
+        for block in range(n_fsdp):
             for i in range(1, n_seq):
-                source = (me_s + i) % n_seq
-                row_copy(block, i, piece).wait_send()
-                remote(
-                    send.at[block, source, piece],
-                    outs[piece].at[source, block],
-                    row_send.at[block, i, piece],
-                    row_recv.at[source, block, piece],
-                    (source, me_f),
-                ).wait_recv()
-    gate_exchange.finish()
-    for block in range(max(0, n_fsdp - 2), n_fsdp):
-        masked_copy(block).wait()
-
-
-def dispatch_rows(x, hot, gates, masked, n_seq, n_fsdp, pieces, capacity, collective_id):
-    rows, width = x.shape
+                row_copy(block, i, piece, (me_s + i) % n_seq).wait_recv()
+
+    ff = w_down.shape[1]
+    tile = min(256, ff)
+    steps = ff // tile
+    spans = seq_tile(n_seq, n_fsdp * capacity, 3072 // n_fsdp)
+    count = spans * n_fsdp * capacity
+    for piece in range(pieces):
+
+        def body(rows, w_gate, w_value, w_back, hidden, act, result, scaled_rows):
+            step = pl.program_id(1)
+            low = rows[...].reshape(count, width)
+            gate = dot(low, w_gate[0], 1, 0)
+            up = dot(low, w_value[0], 1, 0)
+            hidden[0] = gate
+            hidden[1] = up
+            act[...] = (gate * jax.nn.sigmoid(gate) * up).astype(BF)
+            product = dot(act[...], w_back[0], 1, 0)
+
+            @pl.when(step == 0)
+            def _():
+                total[...] = product
+
+            @pl.when(step > 0)
+            def _():
+                total[...] += product
+
+            @pl.when(step == steps - 1)
+            def _():
+                start = pl.multiple_of(pl.program_id(0) * count, 8)
+                column = columns_out[piece, pl.ds(start, count), :]
+                result[...] = total[...].astype(BF)
+                gated = (result[...].astype(F32) * column).astype(BF)
+                scaled_rows[...] = gated.reshape(scaled_rows.shape)
+
+        pltpu.emit_pipeline(
+            body,
+            grid=(n * capacity // count, steps),
+            in_specs=[
+                pl.BlockSpec((spans, n_fsdp, capacity, width), lambda r, i: (r, 0, 0, 0)),
+                pl.BlockSpec((1, width, tile), lambda r, i: (piece, 0, i)),
+                pl.BlockSpec((1, width, tile), lambda r, i: (piece, 0, steps + i)),
+                pl.BlockSpec((1, tile, width), lambda r, i: (piece, i, 0)),
+            ],
+            out_specs=[
+                pl.BlockSpec((2, count, tile), lambda r, i: (0, r, i)),
+                pl.BlockSpec((count, tile), lambda r, i: (r, i)),
+                pl.BlockSpec((count, width), lambda r, i: (r, 0)),
+                pl.BlockSpec((spans, 1, n_fsdp, capacity, width), lambda r, i: (r, piece, 0, 0, 0)),
+            ],
+        )(
+            outs[piece],
+            w_up,
+            w_up,
+            w_down,
+            hiddens[piece],
+            acts[piece],
+            results[piece],
+            scaled,
+        )
+
+    for step in range(1, n_fsdp):
+        around(step, lambda block: own_masked(block).wait())
+    for step in range(1, n_fsdp):
+        for i in range(1, n_seq):
+
+            def done(block):
+                masked_copy(block, i, me_s).wait_send()
+                masked_copy(block, i, (me_s + i) % n_seq).wait_recv()
+
+            around(step, done)
+
+
+def dispatch_rows(
+    x, hot, gates, masked, before, w_up, w_down, n_seq, n_fsdp, capacity, collective_id
+):
+    count, width = x.shape
+    pieces, ff = w_down.shape[:2]
+    rows = n_seq * n_fsdp * capacity
+    tile_rows = seq_tile(n_seq, n_fsdp * capacity, 3072 // n_fsdp) * n_fsdp * capacity
     vmem = pl.BlockSpec(memory_space=pltpu.VMEM)
+    any_space = pl.BlockSpec(memory_space=pl.ANY)
     dma = pltpu.SemaphoreType.DMA
     return pl.pallas_call(
         functools.partial(dispatch_kernel, n_seq, n_fsdp, pieces),
         out_shape=[
-            jax.ShapeDtypeStruct(gates.shape, F32),
-            jax.ShapeDtypeStruct((n_seq, pieces, n_fsdp, capacity, width), BF),
+            jax.ShapeDtypeStruct(before.shape, BF),
+            jax.ShapeDtypeStruct((pieces, rows, 1), F32),
+            jax.ShapeDtypeStruct(before.shape, BF),
         ]
-        + [jax.ShapeDtypeStruct((n_seq, n_fsdp, capacity, width), BF)] * pieces,
-        in_specs=[vmem] * 4,
-        out_specs=[vmem] + [pl.BlockSpec(memory_space=pl.ANY)] * (pieces + 1),
+        + [jax.ShapeDtypeStruct((n_seq, n_fsdp, capacity, width), BF)] * pieces
+        + [jax.ShapeDtypeStruct((2, rows, ff), F32)] * pieces
+        + [jax.ShapeDtypeStruct((rows, ff), BF)] * pieces
+        + [jax.ShapeDtypeStruct((rows, width), BF)] * pieces,
+        in_specs=[vmem] * 4 + [any_space] * 3,
+        out_specs=[any_space, vmem] + [any_space] * (1 + 4 * pieces),
         scratch_shapes=[
-            pltpu.VMEM((n_fsdp, rows, width), BF),
+            pltpu.VMEM(gates.shape, F32),
+            pltpu.VMEM((n_fsdp, count, width), BF),
             pltpu.VMEM((n_fsdp, n_seq, pieces, capacity, width), BF),
+            pltpu.VMEM((tile_rows, width), F32),
             dma((n_fsdp, pieces)),
             dma((2, n_fsdp)),
             dma((n_fsdp,)),
             dma((n_fsdp, n_seq, pieces)),
             dma((n_seq, n_fsdp, pieces)),
-            pltpu.VMEM((2, n_seq, pieces, capacity, width), BF),
-            dma((2,)),
+            dma((n_fsdp,)),
+            dma((n_fsdp, n_seq)),
+            dma((n_seq, n_fsdp)),
         ]
         + exchange_sems(n_seq * n_fsdp),
+        input_output_aliases={4: 0},
         compiler_params=pltpu.CompilerParams(
-            collective_id=collective_id, has_side_effects=True, vmem_limit_bytes=40 << 20
+            collective_id=collective_id, has_side_effects=True, vmem_limit_bytes=60 << 20
         ),
         name="dispatch_rows",
-    )(x, hot, gates, masked)
+    )(x, hot, gates, masked, before, w_up, w_down)
 
 
 def return_kernel(n_seq, n_fsdp, pieces, hot, gates, *refs):
@@ -1262,10 +1449,12 @@
 
 
 def weight_grad_kernel(a, b, *refs):
-    refs[-1][0] = dot(a[...], b[0], 0, 0)
-
-
-def weight_grad(a, b, whole, piece, pieces, part):
+    parts, _, n = b.shape
+    for part in range(parts):
+        refs[-1][0, :, part * n : (part + 1) * n] = dot(a[...], b[part], 0, 0)
+
+
+def weight_grad(a, b, whole, piece, pieces):
     rows, m = a.shape
     parts, _, n = b.shape
     tile = min(256, m)
@@ -1276,94 +1465,25 @@
         grid=(m // tile,),
         in_specs=[
             pl.BlockSpec((rows, tile), lambda i: (0, i)),
-            pl.BlockSpec((1, rows, n), lambda i: (part, 0, 0)),
+            pl.BlockSpec((parts, rows, n), lambda i: (0, 0, 0)),
         ]
         + [pl.BlockSpec(memory_space=pl.ANY)] * len(more),
-        out_specs=pl.BlockSpec((1, tile, n), lambda i: (piece, i, part)),
+        out_specs=pl.BlockSpec((1, tile, n * parts), lambda i: (piece, i, 0)),
         input_output_aliases={2: 0} if more else {},
         cost_estimate=pl.CostEstimate(
-            flops=2 * rows * m * n,
-            bytes_accessed=2 * rows * (m + n) + 4 * m * n,
+            flops=2 * rows * m * n * parts,
+            bytes_accessed=4 * m * n * parts,
             transcendentals=0,
         ),
         name="weight_grad",
     )(a, b, *more)
 
 
-def seq_tile(n_seq, rows_each):
+def seq_tile(n_seq, rows_each, most=1024):
     tile = n_seq
-    while tile > 1 and (tile * rows_each > 1024 or n_seq % tile):
+    while tile > 1 and (tile * rows_each > most or n_seq % tile):
         tile -= 1
     return tile
-
-
-def expert_forward_kernel(x, gates, w_gate, w_up, w_down, *refs):
-    hidden, activation, out, scaled, total = refs[-5:]
-    step = pl.program_id(1)
-    gate = dot(x[...], w_gate[0], 1, 0)
-    up = dot(x[...], w_up[0], 1, 0)
-    hidden[0] = gate
-    hidden[1] = up
-    act = (gate * jax.nn.sigmoid(gate) * up).astype(BF)
-    activation[...] = act
-    product = dot(act, w_down[0], 1, 0)
-
-    @pl.when(step == 0)
-    def _():
-        total[...] = product
-
-    @pl.when(step > 0)
-    def _():
-        total[...] += product
-
-    @pl.when(step == pl.num_programs(1) - 1)
-    def _():
-        low = total[...].astype(BF)
-        out[...] = low
-        scaled[...] = (low.astype(F32) * gates[...]).astype(BF).reshape(scaled.shape)
-
-
-def expert_forward(x, gates, w_up, w_down, whole, piece, n_seq, n_fsdp):
-    rows, width = x.shape
-    pieces, ff = w_down.shape[:2]
-    capacity = rows // (n_seq * n_fsdp)
-    tile = min(256, ff)
-    steps = ff // tile
-    spans = seq_tile(n_seq, n_fsdp * capacity)
-    count = spans * n_fsdp * capacity
-    more = [] if whole is None else [whole]
-    fixed = lambda r, i: (r, 0)
-    return pl.pallas_call(
-        expert_forward_kernel,
-        out_shape=[
-            jax.ShapeDtypeStruct((2, rows, ff), F32),
-            jax.ShapeDtypeStruct((rows, ff), BF),
-            jax.ShapeDtypeStruct((rows, width), BF),
-            jax.ShapeDtypeStruct((n_seq, pieces, n_fsdp, capacity, width), BF),
-        ],
-        grid=(rows // count, steps),
-        in_specs=[
-            pl.BlockSpec((count, width), fixed),
-            pl.BlockSpec((count, 1), fixed),
-            pl.BlockSpec((1, width, tile), lambda r, i: (piece, 0, i)),
-            pl.BlockSpec((1, width, tile), lambda r, i: (piece, 0, steps + i)),
-            pl.BlockSpec((1, tile, width), lambda r, i: (piece, i, 0)),
-        ]
-        + [pl.BlockSpec(memory_space=pl.ANY)] * len(more),
-        out_specs=[
-            pl.BlockSpec((2, count, tile), lambda r, i: (0, r, i)),
-            pl.BlockSpec((count, tile), lambda r, i: (r, i)),
-            pl.BlockSpec((count, width), fixed),
-            pl.BlockSpec((spans, 1, n_fsdp, capacity, width), lambda r, i: (r, piece, 0, 0, 0)),
-        ],
-        scratch_shapes=[pltpu.VMEM((count, width), F32)],
-        input_output_aliases={5: 3} if more else {},
-        compiler_params=pltpu.CompilerParams(vmem_limit_bytes=56 << 20),
-        cost_estimate=pl.CostEstimate(
-            flops=6 * rows * width * ff, bytes_accessed=6 * width * ff, transcendentals=rows * ff
-        ),
-        name="expert_forward",
-    )(x, gates, w_up, w_up, w_down, *more)
 
 
 def expert_backward_kernel(masked, gates, piece_out, hidden, w_down, out, grad, inner, partial):
@@ -1611,7 +1731,7 @@
                 full(2 * heads),
                 pl.BlockSpec((8, block), lambda h, i, n: (0, i)),
                 pl.BlockSpec((8, slot_len), lambda h, i, n: (0, 0)),
-                pl.BlockSpec((4, hd), lambda h, i, n: (0, h)),
+                pl.BlockSpec((8, hd), lambda h, i, n: (0, h)),
                 table,
                 table,
                 whole_table,
@@ -1723,7 +1843,7 @@
                 full(heads),
                 pl.BlockSpec((8, block), lambda h, i, n: (0, i)),
                 pl.BlockSpec((8, slot_len), lambda h, i, n: (0, 0)),
-                pl.BlockSpec((4, hd), lambda h, i, n: (0, h)),
+                pl.BlockSpec((8, hd), lambda h, i, n: (0, h)),
                 table,
                 table,
                 whole_table,
@@ -1867,39 +1987,41 @@
     push_all = functools.partial(push, n_seq=n_seq, n_fsdp=n_fsdp, scope="all")
     push_seq = functools.partial(push, n_seq=n_seq, n_fsdp=n_fsdp, scope="seq")
 
-    gain_size, router_size = norm_gains.size, router_weight.size
-    pieces = [norm_gains.reshape(-1), router_weight.reshape(-1), local_routes.astype(BF).reshape(-1)]
-    small, slot_tokens, qkv_local = first_gather(
-        rows_of(jnp.concatenate(pieces), 16),
+    masked_low = jnp.where(row_valid[:, None] > 0, cotangent[0], jnp.zeros((), BF))
+    own_small = jnp.concatenate(
+        [
+            jnp.pad(norm_gains, ((0, 4), (0, 128 - owned))),
+            local_routes.T.astype(BF),
+            rows_of(router_weight.reshape(-1), 16),
+        ]
+    )
+    small, gains, slot_tokens, qkv_local, cot_all, to_places, to_rows = first_gather(
+        own_small,
         tokens[0],
         qkv_weight,
+        masked_low,
         n_seq,
         n_fsdp,
+        pieces_dev,
+        split,
+        capacity,
+        top_count,
         collective_id=0,
     )
     slot_tokens = slot_tokens.reshape(slot_len, width)
     qkv_local = qkv_local.reshape(width, 3 * head_width)
-    small = small.reshape(n_dev, -1)
-    gains = small[:, :gain_size].reshape(n_dev, 4, owned).swapaxes(0, 1).reshape(4, width).astype(F32)
-    router = small[:, gain_size : gain_size + router_size].reshape(width, experts)
-    all_routes = small[:, gain_size + router_size :][:, : shard_len * top_count]
+    router = small[:, 8 + top_count :].reshape(n_dev, -1)[:, : owned * experts]
+    router = router.reshape(width, experts)
+    all_routes = small[:, 8 : 8 + top_count].swapaxes(1, 2)
     all_routes = all_routes.reshape(n_seq, n_fsdp, shard_len, top_count).astype(jnp.int32)
-
-    masked_low = jnp.where(row_valid[:, None] > 0, cotangent[0], jnp.zeros((), BF))
     proj_later = lax.optimization_barrier((proj_weight, slot_tokens))[0]
     proj_rows = lax.all_gather(proj_later, "fsdp", axis=0, tiled=True)
 
-    plane_routes = lax.dynamic_index_in_dim(all_routes, me_s, 0, keepdims=False)
-    piece_ids = (jnp.arange(n_seq)[:, None] * n_fsdp + me_f) * pieces_dev + jnp.arange(pieces_dev)
-    plane_experts = (piece_ids // split).reshape(-1).astype(jnp.int32)
-    plane_hot = jax.vmap(lambda r: places(r, plane_experts, capacity))(plane_routes)
-    to_rows = plane_hot.reshape(n_fsdp, shard_len, -1).astype(BF)
-    to_places = to_rows.swapaxes(1, 2)
-
     def exchange(rows):
         return lax.all_to_all(rows, "seq", split_axis=0, concat_axis=0, tiled=True)
 
     normed_one, raw, totals = front(slot_tokens, gains, qkv_local, n_seq, collective_id=1)
+
     masked_later = lax.optimization_barrier((masked_low, raw))[0]
     plane_masked = lax.all_gather(masked_later, "fsdp", axis=0)
 
@@ -1929,47 +2051,36 @@
     own_hot = places(local_routes, jnp.arange(experts, dtype=jnp.int32), capacity)
     gate_slot = jnp.sum(own_hot * router_probs[:, :, None], axis=0)
     gate_send = jnp.broadcast_to(gate_slot[:, None], (experts, split, capacity))
-    gate_send = gate_send.reshape(n_dev, pieces_dev * capacity)
-    gate_pad = -pieces_dev * capacity % 1024
-    gate_send = jnp.pad(gate_send, ((0, 0), (0, gate_pad))).reshape(n_dev, -1, 128)
-    gate_recv, cot_rows, *piece_rows = dispatch_rows(
+    gate_send = gate_send.reshape(n_dev, pieces_dev, capacity)
+    gate_send = jnp.pad(gate_send, ((0, 0), (0, -pieces_dev % 8), (0, 128 - capacity)))
+    cot_all, gate_columns, outs, *experts_forward = dispatch_rows(
         normed_two,
         to_places,
         gate_send,
         plane_masked,
+        cot_all,
+        expert_up,
+        expert_down,
         n_seq,
         n_fsdp,
-        pieces_dev,
         capacity,
         collective_id=6,
     )
-    cot_all = exchange(cot_rows)
-    gate_recv = gate_recv.reshape(n_dev, -1)[:, : pieces_dev * capacity]
-    gate_recv = gate_recv.reshape(n_dev, pieces_dev, capacity)
-
-    forward = []
-    outs = None
-    for piece in range(pieces_dev):
-        gate_rows = gate_recv[:, piece].reshape(-1, 1)
-        rows = piece_rows[piece].reshape(-1, width)
-        result = expert_forward(rows, gate_rows, expert_up, expert_down, outs, piece, n_seq, n_fsdp)
-        outs = result[-1]
-        forward.append((gate_rows, rows) + tuple(result[:-1]))
     outs_back = exchange(outs)
-    cot_all, forward = lax.optimization_barrier((cot_all, forward))
     backs, gate_backs = [], []
     up_grad = down_grad = None
     for piece in range(pieces_dev):
-        gate_rows, rows, hidden, activation, piece_out = forward[piece]
+        rows, hidden, activation, piece_out = experts_forward[piece::pieces_dev]
+        rows = rows.reshape(-1, width)
         hidden_grad, out_grad, gate_back = expert_backward(
-            cot_all, gate_rows, piece_out, hidden, expert_down, piece
+            cot_all, gate_columns[piece], piece_out, hidden, expert_down, piece
         )
         gate_backs.append(gate_back[0].reshape(n_dev, capacity))
         backs.append(expert_input(hidden_grad, expert_up, piece))
-        down_grad = weight_grad(activation, out_grad[None], down_grad, piece, pieces_dev, 0)
-        for part in range(2):
-            up_grad = weight_grad(rows, hidden_grad, up_grad, piece, pieces_dev, part)
+        down_grad = weight_grad(activation, out_grad[None], down_grad, piece, pieces_dev)
+        up_grad = weight_grad(rows, hidden_grad, up_grad, piece, pieces_dev)
     back_send = jnp.stack(gate_backs, axis=1).reshape(n_dev, pieces_dev * capacity)
+    gate_pad = -pieces_dev * capacity % 1024
     back_send = jnp.pad(back_send, ((0, 0), (0, gate_pad))).reshape(n_dev, -1, 128)
     backs, outs_back, up_grad, down_grad = lax.optimization_barrier(
         (backs, outs_back, up_grad, down_grad)

time: 725 us -> 697 us (0.961)
  waiting for transfers between devices: 28.9 us -> 0.08 us
    pallas_call x1, Pallas kernels: 75.2 us -> 129 us  [dispatch_rows(): pl.pallas_call(functools.partial(dispatch_kernel, n_seq, n_fsdp, pieces),...]
    pallas_call x3 -> x1, Pallas kernels: 115 us -> 82.3 us  [first_gather(): pl.pallas_call(functools.partial(first_kernel, n_seq, n_fsdp, pieces, spl...]
    all_to_all x2 -> x1, waiting for transfers between devices: 28.8 us -> 0.01 us  [exchange(): return lax.all_to_all(rows, 'seq', split_axis=0, concat_axis=0, tiled=True)]
    pallas_call x6 -> x4, Pallas kernels: 55.1 us -> 41.9 us  [weight_grad(): pl.pallas_call(weight_grad_kernel, out_shape=jax.ShapeDtypeStruct((pieces...]
    unnamed x126 -> x124, local copies, waits for them, and re-layouts: 32 us -> 31.8 us
  transfers between devices with their start and end apart: 6 -> 5, of which waited for: 1 -> 0; matrix products, arithmetic and copies ran while one was open for 5% -> 5% of each run, Pallas kernels for 37% -> 31%
where the time goes in v3:
time: 697 us; the launch traced here: 686 us
  Pallas kernels  565 us (81%)
  local copies, waits for them, and re-layouts  47.9 us (7%)
  matrix products  26.2 us (4%)
  other arithmetic  19.7 us (3%)
  between operations  17.1 us (2%)
  starting transfers between devices  9.68 us (1%)
    pallas_call x1, Pallas kernels, dispatch_rows(): pl.pallas_call(functools.partial(dispatch_kernel, n_seq, n_fsdp, pieces),...  129 us
    pallas_call x1, Pallas kernels, first_gather(): pl.pallas_call(functools.partial(first_kernel, n_seq, n_fsdp, pieces, spl...  82.3 us
    pallas_call x1, Pallas kernels, return_rows(): pl.pallas_call(functools.partial(return_kernel, n_seq, n_fsdp, pieces), o...  79.1 us
    pallas_call x1, Pallas kernels, last_reduce(): pl.pallas_call(functools.partial(last_kernel, n_seq, n_fsdp), out_shape=[...  64 us
    pallas_call x4, Pallas kernels, weight_grad(): pl.pallas_call(weight_grad_kernel, out_shape=jax.ShapeDtypeStruct((pieces...  41.9 us
    pallas_call x1, Pallas kernels, gather_seq(): pl.pallas_call(functools.partial(gather_kernel, n_seq, n_fsdp), out_shape...  34.2 us
    unnamed x124, local copies, waits for them, and re-layouts  31.8 us
    pallas_call x1, Pallas kernels, product_reduced(): pl.pallas_call(functools.partial(reduce_kernel, n_seq, w_dim), out_shape=...  29.9 us
  transfers between devices with their start and end apart: 5, of which 0 were waited for; matrix products, arithmetic and copies ran while one was open for 5% of the time, Pallas kernels for 31%

profile of v3, /device:TPU:0, one launch (start us, length us, event | category | flops | bytes accessed | tf_op | source)
XLA Modules:
  0.0 685.9 jit_solution(7341127997438752213)
XLA Ops:
  8.7 1.2 dynamic_slice.12.length
  10.6 1.9 bitcast_select_fusion.masked
  15.3 1.1 copy-done.19
  16.5 82.3 %first_gather.1 = (bf16[32,48,128]{2,1,0:T(8,128)(2,1)S(1)}, f32[8,2048]{1,0:T(8,128)S(1)}, bf16[8,128,2048]{2,1,0:T(8,128)(2,1)S(1)}, bf16[8,4,64,768]{3,2,1,0:...) custom-call(bf16[48,128]{1,0:T(8,128)(2,1)S(1)} %fusion.24.small, ...), custom_call_target="tpu_custom_call" | custom-call | tf_op jit(solution)/shard_map/first_gather/pallas_call | solution.py:561
  98.8 2.0 copy-done.7
  103.9 16.8 %front.1 = (bf16[1024,2048]{1,0:T(8,128)(2,1)S(1)}, f32[1024,768]{1,0:T(8,128)S(1)}, f32[8,1024]{1,0:T(8,128)S(1)}) custom-call(bf16[1024,2048]{1,0:T(8,128)(2,1)} %bitcast.100, f32[8,2048]{1,0:T(8,128)S(1)} %copy-done.26, bf16[2048,768]{1,0:T(8,128)(2,1)S(1)} %bitcast.96), custom_call_target="tpu_custom_call" | custom-call | tf_op jit(solution)/shard_map/front/pallas_call | solution.py:1648
  120.7 1.7 copy-done
  123.0 2.0 copy-done.34
  127.1 1.3 constant_dynamic-slice_fusion.1.gain
  128.5 1.9 fusion.11
  130.4 1.3 pad_maximum_fusion
  131.7 10.9 %attend.1 = (bf16[1024,256]{1,0:T(8,128)(2,1)}, bf16[1024,256]{1,0:T(8,128)(2,1)}, bf16[1024,256]{1,0:T(8,128)(2,1)}, bf16[1024,256]{1,0:T(8,128)(2,1)}) custom-call(s32[1]{0:T(128)} %dynamic_slice.12.length, f32[1024,768]{1,0:T(8,128)} %copy-done, f32[1024,768]{1,0:T(8,128)} %copy-done, f32[1024,768]{1,0:T(8,128)} %copy-done, f32[8,1024]{1,0:T(8,128)} %copy-done.28, ...), custom_call_target="tpu_custom_call" | custom-call | flops 1073741824 | bytes 8388608 | tf_op jit(solution)/shard_map/attend/pallas_call | solution.py:1722
  142.9 1.3 copy-done.15
  145.2 29.9 %product_reduced.1 = f32[128,2048]{1,0:T(8,128)S(1)} custom-call(bf16[8,128,256]{2,1,0:T(8,128)(2,1)S(1)} %bitcast.104, bf16[256,2048]{1,0:T(8,128)(2,1)S(1)} %copy-done.15), custom_call_target="tpu_custom_call" | custom-call | tf_op jit(solution)/shard_map/product_reduced/pallas_call | solution.py:869
  179.3 129.1 %dispatch_rows.1 = (bf16[8,2,4,24,2048]{4,3,2,1,0:T(8,128)(2,1)}, f32[2,768,1]{2,1,0:T(8,128)}, bf16[8,2,4,24,2048]{4,3,2,1,0:T(8,128)(2,1)}, bf16[8,4,24,2048]{...) custom-call(bf16[128,2048]{1,0:T(8,128)(2,1)} %copy-done.38, ...), custom_call_target="tpu_custom_call", output_to_operand_aliasing={{0}: (4, {})} | custom-call | tf_op jit(solution)/shard_map/dispatch_rows/pallas_call | solution.py:1297
  308.3 5.0 all-to-all-start
  320.0 2.0 multiply_divide_fusion
  322.0 12.3 %expert_backward.3 = (bf16[2,768,1024]{2,1,0:T(8,128)(2,1)S(1)}, bf16[768,2048]{1,0:T(8,128)(2,1)}, f32[8,768]{1,0:T(8,128)S(1)}) custom-call(bf16[8,2,4,24,2048]{4,3,2,1,0:T(8,128)(2,1)} %get-tuple-element.81.masked, f32[768,1]{1,0:T(8,128)S(1)} %get-tuple-element.163.gates, bf16[768,2048]{1,0:T(8,128)(2,1)} %get-tuple-element.86.piece_out, ...), custom_call_target="tpu_custom_call" | custom-call | flops 3221225472 | bytes 9437184 | tf_op jit(solution)/shard_map/expert_backward/pallas_call | solution.py:1521
  334.3 1.6 copy-done.9
  336.1 12.3 %expert_backward.2 = (bf16[2,768,1024]{2,1,0:T(8,128)(2,1)S(1)}, bf16[768,2048]{1,0:T(8,128)(2,1)}, f32[8,768]{1,0:T(8,128)S(1)}) custom-call(bf16[8,2,4,24,2048]{4,3,2,1,0:T(8,128)(2,1)} %get-tuple-element.81.masked, f32[768,1]{1,0:T(8,128)S(1)} %get-tuple-element.162.gates, bf16[768,2048]{1,0:T(8,128)(2,1)} %get-tuple-element.83.piece_out, ...), custom_call_target="tpu_custom_call" | custom-call | flops 3221225472 | bytes 9437184 | tf_op jit(solution)/shard_map/expert_backward/pallas_call | solution.py:1521
  348.4 1.7 copy-done.10
  351.2 8.0 %weight_grad.6.refs_0_ = f32[2,1024,2048]{2,1,0:T(8,128)} custom-call(bf16[768,1024]{1,0:T(8,128)(2,1)} %get-tuple-element.96.a, bf16[1,768,2048]{2,1,0:T(8,128)(2,1)} %bitcast.111), custom_call_target="tpu_custom_call" | custom-call | flops 3221225472 | bytes 8388608 | tf_op jit(solution)/shard_map/weight_grad/pallas_call | solution.py:1462
  359.2 8.0 %weight_grad.7 = f32[2,1024,2048]{2,1,0:T(8,128)} custom-call(bf16[768,1024]{1,0:T(8,128)(2,1)} %get-tuple-element.94.a, bf16[1,768,2048]{2,1,0:T(8,128)(2,1)} %bitcast.109, f32[2,1024,2048]{2,1,0:T(8,128)} %weight_grad.6.refs_0_), custom_call_target="tpu_custom_call", output_to_operand_aliasing={{}: (2, {})} | custom-call | flops 3221225472 | bytes 8388608 | tf_op jit(solution)/shard_map/weight_grad/pallas_call | solution.py:1462
  367.2 12.4 %expert_input.2 = bf16[768,2048]{1,0:T(8,128)(2,1)} custom-call(bf16[2,768,1024]{2,1,0:T(8,128)(2,1)} %copy-done.10, bf16[2,2048,2048]{2,1,0:T(8,128)(2,1)} %w_up.5), custom_call_target="tpu_custom_call" | custom-call | flops 6442450944 | bytes 8388608 | tf_op jit(solution)/shard_map/expert_input/pallas_call | solution.py:1560
  379.6 12.4 %expert_input.3 = bf16[768,2048]{1,0:T(8,128)(2,1)} custom-call(bf16[2,768,1024]{2,1,0:T(8,128)(2,1)} %copy-done.9, bf16[2,2048,2048]{2,1,0:T(8,128)(2,1)} %w_up.5), custom_call_target="tpu_custom_call" | custom-call | flops 6442450944 | bytes 8388608 | tf_op jit(solution)/shard_map/expert_input/pallas_call | solution.py:1560
  392.0 12.7 %weight_grad.4.refs_0_ = f32[2,2048,2048]{2,1,0:T(8,128)} custom-call(bf16[768,2048]{1,0:T(8,128)(2,1)} %bitcast.108, bf16[2,768,1024]{2,1,0:T(8,128)(2,1)} %copy-done.10), custom_call_target="tpu_custom_call" | custom-call | flops 6442450944 | bytes 16777216 | tf_op jit(solution)/shard_map/weight_grad/pallas_call | solution.py:1462
  404.7 13.2 %weight_grad.5 = f32[2,2048,2048]{2,1,0:T(8,128)} custom-call(bf16[768,2048]{1,0:T(8,128)(2,1)} %bitcast.107, bf16[2,768,1024]{2,1,0:T(8,128)(2,1)} %copy-done.9, f32[2,2048,2048]{2,1,0:T(8,128)} %weight_grad.4.refs_0_), custom_call_target="tpu_custom_call", output_to_operand_aliasing={{}: (2, {})} | custom-call | flops 6442450944 | bytes 16777216 | tf_op jit(solution)/shard_map/weight_grad/pallas_call | solution.py:1462
  417.9 1.9 copy-done.12
  420.7 79.1 %return_rows.1 = (f32[128,2048]{1,0:T(8,128)S(1)}, f32[32,8,128]{2,1,0:T(8,128)S(1)}) custom-call(bf16[4,128,384]{2,1,0:T(8,128)(2,1)S(1)} %get-tuple-element.76.hot, f32[32,8,128]{2,1,0:T(8,128)S(1)} %copy-done.23, bf16[8,4,24,2048]{3,2,1,0:T(8,128)(2,1)S(1)} %bitcast.101, bf16[8,4,24,2048]{3,2,1,0:T(8,128)(2,1)S(1)} %bitcast.102), custom_call_target="tpu_custom_call" | custom-call | tf_op jit(solution)/shard_map/return_rows/pallas_call | solution.py:1425
  502.9 2.7 multiply_reduce_fusion
  505.7 3.5 slice_bitcast_fusion
  510.0 2.2 fusion.1
  512.2 1.5 fusion.30
  513.7 4.6 all-to-all-start.1
  518.4 1.2 fusion.27.terms
  519.6 34.2 %gather_seq.1 = (bf16[8,128,2048]{2,1,0:T(8,128)(2,1)}, f32[64,256]{1,0:T(8,128)}) custom-call(bf16[128,2048]{1,0:T(8,128)(2,1)} %get-tuple-element.104.x, f32[64,2048]{1,0:T(8,128)} %fusion.27.terms), custom_call_target="tpu_custom_call" | custom-call | bytes 67108864 | tf_op jit(solution)/shard_map/gather_seq/pallas_call | solution.py:719
  553.8 4.5 convolution_convert_fusion.1
  558.4 4.3 convolution_convert_fusion.2.g_ref
  562.7 17.3 %attend_back.1 = (f32[1024,256]{1,0:T(8,128)}, f32[1024,256]{1,0:T(8,128)}, bf16[1024,256]{1,0:T(8,128)(2,1)}, f32[8,1024]{1,0:T(8,128)}, f32[8,256]{1,0:T(8,128)}) custom-call(s32[1]{0:T(128)} %dynamic_slice.12.length, bf16[1024,256]{1,0:T(8,128)(2,1)} %get-tuple-element.73.q_ref, bf16[1024,256]{1,0:T(8,128)(2,1)} %get-tuple-element.74.k_ref, ...), custom_call_target="tpu_custom_call" | custom-call | flops 5368709120 | bytes 16777216 | tf_op jit(solution)/shard_map/attend_back/pallas_call | solution.py:1825
  580.8 1.2 copy-done.17
  582.0 1.2 copy-done.18
  585.0 10.3 %raw_back.1 = (bf16[1024,768]{1,0:T(8,128)(2,1)S(1)}, f32[64,256]{1,0:T(8,128)S(1)}) custom-call(f32[1024,256]{1,0:T(8,128)S(1)} %copy-done.17, f32[1024,256]{1,0:T(8,128)S(1)} %copy-done.18, bf16[1024,256]{1,0:T(8,128)(2,1)S(1)} %copy-done.22, f32[1024,768]{1,0:T(8,128)S(1)} %copy-done.1, f32[8,1024]{1,0:T(8,128)S(1)} %copy-done.29, ...), custom_call_target="tpu_custom_call" | custom-call | tf_op jit(solution)/shard_map/raw_back/pallas_call | solution.py:1915
  595.3 1.1 copy-done.13
  597.3 1.8 convert_element_type.121
  599.0 8.0 %convolution_convert_fusion = bf16[2048,768]{1,0:T(8,128)(2,1)} fusion(bf16[1024,2048]{1,0:T(8,128)(2,1)} %copy-done.34, bf16[1024,768]{1,0:T(8,128)(2,1)} %copy-done.13), kind=kOutput, calls=%fused_computation.6 | convolution fusion | flops 3222798336 | bytes 8912896 | tf_op jit(solution)/shard_map/dot_general | solution.py:21
  607.0 64.0 %last_reduce.1 = (bf16[128,2048]{1,0:T(8,128)(2,1)S(1)}, f32[64,6144]{1,0:T(8,128)S(1)}, f32[8,256]{1,0:T(8,128)S(1)}) custom-call(bf16[8,128,768]{2,1,0:T(8,128)(2,1)} %bitcast.103, bf16[2048,768]{1,0:T(8,128)(2,1)} %bitcast.97, bf16[8,4,64,768]{3,2,1,0:T(8,128)(2,1)} %bitcast.110, bf16[128,2048]{1,0:T(8,128)(2,1)S(1)} %bitcast.99, ...), custom_call_target="tpu_custom_call" | custom-call | bytes 134217728 | tf_op jit(solution)/shard_map/last_reduce/pallas_call | solution.py:1050
  671.1 2.2 convert_reduce_fusion
  676.9 1.1 copy.71
  (178 shorter events, 34.5 us)
Async XLA Ops:
  7.2 135.7 %all-gather.4.cloned.1.call-start = ((), (), s32[]{:S(2)}) async-start(), calls=%async_computation.3 | async-start | bytes 1310720 | tf_op jit(solution)/shard_map/all_gather | solution.py:2018
  10.6 2.6 copy-start.54
  15.3 1.1 copy-start.19
  98.8 2.0 copy-start.7
  102.9 17.8 %copy-start.2 = (bf16[8,4,64,768]{3,2,1,0:T(8,128)(2,1)}, bf16[8,4,64,768]{3,2,1,0:T(8,128)(2,1)S(1)}, u32[]{:S(2)}) copy-start(bf16[8,4,64,768]{3,2,1,0:T(8,128)(2,1)S(1)} %get-tuple-element.68) | copy-start | bytes 9437188
  103.0 76.3 %all-gather.6.cloned.1.call-start = ((), (), s32[]{:S(2)}) async-start(), calls=%async_computation.5 | async-start | bytes 2621440 | tf_op jit(solution)/shard_map/all_gather | solution.py:2026
  120.7 1.7 copy-start
  123.0 2.0 copy-start.34
  127.1 49.5 %copy-start.40 = (bf16[2048,64]{1,0:T(8,128)(2,1)}, bf16[2048,64]{1,0:T(8,128)(2,1)S(1)}, u32[]{:S(2)}) copy-start(bf16[2048,64]{1,0:T(8,128)(2,1)S(1)} %reshape_reshape.3) | copy-start | bytes 786436
  131.7 11.0 %copy-start.49 = (s32[1,128,8]{1,2,0:T(8,128)S(1)}, s32[1,128,8]{1,2,0:T(8,128)}, u32[]{:S(2)}) copy-start(s32[1,128,8]{1,2,0:T(8,128)} %param.13) | copy-start | bytes 12292
  131.7 43.4 %copy-start.5 = (bf16[1,128,2048]{2,1,0:T(8,128)(2,1)S(1)}, bf16[1,128,2048]{2,1,0:T(8,128)(2,1)}, u32[]{:S(2)}) copy-start(bf16[1,128,2048]{2,1,0:T(8,128)(2,1)} %param.10) | copy-start | bytes 1572868
  142.7 35.0 %copy-start.47 = (f32[128,64]{0,1:T(8,128)}, f32[128,64]{0,1:T(8,128)S(1)}, u32[]{:S(2)}) copy-start(f32[128,64]{0,1:T(8,128)S(1)} %convert_reduce_fusion.1) | copy-start | bytes 98308
  142.9 34.8 %copy-start.48 = (f32[128,64]{0,1:T(8,128)}, f32[128,64]{0,1:T(8,128)S(1)}, u32[]{:S(2)}) copy-start(f32[128,64]{0,1:T(8,128)S(1)} %fusion.14) | copy-start | bytes 98308
  142.9 1.3 copy-start.15
  176.7 2.6 copy-start.38
  177.0 1.5 copy-start.46
  308.3 5.0 copy-start.56
  308.3 109.6 %all-to-all-start = ((bf16[8,2,4,24,2048]{4,3,2,1,0:T(8,128)(2,1)}), bf16[8,2,4,24,2048]{4,3,2,1,0:T(8,128)(2,1)}, u32[]{:S(2)}, u32[]{:S(2)}) async-start(bf16[8,2,4,24,2048]{4,3,2,1,0:T(8,128)(2,1)} %get-tuple-element.91), calls=%async_computation | async-start | bytes 12582912 | tf_op jit(solution)/shard_map/all_to_all | solution.py:2021
  318.0 4.0 copy-start.43
  334.3 1.6 copy-start.9
  348.4 1.7 copy-start.10
  404.7 13.2 %copy-start.11 = (bf16[768,2048]{1,0:T(8,128)(2,1)S(1)}, bf16[768,2048]{1,0:T(8,128)(2,1)}, u32[]{:S(2)}) copy-start(bf16[768,2048]{1,0:T(8,128)(2,1)} %expert_input.2) | copy-start | bytes 9437188
  417.9 1.9 copy-start.12
  505.7 3.5 copy-start.42
  509.9 2.2 copy-start.36
  509.9 2.2 copy-start.41
  509.9 2.2 copy-start.53
  509.9 2.2 copy-start.55
  510.0 2.2 copy-start.58
  513.7 4.7 copy-start.39
  513.7 4.7 copy-start.45
  513.7 4.7 copy-start.51
  513.7 40.1 %copy-start.21 = (bf16[1024,256]{1,0:T(8,128)(2,1)S(1)}, bf16[1024,256]{1,0:T(8,128)(2,1)}, u32[]{:S(2)}) copy-start(bf16[1024,256]{1,0:T(8,128)(2,1)} %get-tuple-element.71) | copy-start | bytes 1572868
  513.7 85.4 %all-to-all-start.1 = ((bf16[4,128,2048]{2,1,0:T(8,128)(2,1)}), bf16[4,128,2048]{2,1,0:T(8,128)(2,1)}, u32[]{:S(2)}, u32[]{:S(2)}) async-start(bf16[4,128,2048]{2,1,0:T(8,128)(2,1)} %fusion.1), calls=%async_computation.1 | async-start | bytes 4194304 | tf_op jit(solution)/shard_map/all_to_all | solution.py:2127
  518.3 79.0 %reduce-scatter.2.cloned.1.call-start = ((), (), s32[]{:S(2)}) async-start(), calls=%async_computation.4 | async-start | bytes 1310720 | tf_op jit(solution)/shard_map/reduce_scatter | solution.py:2186
  553.8 4.6 copy-start.16
  562.7 18.0 %copy-start.1 = (f32[1024,768]{1,0:T(8,128)S(1)}, f32[1024,768]{1,0:T(8,128)}, u32[]{:S(2)}) copy-start(f32[1024,768]{1,0:T(8,128)} %copy-done) | copy-start | bytes 9437188
  562.7 18.0 %copy-start.29 = (f32[8,1024]{1,0:T(8,128)S(1)}, f32[8,1024]{1,0:T(8,128)}, u32[]{:S(2)}) copy-start(f32[8,1024]{1,0:T(8,128)} %copy-done.28) | copy-start | bytes 98308
  562.7 18.0 %copy-start.31 = (f32[8,256]{1,0:T(8,128)S(1)}, f32[8,256]{1,0:T(8,128)}, u32[]{:S(2)}) copy-start(f32[8,256]{1,0:T(8,128)} %constant_dynamic-slice_fusion.1.gain) | copy-start | bytes 24580
  562.7 18.0 %copy-start.32 = (f32[64,256]{1,0:T(8,128)S(1)}, f32[64,256]{1,0:T(8,128)}, u32[]{:S(2)}) copy-start(f32[64,256]{1,0:T(8,128)} %get-tuple-element.110.terms) | copy-start | bytes 196612
  580.7 1.2 copy-start.17
  582.0 1.2 copy-start.18
  595.3 1.1 copy-start.13
  599.0 8.0 %copy-start.6 = (bf16[1,128,2048]{2,1,0:T(8,128)(2,1)S(1)}, bf16[1,128,2048]{2,1,0:T(8,128)(2,1)}, u32[]{:S(2)}) copy-start(bf16[1,128,2048]{2,1,0:T(8,128)(2,1)} %param.10) | copy-start | bytes 1572868
  599.0 8.0 %copy-start.8 = (f32[128,2048]{1,0:T(8,128)S(1)}, f32[128,2048]{1,0:T(8,128)}, u32[]{:S(2)}) copy-start(f32[128,2048]{1,0:T(8,128)} %get-tuple-element.155.mid) | copy-start | bytes 3145732
  599.0 8.0 %copy-start.27 = (f32[8,2048]{1,0:T(8,128)S(1)}, f32[8,2048]{1,0:T(8,128)}, u32[]{:S(2)}) copy-start(f32[8,2048]{1,0:T(8,128)} %copy-done.25) | copy-start | bytes 196612
  671.0 2.3 copy-start.37
  671.0 3.2 copy-start.57
  (16 other events, 13.2 us)
Sparse Core Ops, SparseCore 0:
  103.1 27.3 all-gather.3
  132.7 45.3 all-gather.5
  558.5 27.6 reduce-scatter.1

commit v4 on v3

--- a/solution.py
+++ b/solution.py
@@ -302,6 +302,7 @@
     tokens,
     qkv,
     masked,
+    lengths,
     small_all,
     gains,
     slot,
@@ -309,6 +310,7 @@
     masked_all,
     to_places,
     to_rows,
+    counts,
     send,
     own_sem,
     small_send,
@@ -494,8 +496,7 @@
     for stage in range(2, stages + 1):
         point(stage)
     scatter()
-    for step in range(1, n_fsdp):
-        column_step(step)
+    column_step(1)
     for i in range(1, n_fsdp):
         block = (me_f + i) % n_fsdp
         small_arrived(me_s * n_fsdp + block).wait_recv()
@@ -524,6 +525,25 @@
             total = total + (pltpu.roll(some, k * owned, 1) if k else some)
         gains[:, j * 128 : (j + 1) * 128] = total
 
+    all_ids = lax.broadcasted_iota(jnp.int32, (counts.shape[1], 1), 0)
+    position = lax.broadcasted_iota(jnp.int32, (1, tokens.shape[0]), 1)
+
+    def seen(device, sums):
+        routes = small_all[device, 8 : 8 + top, :].astype(F32).astype(jnp.int32)
+        match = jnp.zeros(sums.shape, F32)
+        for k in range(top):
+            match = match + (routes[k : k + 1, :] == all_ids).astype(F32)
+        first = (device // n_fsdp) * tokens.shape[0]
+        live = (position + first < lengths[device % n_fsdp]).astype(F32)
+        return sums + match * live
+
+    sums = jnp.zeros((counts.shape[1], tokens.shape[0]), F32)
+    sums = lax.fori_loop(0, n, seen, sums)
+    counts[...] = jnp.broadcast_to(jnp.sum(sums.T, axis=0, keepdims=True), counts.shape)
+
+    for step in range(2, n_fsdp):
+        column_step(step)
+
     def column_sent(i, carry):
         for part in range(3):
             column_copy(i, part).wait_send()
@@ -548,7 +568,19 @@
 
 
 def first_gather(
-    small, tokens, qkv, masked, n_seq, n_fsdp, pieces, split, capacity, top, collective_id
+    small,
+    tokens,
+    qkv,
+    masked,
+    lengths,
+    n_seq,
+    n_fsdp,
+    pieces,
+    split,
+    capacity,
+    top,
+    experts,
+    collective_id,
 ):
     owned = qkv.shape[0]
     rows, width = tokens.shape
@@ -568,9 +600,10 @@
             jax.ShapeDtypeStruct((n_seq, pieces, n_fsdp, capacity, width), BF),
             jax.ShapeDtypeStruct((n_fsdp, places_all, rows), BF),
             jax.ShapeDtypeStruct((n_fsdp, rows, places_all), BF),
+            jax.ShapeDtypeStruct((8, experts), F32),
         ],
-        in_specs=[vmem] * 4,
-        out_specs=[vmem, vmem, any_space, any_space, any_space, vmem, vmem],
+        in_specs=[vmem] * 4 + [pl.BlockSpec(memory_space=pltpu.SMEM)],
+        out_specs=[vmem, vmem, any_space, any_space, any_space, vmem, vmem, vmem],
         scratch_shapes=[
             pltpu.VMEM((n_seq, pieces, capacity, width), BF),
             dma((5,)),
@@ -590,7 +623,7 @@
             collective_id=collective_id, has_side_effects=True, vmem_limit_bytes=40 << 20
         ),
         name="first_gather",
-    )(small, tokens, qkv, masked)
+    )(small, tokens, qkv, masked, lengths)
 
 
 def greet_seq(n_seq):
@@ -884,24 +917,27 @@
     n_fsdp,
     a,
     w,
-    part,
+    normed,
     x,
     mid,
     gains,
     terms_in,
     heads,
+    resid,
+    ready,
     input_out,
     qkv_out,
     total,
+    layer_out,
     *scratch,
 ):
     up, down, done, got, up_send, up_recv, down_send, down_recv, done_send, done_recv = scratch[:10]
-    one, terms, seq_terms, fsdp_terms, seq_send, seq_recv, fsdp_send, fsdp_recv = scratch[10:18]
+    one, part, terms, seq_terms, fsdp_terms, seq_send, seq_recv, fsdp_send, fsdp_recv = scratch[10:19]
     me_s, me_f = lax.axis_index("seq"), lax.axis_index("fsdp")
-    head_width = part.shape[3] // 3
+    head_width = a.shape[2] // 3
     width = n_seq * head_width
     greet_lines(n_seq, n_fsdp)
-    reduce = SeqReduce(n_seq, a, w, 1, *scratch[18:])
+    reduce = SeqReduce(n_seq, a, w, 1, *scratch[19:])
     term_sum = TermSum(
         n_seq,
         n_fsdp,
@@ -928,6 +964,10 @@
             result = scale * weighted - values * (scale * scale * scale * mean)
             input_out[rows, :] = (mid[rows, :] + result).astype(BF)
             terms[0:1, :] += jnp.sum(grad * values * scale, axis=0, keepdims=True)
+            layer = resid[rows, :]
+            for block in range(n_fsdp):
+                layer = layer + ready[block, rows, :].astype(F32)
+            layer_out[rows, :] = layer.astype(BF)
             return carry
 
         lax.fori_loop(0, x.shape[0] // tile, some, 0)
@@ -980,19 +1020,29 @@
     lag = 2
     slots = n_seq * (n_fsdp - 1) + lag * (n_fsdp - 1)
 
+    owned = part.shape[2]
+    stripe = n_fsdp * owned
+
+    def make(s):
+        lanes = pl.ds(pl.multiple_of(s * stripe, 128), stripe)
+        every = a[...].reshape(-1, a.shape[2])
+        product = dot(normed[:, lanes], every, 0, 0).astype(BF)
+        for block in range(n_fsdp):
+            part[s, block] = product[block * owned : (block + 1) * owned]
+        done[s] = part[s, me_f]
+
     def run(first, last):
         def slot(number, carry):
+            @pl.when(number < n_seq)
+            def _():
+                make((me_s + number) % n_seq)
+
             stream(0, number - lag * me_f)
             stream(1, number - lag * (n_fsdp - 1 - me_f))
             return carry
 
         lax.fori_loop(first, last, slot, 0)
 
-    def begin(i, carry):
-        done[i] = part[i, me_f]
-        return carry
-
-    lax.fori_loop(0, n_seq, begin, 0)
     reached = 0
     for number, event in enumerate(
         reduce.events(one)
@@ -1042,9 +1092,12 @@
     total[...] = term_sum.finish()
 
 
-def last_reduce(a, w, part, x, mid, gains, terms, heads, n_seq, n_fsdp, collective_id):
+def last_reduce(
+    a, w, normed, x, mid, gains, terms, heads, resid, ready, n_seq, n_fsdp, collective_id
+):
     rows, width = a.shape[0] // n_seq, w.shape[0]
-    owned, columns = part.shape[2:]
+    columns = a.shape[1]
+    owned = width // (n_seq * n_fsdp)
     vmem = pl.BlockSpec(memory_space=pltpu.VMEM)
     dma = pltpu.SemaphoreType.DMA
     return pl.pallas_call(
@@ -1053,9 +1106,10 @@
             jax.ShapeDtypeStruct((rows, width), BF),
             jax.ShapeDtypeStruct((owned, n_seq * columns), F32),
             jax.ShapeDtypeStruct(heads.shape, F32),
+            jax.ShapeDtypeStruct((rows, width), BF),
         ],
-        in_specs=[vmem] * 8,
-        out_specs=[vmem] * 3,
+        in_specs=[vmem] * 10,
+        out_specs=[vmem] * 4,
         scratch_shapes=[
             pltpu.VMEM((n_fsdp, n_seq, owned, columns), BF),
             pltpu.VMEM((n_fsdp, n_seq, owned, columns), BF),
@@ -1068,16 +1122,17 @@
             dma((n_seq,)),
             dma((n_seq,)),
             pltpu.VMEM((rows, width), F32),
+            pltpu.VMEM((n_seq, n_fsdp, owned, columns), BF),
             pltpu.VMEM(terms.shape, F32),
         ]
         + term_scratch(n_seq, n_fsdp, heads.shape)
         + reduce_scratch(n_seq, rows, width),
         compiler_params=pltpu.CompilerParams(
-            collective_id=collective_id, has_side_effects=True, vmem_limit_bytes=50 << 20
+            collective_id=collective_id, has_side_effects=True, vmem_limit_bytes=60 << 20
         ),
         cost_estimate=pl.CostEstimate(flops=0, bytes_accessed=1 << 27, transcendentals=0),
         name="last_reduce",
-    )(a.reshape(n_seq, rows, -1), w, part, x, mid, gains, terms, heads)
+    )(a.reshape(n_seq, rows, -1), w, normed, x, mid, gains, terms, heads, resid, ready)
 
 
 def chunked(total, size, body):
@@ -1330,32 +1385,46 @@
     )(x, hot, gates, masked, before, w_up, w_down)
 
 
-def return_kernel(n_seq, n_fsdp, pieces, hot, gates, *refs):
-    rows = refs[:pieces]
-    out, gates_out, got, parts, sums, own_sem, row_send, row_recv, part_send, part_recv = refs[
-        pieces : pieces + 10
-    ]
-    gate_exchange = Exchange(n_seq, n_fsdp, gates, gates_out, refs[pieces + 10 :])
+def return_kernel(n_seq, n_fsdp, pieces, hot, gates, ready, w_up, *refs):
+    grads = refs[:pieces]
+    out, gates_out, ready_sums = refs[pieces : pieces + 3]
+    rest = refs[pieces + 3 :]
+    weights, hidden, rows, got, parts, sums, some_ready = rest[:7]
+    w_sem, h_sem, ready_sem, own_sem, row_send, row_recv, part_send, part_recv = rest[7:15]
+    gate_exchange = Exchange(n_seq, n_fsdp, gates, gates_out, rest[15:])
     me_s, me_f = lax.axis_index("seq"), lax.axis_index("fsdp")
     width = out.shape[1]
-    capacity = rows[0].shape[2]
-    greet_all(n_seq, n_fsdp)
-
-    def row_copy(j, i, piece):
-        other, block = (me_s + i) % n_seq, (me_f + j) % n_fsdp
+    capacity = rows.shape[3]
+    ff = hidden.shape[5]
+    tile = min(256, width)
+    chunks = width // tile
+
+    def weight_copy(piece, chunk):
+        lines = pl.ds(pl.multiple_of(chunk * tile, tile), tile)
+        return pltpu.make_async_copy(
+            w_up.at[piece, lines], weights.at[piece, lines], w_sem.at[piece, chunk]
+        )
+
+    def hidden_copy(piece):
+        return pltpu.make_async_copy(grads[piece], hidden.at[piece], h_sem.at[piece])
+
+    def ready_copy(block):
+        return pltpu.make_async_copy(
+            ready.at[:, :, block], some_ready.at[block % 2], ready_sem.at[block % 2]
+        )
+
+    def row_copy(block, i, place):
+        other = (me_s + i) % n_seq
         return remote(
-            rows[piece].at[other, block],
-            got.at[block, me_s, piece],
-            row_send.at[j % n_fsdp, i, piece],
-            row_recv.at[block, me_s, piece],
+            rows.at[block, other],
+            got.at[block, place],
+            row_send.at[block, i],
+            row_recv.at[block, place],
             (other, me_f),
         )
 
-    def own_copy(j, piece):
-        block = (me_f + j) % n_fsdp
-        return pltpu.make_async_copy(
-            rows[piece].at[me_s, block], got.at[block, me_s, piece], own_sem.at[j % n_fsdp, piece]
-        )
+    def own_copy(block):
+        return pltpu.make_async_copy(rows.at[block, me_s], got.at[block, me_s], own_sem.at[block])
 
     def part_copy(j):
         block = (me_f + j) % n_fsdp
@@ -1363,25 +1432,46 @@
             parts.at[block], sums.at[me_f], part_send.at[j], part_recv.at[me_f], (me_s, block)
         )
 
-    for j in range(1, n_fsdp + 1):
-        for piece in range(pieces):
-            for i in range(1, n_seq):
-                row_copy(j, i, piece).start()
-            own_copy(j, piece).start()
+    for piece in range(pieces):
+        hidden_copy(piece).start()
+
+        def begin(chunk, carry):
+            weight_copy(piece, chunk).start()
+            return carry
+
+        lax.fori_loop(0, chunks, begin, 0)
+    for block in range(min(2, n_fsdp)):
+        ready_copy(block).start()
+    greet_all(n_seq, n_fsdp)
     gate_exchange.start()
-    for j in range(1, n_fsdp + 1):
+
+    def compute(j):
         block = (me_f + j) % n_fsdp
         for piece in range(pieces):
-            own_copy(j, piece).wait()
-            for i in range(1, n_seq):
-                source = (me_s + i) % n_seq
-                remote(
-                    rows[piece].at[source, block],
-                    got.at[block, source, piece],
-                    row_send.at[0, i, piece],
-                    row_recv.at[block, source, piece],
-                    (source, me_f),
-                ).wait_recv()
+            if j == 1:
+                hidden_copy(piece).wait()
+            gate_grad = hidden[piece, 0, :, block].reshape(-1, ff)
+            up_grad = hidden[piece, 1, :, block].reshape(-1, ff)
+
+            def some(chunk, carry):
+                if j == 1:
+                    weight_copy(piece, chunk).wait()
+                lines = pl.ds(pl.multiple_of(chunk * tile, tile), tile)
+                total = dot(gate_grad, weights[piece, lines, :ff], 1, 1)
+                total = total + dot(up_grad, weights[piece, lines, ff:], 1, 1)
+                rows[block, :, piece, :, lines] = total.astype(BF).reshape(n_seq, capacity, -1)
+                return carry
+
+            lax.fori_loop(0, chunks, some, 0)
+        for i in range(1, n_seq):
+            row_copy(block, i, me_s).start()
+        own_copy(block).start()
+
+    def finish(j):
+        block = (me_f + j) % n_fsdp
+        own_copy(block).wait()
+        for i in range(1, n_seq):
+            row_copy(block, i, (me_s + i) % n_seq).wait_recv()
 
         def some(columns):
             arrived = got[block, :, :, :, columns].reshape(n_seq * pieces * capacity, -1)
@@ -1394,6 +1484,27 @@
         chunked(width, 512, some)
         if j < n_fsdp:
             part_copy(j).start()
+
+    def sum_ready(block):
+        ready_copy(block).wait()
+
+        def some(columns):
+            arrived = some_ready[block % 2, :, :, :, columns]
+            arrived = arrived.reshape(n_seq * pieces * capacity, -1)
+            ready_sums[block, :, columns] = dot(hot[block], arrived, 1, 0).astype(BF)
+
+        chunked(width, 512, some)
+        if block + 2 < n_fsdp:
+            ready_copy(block + 2).start()
+
+    for j in range(1, n_fsdp + 1):
+        compute(j)
+        if j >= 3:
+            finish(j - 2)
+    for block in range(n_fsdp):
+        sum_ready(block)
+    for j in range(max(1, n_fsdp - 1), n_fsdp + 1):
+        finish(j)
     for j in range(1, n_fsdp):
         source = (me_f + n_fsdp - j) % n_fsdp
         remote(
@@ -1409,43 +1520,52 @@
     chunked(width, 512, add)
     for j in range(1, n_fsdp):
         part_copy(j).wait_send()
-    for j in range(1, n_fsdp + 1):
-        for piece in range(pieces):
-            for i in range(1, n_seq):
-                row_copy(j, i, piece).wait_send()
+    for block in range(n_fsdp):
+        for i in range(1, n_seq):
+            row_copy(block, i, me_s).wait_send()
     gate_exchange.finish()
 
 
-def return_rows(piece_rows, hot, gates, n_seq, n_fsdp, collective_id):
-    pieces = len(piece_rows)
-    capacity, width = piece_rows[0].shape[2:]
+def return_rows(grads, w_up, hot, gates, ready, n_seq, n_fsdp, collective_id):
+    pieces, width = w_up.shape[:2]
+    ff = w_up.shape[2] // 2
     count = hot.shape[1]
+    capacity = ready.shape[3]
     vmem = pl.BlockSpec(memory_space=pltpu.VMEM)
+    any_space = pl.BlockSpec(memory_space=pl.ANY)
     dma = pltpu.SemaphoreType.DMA
     return pl.pallas_call(
         functools.partial(return_kernel, n_seq, n_fsdp, pieces),
         out_shape=[
             jax.ShapeDtypeStruct((count, width), F32),
             jax.ShapeDtypeStruct(gates.shape, F32),
+            jax.ShapeDtypeStruct((n_fsdp, count, width), BF),
         ],
-        in_specs=[vmem, vmem] + [pl.BlockSpec(memory_space=pl.ANY)] * pieces,
-        out_specs=[vmem, vmem],
+        in_specs=[vmem, vmem, any_space, any_space] + [any_space] * pieces,
+        out_specs=[vmem] * 3,
         scratch_shapes=[
+            pltpu.VMEM(w_up.shape, BF),
+            pltpu.VMEM((pieces, 2, n_seq, n_fsdp, capacity, ff), BF),
+            pltpu.VMEM((n_fsdp, n_seq, pieces, capacity, width), BF),
             pltpu.VMEM((n_fsdp, n_seq, pieces, capacity, width), BF),
             pltpu.VMEM((n_fsdp, count, width), BF),
             pltpu.VMEM((n_fsdp, count, width), BF),
-            dma((n_fsdp, pieces)),
-            dma((n_fsdp, n_seq, pieces)),
-            dma((n_fsdp, n_seq, pieces)),
+            pltpu.VMEM((2, n_seq, pieces, capacity, width), BF),
+            dma((pieces, width // min(256, width))),
+            dma((pieces,)),
+            dma((2,)),
+            dma((n_fsdp,)),
+            dma((n_fsdp, n_seq)),
+            dma((n_fsdp, n_seq)),
             dma((n_fsdp,)),
             dma((n_fsdp,)),
         ]
         + exchange_sems(n_seq * n_fsdp),
         compiler_params=pltpu.CompilerParams(
-            collective_id=collective_id, has_side_effects=True, vmem_limit_bytes=40 << 20
+            collective_id=collective_id, has_side_effects=True, vmem_limit_bytes=60 << 20
         ),
         name="return_rows",
-    )(hot, gates, *piece_rows)
+    )(hot, gates, ready, w_up, *grads)
 
 
 def weight_grad_kernel(a, b, *refs):
@@ -1545,32 +1665,6 @@
         ),
         name="expert_backward",
     )(masked, gates, piece_out, hidden, w_down)
-
-
-def expert_input_kernel(grad, w_up, out):
-    ff = grad.shape[2]
-    total = dot(grad[0], w_up[0, :, :ff], 1, 1) + dot(grad[1], w_up[0, :, ff:], 1, 1)
-    out[...] = total.astype(BF)
-
-
-def expert_input(grad, w_up, piece):
-    rows, ff = grad.shape[1:]
-    width = w_up.shape[1]
-    tile = min(256, width)
-    return pl.pallas_call(
-        expert_input_kernel,
-        out_shape=jax.ShapeDtypeStruct((rows, width), BF),
-        grid=(width // tile,),
-        in_specs=[
-            pl.BlockSpec((2, rows, ff), lambda i: (0, 0, 0)),
-            pl.BlockSpec((1, tile, 2 * ff), lambda i: (piece, i, 0)),
-        ],
-        out_specs=pl.BlockSpec((rows, tile), lambda i: (0, i)),
-        cost_estimate=pl.CostEstimate(
-            flops=4 * rows * width * ff, bytes_accessed=4 * width * ff, transcendentals=0
-        ),
-        name="expert_input",
-    )(grad, w_up)
 
 
 class SeqShare:
@@ -1995,25 +2089,25 @@
             rows_of(router_weight.reshape(-1), 16),
         ]
     )
-    small, gains, slot_tokens, qkv_local, cot_all, to_places, to_rows = first_gather(
+    small, gains, slot_tokens, qkv_local, cot_all, to_places, to_rows, counts = first_gather(
         own_small,
         tokens[0],
         qkv_weight,
         masked_low,
+        lengths,
         n_seq,
         n_fsdp,
         pieces_dev,
         split,
         capacity,
         top_count,
+        experts,
         collective_id=0,
     )
     slot_tokens = slot_tokens.reshape(slot_len, width)
     qkv_local = qkv_local.reshape(width, 3 * head_width)
     router = small[:, 8 + top_count :].reshape(n_dev, -1)[:, : owned * experts]
     router = router.reshape(width, experts)
-    all_routes = small[:, 8 : 8 + top_count].swapaxes(1, 2)
-    all_routes = all_routes.reshape(n_seq, n_fsdp, shard_len, top_count).astype(jnp.int32)
     proj_later = lax.optimization_barrier((proj_weight, slot_tokens))[0]
     proj_rows = lax.all_gather(proj_later, "fsdp", axis=0, tiled=True)
 
@@ -2024,14 +2118,6 @@
 
     masked_later = lax.optimization_barrier((masked_low, raw))[0]
     plane_masked = lax.all_gather(masked_later, "fsdp", axis=0)
-
-    def combine(pieces_back):
-        total = 0.0
-        for piece in range(pieces_dev):
-            back = pieces_back[:, piece]
-            hot = to_rows.reshape(n_fsdp, shard_len, n_seq, pieces_dev, capacity)[:, :, :, piece]
-            total = total + jnp.einsum("ftsc,sfcd->ftd", hot, back, preferred_element_type=F32)
-        return total.astype(BF)
 
     def rms(values):
         return lax.rsqrt(jnp.mean(values * values, axis=-1, keepdims=True) + epsilon)
@@ -2076,7 +2162,7 @@
             cot_all, gate_columns[piece], piece_out, hidden, expert_down, piece
         )
         gate_backs.append(gate_back[0].reshape(n_dev, capacity))
-        backs.append(expert_input(hidden_grad, expert_up, piece))
+        backs.append(hidden_grad.reshape(2, n_seq, n_fsdp, capacity, piece_ff))
         down_grad = weight_grad(activation, out_grad[None], down_grad, piece, pieces_dev)
         up_grad = weight_grad(rows, hidden_grad, up_grad, piece, pieces_dev)
     back_send = jnp.stack(gate_backs, axis=1).reshape(n_dev, pieces_dev * capacity)
@@ -2085,18 +2171,14 @@
     backs, outs_back, up_grad, down_grad = lax.optimization_barrier(
         (backs, outs_back, up_grad, down_grad)
     )
-    backs = [rows.reshape(n_seq, n_fsdp, capacity, width) for rows in backs]
-    normed_two_grad, back_recv = return_rows(
-        backs, to_rows, back_send, n_seq, n_fsdp, collective_id=7
+    backs, outs_back, up_grad, down_grad = lax.optimization_barrier(
+        (backs, outs_back, up_grad, down_grad)
     )
-    outs_back = lax.optimization_barrier((outs_back, normed_two_grad))[0]
-    outs_sums = combine(outs_back)
-
-    seen = (all_routes[..., None] == jnp.arange(experts, dtype=jnp.int32)).astype(BF)
-    live = jnp.arange(slot_len, dtype=jnp.int32).reshape(n_seq, 1, shard_len) < lengths[None, :, None]
-    live = jnp.broadcast_to(live[..., None], all_routes.shape).astype(BF)
-    counts = dot(live.reshape(1, -1), seen.reshape(-1, experts), 1, 0)[0]
-    fraction = counts / (top_count * valid_total)
+    normed_two_grad, back_recv, outs_sums = return_rows(
+        backs, expert_up, to_rows, back_send, outs_back, n_seq, n_fsdp, collective_id=7
+    )
+
+    fraction = counts[0] / (top_count * valid_total)
     back_recv = back_recv.reshape(n_dev, -1)
     slot_gates_grad = back_recv[:, : pieces_dev * capacity].reshape(experts, split, capacity).sum(axis=1)
     probs_grad = (
@@ -2123,10 +2205,9 @@
     mid_part, gain_three = rms_back(resid_mid, mid_rms, gains[3], normed_two_grad)
     mid_grad = masked_low.astype(F32) + mid_part
     branch_grad = mid_grad.astype(BF)
-    branch_later, outs_sums = lax.optimization_barrier((branch_grad, outs_sums))
     outs_parts = lax.all_to_all(outs_sums, "fsdp", split_axis=0, concat_axis=0, tiled=True)
     slot_branch, router_parts = gather_seq(
-        branch_later, router_term, n_seq, n_fsdp, collective_id=9
+        branch_grad, router_term, n_seq, n_fsdp, collective_id=9
     )
     slot_branch = slot_branch.reshape(slot_len, width)
     heads_grad = dot(slot_branch, proj_rows, 1, 1).astype(BF)
@@ -2159,28 +2240,28 @@
         collective_id=4,
     )
     raw_grad, outs_parts = lax.optimization_barrier((raw_grad, outs_parts))
-    layer_out = (resid_mid + jnp.sum(outs_parts.astype(F32), axis=0)).astype(BF)[None]
-
-    qkv_part = dot(normed_one, raw_grad, 0, 0).astype(BF)
-    qkv_part = qkv_part.reshape(n_seq, n_fsdp, owned, 3 * head_width)
+
     prob_part = jnp.sum(router_probs * row_valid[:, None], axis=0)
     prob_row = jnp.tile(jnp.pad(prob_part, (0, head_width - experts)), n_seq)
     terms = jnp.pad(jnp.stack([gain_three, prob_row]), ((1, 5), (0, 0)))
     heads_terms = jnp.pad(heads_gain[:2], ((3, 3), (0, 0)))
-    input_grad, qkv_grad, last = last_reduce(
+    input_grad, qkv_grad, last, layer_out = last_reduce(
         raw_grad,
         qkv_local,
-        qkv_part,
+        normed_one,
         tokens[0],
         mid_grad,
         gains,
         terms,
         heads_terms,
+        resid_mid,
+        outs_parts,
         n_seq,
         n_fsdp,
         collective_id=10,
     )
     input_grad = input_grad[None]
+    layer_out = layer_out[None]
 
     proj_part = dot(attended, slot_branch, 0, 0).astype(BF)
     proj_grad = lax.psum_scatter(proj_part, "fsdp", scatter_dimension=0, tiled=True).astype(F32)

time: 697 us -> 664 us (0.953)
  matrix products: 26.2 us -> 13.9 us
  Pallas kernels: 565 us -> 555 us
    pallas_call x2 -> x0, Pallas kernels: 24.8 us -> none  [expert_input(): pl.pallas_call(expert_input_kernel, out_shape=jax.ShapeDtypeStruct((rows,...]
    dot_general x5 -> x3, matrix products: 19 us -> 9.11 us  [dot(): lax.dot_general(a, b, (((ca,), (cb,)), ((), ())), preferred_element_type=...]
    pallas_call x1, Pallas kernels: 79.1 us -> 87.5 us  [return_rows(): pl.pallas_call(functools.partial(return_kernel, n_seq, n_fsdp, pieces), o...]
    unnamed x124 -> x81, local copies, waits for them, and re-layouts: 31.8 us -> 31.6 us
  transfers between devices with their start and end apart: 5 -> 5, of which waited for: 0 -> 1; matrix products, arithmetic and copies ran while one was open for 5% -> 4% of each run, Pallas kernels for 31% -> 29%
where the time goes in v4:
time: 664 us; the launch traced here: 654 us
  Pallas kernels  555 us (84%)
  local copies, waits for them, and re-layouts  41.5 us (6%)
  between operations  17.1 us (3%)
  other arithmetic  14.9 us (2%)
  matrix products  13.9 us (2%)
  starting transfers between devices  9.66 us (1%)
    pallas_call x1, Pallas kernels, dispatch_rows(): pl.pallas_call(functools.partial(dispatch_kernel, n_seq, n_fsdp, pieces),...  130 us
    pallas_call x1, Pallas kernels, return_rows(): pl.pallas_call(functools.partial(return_kernel, n_seq, n_fsdp, pieces), o...  87.5 us
    pallas_call x1, Pallas kernels, first_gather(): pl.pallas_call(functools.partial(first_kernel, n_seq, n_fsdp, pieces, spl...  81.4 us
    pallas_call x1, Pallas kernels, last_reduce(): pl.pallas_call(functools.partial(last_kernel, n_seq, n_fsdp), out_shape=[...  69 us
    pallas_call x4, Pallas kernels, weight_grad(): pl.pallas_call(weight_grad_kernel, out_shape=jax.ShapeDtypeStruct((pieces...  41.4 us
    pallas_call x1, Pallas kernels, gather_seq(): pl.pallas_call(functools.partial(gather_kernel, n_seq, n_fsdp), out_shape...  35 us
    unnamed x81, local copies, waits for them, and re-layouts  31.6 us
    pallas_call x1, Pallas kernels, product_reduced(): pl.pallas_call(functools.partial(reduce_kernel, n_seq, w_dim), out_shape=...  29.9 us
  transfers between devices with their start and end apart: 5, of which 1 were waited for; matrix products, arithmetic and copies ran while one was open for 4% of the time, Pallas kernels for 29%

profile of v4, /device:TPU:0, one launch (start us, length us, event | category | flops | bytes accessed | tf_op | source)
XLA Modules:
  0.0 653.9 jit_solution(14672330387025671023)
XLA Ops:
  8.7 1.2 dynamic_slice.12.length
  10.6 1.9 bitcast_select_fusion.masked
  13.2 1.0 copy-done.5
  14.3 1.0 copy-done.7
  15.3 1.1 copy-done.15
  17.1 81.4 %first_gather.1 = (bf16[32,48,128]{2,1,0:T(8,128)(2,1)S(1)}, f32[8,2048]{1,0:T(8,128)S(1)}, bf16[8,128,2048]{2,1,0:T(8,128)(2,1)S(1)}, bf16[8,4,64,768]{3,2,1,0:...) custom-call(bf16[48,128]{1,0:T(8,128)(2,1)S(1)} %fusion.15.small, ...), custom_call_target="tpu_custom_call" | custom-call | tf_op jit(solution)/shard_map/first_gather/pallas_call | solution.py:593
  98.6 2.0 copy-done.9
  102.9 17.8 %front.1 = (bf16[1024,2048]{1,0:T(8,128)(2,1)S(1)}, f32[1024,768]{1,0:T(8,128)S(1)}, f32[8,1024]{1,0:T(8,128)S(1)}) custom-call(bf16[1024,2048]{1,0:T(8,128)(2,1)} %bitcast.62, f32[8,2048]{1,0:T(8,128)S(1)} %get-tuple-element.67.gain.gains, bf16[2048,768]{1,0:T(8,128)(2,1)S(1)} %bitcast.58), custom_call_target="tpu_custom_call" | custom-call | tf_op jit(solution)/shard_map/front/pallas_call | solution.py:1742
  120.7 1.7 copy-done
  122.4 1.9 copy-done.8
  126.0 1.1 reshape_reshape.3
  127.6 1.9 fusion.2
  129.5 1.3 pad_maximum_fusion
  130.9 10.9 %attend.1 = (bf16[1024,256]{1,0:T(8,128)(2,1)}, bf16[1024,256]{1,0:T(8,128)(2,1)}, bf16[1024,256]{1,0:T(8,128)(2,1)}, bf16[1024,256]{1,0:T(8,128)(2,1)}) custom-call(s32[1]{0:T(128)} %dynamic_slice.12.length, f32[1024,768]{1,0:T(8,128)} %copy-done, f32[1024,768]{1,0:T(8,128)} %copy-done, f32[1024,768]{1,0:T(8,128)} %copy-done, f32[8,1024]{1,0:T(8,128)} %copy-done.22, ...), custom_call_target="tpu_custom_call" | custom-call | flops 1073741824 | bytes 8388608 | tf_op jit(solution)/shard_map/attend/pallas_call | solution.py:1816
  142.1 1.2 copy-done.11
  144.4 29.9 %product_reduced.1 = f32[128,2048]{1,0:T(8,128)S(1)} custom-call(bf16[8,128,256]{2,1,0:T(8,128)(2,1)S(1)} %bitcast.64, bf16[256,2048]{1,0:T(8,128)(2,1)S(1)} %copy-done.11), custom_call_target="tpu_custom_call" | custom-call | tf_op jit(solution)/shard_map/product_reduced/pallas_call | solution.py:902
  176.0 2.0 all-gather.6.cloned.1.call-done
  178.1 130.0 %dispatch_rows.1 = (bf16[8,2,4,24,2048]{4,3,2,1,0:T(8,128)(2,1)}, f32[2,768,1]{2,1,0:T(8,128)}, bf16[8,2,4,24,2048]{4,3,2,1,0:T(8,128)(2,1)}, bf16[8,4,24,2048]{...) custom-call(bf16[128,2048]{1,0:T(8,128)(2,1)} %copy-done.31, ...), custom_call_target="tpu_custom_call", output_to_operand_aliasing={{0}: (4, {})} | custom-call | tf_op jit(solution)/shard_map/dispatch_rows/pallas_call | solution.py:1352
  308.1 4.9 all-to-all-start
  314.4 1.2 slice_bitcast_fusion.1
  315.5 12.3 %expert_backward.3 = (bf16[2,768,1024]{2,1,0:T(8,128)(2,1)S(1)}, bf16[768,2048]{1,0:T(8,128)(2,1)}, f32[8,768]{1,0:T(8,128)S(1)}) custom-call(bf16[8,2,4,24,2048]{4,3,2,1,0:T(8,128)(2,1)} %get-tuple-element.81.masked, f32[768,1]{1,0:T(8,128)S(1)} %get-tuple-element.163.gates, bf16[768,2048]{1,0:T(8,128)(2,1)} %get-tuple-element.86.piece_out, ...), custom_call_target="tpu_custom_call" | custom-call | flops 3221225472 | bytes 9437184 | tf_op jit(solution)/shard_map/expert_backward/pallas_call | solution.py:1641
  327.8 1.7 copy-done.2
  329.6 12.3 %expert_backward.2 = (bf16[2,768,1024]{2,1,0:T(8,128)(2,1)S(1)}, bf16[768,2048]{1,0:T(8,128)(2,1)}, f32[8,768]{1,0:T(8,128)S(1)}) custom-call(bf16[8,2,4,24,2048]{4,3,2,1,0:T(8,128)(2,1)} %get-tuple-element.81.masked, f32[768,1]{1,0:T(8,128)S(1)} %get-tuple-element.162.gates, bf16[768,2048]{1,0:T(8,128)(2,1)} %get-tuple-element.83.piece_out, ...), custom_call_target="tpu_custom_call" | custom-call | flops 3221225472 | bytes 9437184 | tf_op jit(solution)/shard_map/expert_backward/pallas_call | solution.py:1641
  342.0 1.7 copy-done.3
  344.8 8.0 %weight_grad.6.refs_0_ = f32[2,1024,2048]{2,1,0:T(8,128)} custom-call(bf16[768,1024]{1,0:T(8,128)(2,1)} %get-tuple-element.96.a, bf16[1,768,2048]{2,1,0:T(8,128)(2,1)} %bitcast.68), custom_call_target="tpu_custom_call" | custom-call | flops 3221225472 | bytes 8388608 | tf_op jit(solution)/shard_map/weight_grad/pallas_call | solution.py:1582
  352.8 8.0 %weight_grad.7 = f32[2,1024,2048]{2,1,0:T(8,128)} custom-call(bf16[768,1024]{1,0:T(8,128)(2,1)} %get-tuple-element.94.a, bf16[1,768,2048]{2,1,0:T(8,128)(2,1)} %bitcast.67, f32[2,1024,2048]{2,1,0:T(8,128)} %weight_grad.6.refs_0_), custom_call_target="tpu_custom_call", output_to_operand_aliasing={{}: (2, {})} | custom-call | flops 3221225472 | bytes 8388608 | tf_op jit(solution)/shard_map/weight_grad/pallas_call | solution.py:1582
  360.8 12.7 %weight_grad.4.refs_0_ = f32[2,2048,2048]{2,1,0:T(8,128)} custom-call(bf16[768,2048]{1,0:T(8,128)(2,1)} %bitcast.66, bf16[2,768,1024]{2,1,0:T(8,128)(2,1)} %copy-done.3), custom_call_target="tpu_custom_call" | custom-call | flops 6442450944 | bytes 16777216 | tf_op jit(solution)/shard_map/weight_grad/pallas_call | solution.py:1582
  373.5 12.7 %weight_grad.5 = f32[2,2048,2048]{2,1,0:T(8,128)} custom-call(bf16[768,2048]{1,0:T(8,128)(2,1)} %bitcast.65, bf16[2,768,1024]{2,1,0:T(8,128)(2,1)} %copy-done.2, f32[2,2048,2048]{2,1,0:T(8,128)} %weight_grad.4.refs_0_), custom_call_target="tpu_custom_call", output_to_operand_aliasing={{}: (2, {})} | custom-call | flops 6442450944 | bytes 16777216 | tf_op jit(solution)/shard_map/weight_grad/pallas_call | solution.py:1582
  386.1 87.5 %return_rows.1 = (f32[128,2048]{1,0:T(8,128)}, f32[32,8,128]{2,1,0:T(8,128)}, bf16[4,128,2048]{2,1,0:T(8,128)(2,1)}) custom-call(bf16[4,128,384]{2,1,0:T(8,128)(2,1)} %copy-done.19, f32[32,8,128]{2,1,0:T(8,128)} %copy.36.gates, bf16[8,2,4,24,2048]{4,3,2,1,0:T(8,128)(2,1)} %all-to-all-done.ready, bf16[2,2048,2048]{2,1,0:T(8,128)(2,1)} %w_up.3, ...), custom_call_target="tpu_custom_call" | custom-call | tf_op jit(solution)/shard_map/return_rows/pallas_call | solution.py:1537
  475.2 1.2 fusion.16.terms
  476.4 3.2 multiply_reduce_fusion
  479.6 4.6 all-to-all-start.1
  484.3 1.5 fusion.19
  485.8 35.0 %gather_seq.1 = (bf16[8,128,2048]{2,1,0:T(8,128)(2,1)}, f32[64,256]{1,0:T(8,128)}) custom-call(bf16[128,2048]{1,0:T(8,128)(2,1)} %get-tuple-element.154.x, f32[64,2048]{1,0:T(8,128)} %fusion.16.terms), custom_call_target="tpu_custom_call" | custom-call | bytes 67108864 | tf_op jit(solution)/shard_map/gather_seq/pallas_call | solution.py:752
  520.9 4.6 convolution_convert_fusion
  525.6 4.3 convolution_convert_fusion.1.g_ref
  529.9 17.3 %attend_back.1 = (f32[1024,256]{1,0:T(8,128)}, f32[1024,256]{1,0:T(8,128)}, bf16[1024,256]{1,0:T(8,128)(2,1)}, f32[8,1024]{1,0:T(8,128)}, f32[8,256]{1,0:T(8,128)}) custom-call(s32[1]{0:T(128)} %dynamic_slice.12.length, bf16[1024,256]{1,0:T(8,128)(2,1)} %get-tuple-element.71.q_ref, bf16[1024,256]{1,0:T(8,128)(2,1)} %get-tuple-element.72.k_ref, ...), custom_call_target="tpu_custom_call" | custom-call | flops 5368709120 | bytes 16777216 | tf_op jit(solution)/shard_map/attend_back/pallas_call | solution.py:1919
  548.5 1.2 copy-done.13
  549.7 1.2 copy-done.14
  551.0 1.0 copy-done.18
  552.8 9.9 %raw_back.1 = (bf16[1024,768]{1,0:T(8,128)(2,1)S(1)}, f32[64,256]{1,0:T(8,128)S(1)}) custom-call(f32[1024,256]{1,0:T(8,128)S(1)} %copy-done.13, f32[1024,256]{1,0:T(8,128)S(1)} %copy-done.14, bf16[1024,256]{1,0:T(8,128)(2,1)S(1)} %copy-done.18, f32[1024,768]{1,0:T(8,128)S(1)} %copy-done.1, f32[8,1024]{1,0:T(8,128)S(1)} %copy-done.23, ...), custom_call_target="tpu_custom_call" | custom-call | tf_op jit(solution)/shard_map/raw_back/pallas_call | solution.py:2009
  562.7 1.1 copy-done.10
  565.3 1.8 convert_element_type.87
  567.0 69.0 %last_reduce.1 = (bf16[128,2048]{1,0:T(8,128)(2,1)}, f32[64,6144]{1,0:T(8,128)}, f32[8,256]{1,0:T(8,128)}, bf16[128,2048]{1,0:T(8,128)(2,1)}) custom-call(bf16[8,128,768]{2,1,0:T(8,128)(2,1)} %bitcast.63, bf16[2048,768]{1,0:T(8,128)(2,1)} %bitcast.59, bf16[1024,2048]{1,0:T(8,128)(2,1)} %copy-done.8, bf16[128,2048]{1,0:T(8,128)(2,1)} %bitcast.60, ...), custom_call_target="tpu_custom_call" | custom-call | bytes 134217728 | tf_op jit(solution)/shard_map/last_reduce/pallas_call | solution.py:1103
  636.8 1.3 divide_reduce_fusion
  639.3 1.9 copy.47
  641.2 1.9 copy.48
  643.1 2.7 copy.49
  (119 shorter events, 19.4 us)
Async XLA Ops:
  7.2 134.9 %all-gather.4.cloned.1.call-start = ((), (), s32[]{:S(2)}) async-start(), calls=%async_computation.3 | async-start | bytes 1310720 | tf_op jit(solution)/shard_map/all_gather | solution.py:2112
  13.2 1.0 copy-start.5
  14.3 1.0 copy-start.7
  15.3 1.1 copy-start.15
  16.5 0.7 copy-start.28
  98.6 2.0 copy-start.9
  100.6 0.8 copy-start.19
  101.3 0.7 copy-start.20
  102.1 0.7 copy-start.24
  102.8 23.1 %copy-start.4 = (bf16[8,4,64,768]{3,2,1,0:T(8,128)(2,1)}, bf16[8,4,64,768]{3,2,1,0:T(8,128)(2,1)S(1)}, u32[]{:S(2)}) copy-start(bf16[8,4,64,768]{3,2,1,0:T(8,128)(2,1)S(1)} %get-tuple-element.68) | copy-start | bytes 9437188
  102.8 24.2 %copy-start.21 = (f32[8,2048]{1,0:T(8,128)}, f32[8,2048]{1,0:T(8,128)S(1)}, u32[]{:S(2)}) copy-start(f32[8,2048]{1,0:T(8,128)S(1)} %get-tuple-element.67.gain.gains) | copy-start | bytes 196612
  102.9 75.2 %all-gather.6.cloned.1.call-start = ((), (), s32[]{:S(2)}) async-start(), calls=%async_computation.5 | async-start | bytes 2621440 | tf_op jit(solution)/shard_map/all_gather | solution.py:2120
  120.7 1.7 copy-start
  122.4 1.9 copy-start.8
  124.3 0.6 copy-start.22
  130.9 11.0 %copy-start.36 = (s32[1,128,8]{1,2,0:T(8,128)S(1)}, s32[1,128,8]{1,2,0:T(8,128)}, u32[]{:S(2)}) copy-start(s32[1,128,8]{1,2,0:T(8,128)} %param.13) | copy-start | bytes 12292
  130.9 43.4 %copy-start.6 = (bf16[1,128,2048]{2,1,0:T(8,128)(2,1)S(1)}, bf16[1,128,2048]{2,1,0:T(8,128)(2,1)}, u32[]{:S(2)}) copy-start(bf16[1,128,2048]{2,1,0:T(8,128)(2,1)} %param.10) | copy-start | bytes 1572868
  130.9 43.8 %copy-start.33 = (bf16[2048,64]{1,0:T(8,128)(2,1)S(1)}, bf16[2048,64]{1,0:T(8,128)(2,1)}, u32[]{:S(2)}) copy-start(bf16[2048,64]{1,0:T(8,128)(2,1)} %reshape_reshape.3) | copy-start | bytes 786436
  142.1 1.2 copy-start.11
  143.3 1.0 copy-start.16
  174.5 309.8 %copy-start.30 = (f32[128,2048]{1,0:T(8,128)}, f32[128,2048]{1,0:T(8,128)S(1)}, u32[]{:S(2)}) copy-start(f32[128,2048]{1,0:T(8,128)S(1)} %get-tuple-element.159.resid) | copy-start | bytes 3145732
  174.6 3.4 copy-start.31
  308.1 5.0 copy-start.29
  308.1 78.0 %all-to-all-start = ((bf16[8,2,4,24,2048]{4,3,2,1,0:T(8,128)(2,1)}), bf16[8,2,4,24,2048]{4,3,2,1,0:T(8,128)(2,1)}, u32[]{:S(2)}, u32[]{:S(2)}) async-start(bf16[8,2,4,24,2048]{4,3,2,1,0:T(8,128)(2,1)} %get-tuple-element.91), calls=%async_computation | async-start | bytes 12582912 | tf_op jit(solution)/shard_map/all_to_all | solution.py:2115
  327.8 1.7 copy-start.2
  342.0 1.7 copy-start.3
  386.1 89.0 %copy-start.32 = (bf16[128,2048]{1,0:T(8,128)(2,1)S(1)}, bf16[128,2048]{1,0:T(8,128)(2,1)}, u32[]{:S(2)}) copy-start(bf16[128,2048]{1,0:T(8,128)(2,1)} %copy-done.31) | copy-start | bytes 1572868
  476.4 7.8 %copy-start.35 = (bf16[1,128,2048]{2,1,0:T(8,128)(2,1)S(1)}, bf16[1,128,2048]{2,1,0:T(8,128)(2,1)}, u32[]{:S(2)}) copy-start(bf16[1,128,2048]{2,1,0:T(8,128)(2,1)} %param.11) | copy-start | bytes 1572868
  479.6 4.7 copy-start.34
  479.6 41.3 %copy-start.17 = (bf16[1024,256]{1,0:T(8,128)(2,1)S(1)}, bf16[1024,256]{1,0:T(8,128)(2,1)}, u32[]{:S(2)}) copy-start(bf16[1024,256]{1,0:T(8,128)(2,1)} %get-tuple-element.74) | copy-start | bytes 1572868
  479.6 87.5 %all-to-all-start.1 = ((bf16[4,128,2048]{2,1,0:T(8,128)(2,1)}), bf16[4,128,2048]{2,1,0:T(8,128)(2,1)}, u32[]{:S(2)}, u32[]{:S(2)}) async-start(bf16[4,128,2048]{2,1,0:T(8,128)(2,1)} %get-tuple-element.111), calls=%async_computation.1 | async-start | bytes 4194304 | tf_op jit(solution)/shard_map/all_to_all | solution.py:2208
  484.2 81.1 %reduce-scatter.2.cloned.1.call-start = ((), (), s32[]{:S(2)}) async-start(), calls=%async_computation.4 | async-start | bytes 1310720 | tf_op jit(solution)/shard_map/reduce_scatter | solution.py:2267
  520.8 4.7 copy-start.12
  529.8 18.6 %copy-start.1 = (f32[1024,768]{1,0:T(8,128)S(1)}, f32[1024,768]{1,0:T(8,128)}, u32[]{:S(2)}) copy-start(f32[1024,768]{1,0:T(8,128)} %copy-done) | copy-start | bytes 9437188
  529.9 18.6 %copy-start.23 = (f32[8,1024]{1,0:T(8,128)S(1)}, f32[8,1024]{1,0:T(8,128)}, u32[]{:S(2)}) copy-start(f32[8,1024]{1,0:T(8,128)} %copy-done.22) | copy-start | bytes 98308
  529.9 18.6 %copy-start.25 = (f32[8,256]{1,0:T(8,128)S(1)}, f32[8,256]{1,0:T(8,128)}, u32[]{:S(2)}) copy-start(f32[8,256]{1,0:T(8,128)} %constant_dynamic-slice_fusion.1.gain) | copy-start | bytes 24580
  529.9 18.6 %copy-start.26 = (f32[64,256]{1,0:T(8,128)S(1)}, f32[64,256]{1,0:T(8,128)}, u32[]{:S(2)}) copy-start(f32[64,256]{1,0:T(8,128)} %get-tuple-element.109.terms) | copy-start | bytes 196612
  548.5 1.2 copy-start.13
  549.7 1.2 copy-start.14
  551.0 1.0 copy-start.18
  552.0 0.8 copy-start.27
  562.7 1.1 copy-start.10
Sparse Core Ops, SparseCore 0:
  103.0 27.3 all-gather.3
  132.6 45.4 all-gather.5
  525.6 27.2 reduce-scatter.1

commit v5 on v4

--- a/solution.py
+++ b/solution.py
@@ -142,6 +142,27 @@
             barrier, inc=1, device_id=(me_s, (me_f + i) % n_fsdp), device_id_type=MESH
         )
     pl.semaphore_wait(barrier, n_seq + n_fsdp - 2)
+
+
+def loading(body, greet, inputs):
+    def kernel(*refs):
+        held, sems = refs[-1 - inputs : -1], refs[-1]
+        copies = [
+            pltpu.make_async_copy(refs[i], held[i], sems.at[i]) for i in range(inputs)
+        ]
+        for copy in copies:
+            copy.start()
+        greet()
+        for copy in copies:
+            copy.wait()
+        body(*held, *refs[inputs : -1 - inputs])
+
+    return kernel
+
+
+def load_scratch(arrays):
+    held = [pltpu.VMEM(array.shape, array.dtype) for array in arrays]
+    return held + [pltpu.SemaphoreType.DMA((len(arrays),))]
 
 
 class Exchange:
@@ -350,7 +371,6 @@
     ]
     for copy in own:
         copy.start()
-    greet_all(n_seq, n_fsdp)
 
     def small_copy(i):
         other = (me + i) % n
@@ -591,7 +611,11 @@
     any_space = pl.BlockSpec(memory_space=pl.ANY)
     dma = pltpu.SemaphoreType.DMA
     return pl.pallas_call(
-        functools.partial(first_kernel, n_seq, n_fsdp, pieces, split, capacity, owned, top),
+        loading(
+            functools.partial(first_kernel, n_seq, n_fsdp, pieces, split, capacity, owned, top),
+            functools.partial(greet_all, n_seq, n_fsdp),
+            4,
+        ),
         out_shape=[
             jax.ShapeDtypeStruct((n,) + small.shape, BF),
             jax.ShapeDtypeStruct((8, width), F32),
@@ -602,7 +626,7 @@
             jax.ShapeDtypeStruct((n_fsdp, rows, places_all), BF),
             jax.ShapeDtypeStruct((8, experts), F32),
         ],
-        in_specs=[vmem] * 4 + [pl.BlockSpec(memory_space=pltpu.SMEM)],
+        in_specs=[pl.BlockSpec(memory_space=pltpu.HBM)] * 4 + [pl.BlockSpec(memory_space=pltpu.SMEM)],
         out_specs=[vmem, vmem, any_space, any_space, any_space, vmem, vmem, vmem],
         scratch_shapes=[
             pltpu.VMEM((n_seq, pieces, capacity, width), BF),
@@ -618,9 +642,10 @@
             dma((n_seq,)),
             dma((n_seq,)),
             dma,
-        ],
+        ]
+        + load_scratch([small, tokens, qkv, masked]),
         compiler_params=pltpu.CompilerParams(
-            collective_id=collective_id, has_side_effects=True, vmem_limit_bytes=40 << 20
+            collective_id=collective_id, has_side_effects=True, vmem_limit_bytes=62 << 20
         ),
         name="first_gather",
     )(small, tokens, qkv, masked, lengths)
@@ -888,7 +913,6 @@
 
 
 def reduce_kernel(n_seq, w_dim, a, w, out, *scratch):
-    greet_seq(n_seq)
     reduce = SeqReduce(n_seq, a, w, w_dim, *scratch)
     for stage in range(reduce.stages):
         reduce.start(stage)
@@ -899,17 +923,22 @@
 def product_reduced(a, w, w_dim, n_seq, collective_id):
     rows = a.shape[0] // n_seq
     width = w.shape[1 - w_dim]
+    a = a.reshape(n_seq, rows, -1)
     return pl.pallas_call(
-        functools.partial(reduce_kernel, n_seq, w_dim),
+        loading(
+            functools.partial(reduce_kernel, n_seq, w_dim),
+            functools.partial(greet_seq, n_seq),
+            2,
+        ),
         out_shape=jax.ShapeDtypeStruct((rows, width), F32),
-        in_specs=[pl.BlockSpec(memory_space=pltpu.VMEM)] * 2,
+        in_specs=[pl.BlockSpec(memory_space=pltpu.HBM)] * 2,
         out_specs=pl.BlockSpec(memory_space=pltpu.VMEM),
-        scratch_shapes=reduce_scratch(n_seq, rows, width),
+        scratch_shapes=reduce_scratch(n_seq, rows, width) + load_scratch([a, w]),
         compiler_params=pltpu.CompilerParams(
-            collective_id=collective_id, has_side_effects=True, vmem_limit_bytes=40 << 20
+            collective_id=collective_id, has_side_effects=True, vmem_limit_bytes=62 << 20
         ),
         name="product_reduced",
-    )(a.reshape(n_seq, rows, -1), w)
+    )(a, w)
 
 
 def last_kernel(
@@ -1147,9 +1176,10 @@
     masked_all, columns_out, scaled = refs[:3]
     outs, hiddens, acts, results = (refs[3 + k * pieces : 3 + (k + 1) * pieces] for k in range(4))
     rest = refs[3 + 4 * pieces :]
-    gates_out, gathered, send, total = rest[:4]
-    own_sem, line_send, line_recv, row_send, row_recv, own_two, send_two, recv_two = rest[4:12]
-    gate_exchange = Exchange(n_seq, n_fsdp, gates, gates_out, rest[12:])
+    gates_out, gathered, gathered_two, send, total = rest[:5]
+    own_sem, line_send, line_recv, row_send, row_recv, own_two, send_two, recv_two = rest[5:13]
+    line_send_two, line_recv_two = rest[13:15]
+    gate_exchange = Exchange(n_seq, n_fsdp, gates, gates_out, rest[15:])
     me_s, me_f = lax.axis_index("seq"), lax.axis_index("fsdp")
     width = x.shape[1]
     capacity = outs[0].shape[2]
@@ -1159,6 +1189,16 @@
         src = x if step == 0 else gathered.at[block]
         return remote(
             src, gathered.at[block], line_send.at[way, step], line_recv.at[block], (me_s, to)
+        )
+
+    def line_two(step, block, way, to):
+        src = masked if step == 0 else gathered_two.at[block]
+        return remote(
+            src,
+            gathered_two.at[block],
+            line_send_two.at[way, step],
+            line_recv_two.at[block],
+            (me_s, to),
         )
 
     def row_copy(block, i, piece, place):
@@ -1211,7 +1251,7 @@
             own_copy(block, piece).wait()
             for i in range(1, n_seq):
                 row_copy(block, i, piece, me_s).wait_send()
-        pick(block, masked.at[block])
+        pick(block, gathered_two.at[block])
         for i in range(1, n_seq):
             masked_copy(block, i, me_s).start()
         own_masked(block).start()
@@ -1243,12 +1283,28 @@
             lambda block, way, to: line_copy(step, block, way, to).start(),
         )
         around(step, lambda block: scatter(block, gathered.at[block]))
+
+    @pl.when(me_f + 1 < n_fsdp)
+    def _():
+        line_two(0, me_f, 0, me_f + 1).start()
+
+    @pl.when(me_f >= 1)
+    def _():
+        line_two(0, me_f, 1, me_f - 1).start()
+
     for step in range(1, n_fsdp):
+        line_step(
+            n_fsdp,
+            step,
+            lambda block: line_two(1, block, 0, me_f).wait_recv(),
+            lambda block, way, to: line_two(step, block, way, to).start(),
+        )
         around(step, scatter_masked)
     for step in range(n_fsdp):
         line_sent(
             n_fsdp, step, lambda block, way, to: line_copy(step, block, way, to).wait_send()
         )
+        line_sent(n_fsdp, step, lambda block, way, to: line_two(step, block, way, to).wait_send())
 
     gate_exchange.finish()
     n = n_seq * n_fsdp
@@ -1365,6 +1421,7 @@
         scratch_shapes=[
             pltpu.VMEM(gates.shape, F32),
             pltpu.VMEM((n_fsdp, count, width), BF),
+            pltpu.VMEM((n_fsdp, count, width), BF),
             pltpu.VMEM((n_fsdp, n_seq, pieces, capacity, width), BF),
             pltpu.VMEM((tile_rows, width), F32),
             dma((n_fsdp, pieces)),
@@ -1375,6 +1432,8 @@
             dma((n_fsdp,)),
             dma((n_fsdp, n_seq)),
             dma((n_seq, n_fsdp)),
+            dma((2, n_fsdp)),
+            dma((n_fsdp,)),
         ]
         + exchange_sems(n_seq * n_fsdp),
         input_output_aliases={4: 0},
@@ -1659,7 +1718,7 @@
             pl.BlockSpec((8, count), lambda r, i: (0, r)),
         ],
         scratch_shapes=[pltpu.VMEM((count, 128), F32)],
-        compiler_params=pltpu.CompilerParams(vmem_limit_bytes=48 << 20),
+        compiler_params=pltpu.CompilerParams(vmem_limit_bytes=62 << 20),
         cost_estimate=pl.CostEstimate(
             flops=2 * rows * width * ff, bytes_accessed=12 * rows * ff, transcendentals=rows * ff
         ),
@@ -1712,8 +1771,7 @@
     )
 
 
-def front_kernel(n_seq, x, gain, w, normed, raw, totals, *scratch):
-    greet_seq(n_seq)
+def front_kernel(n_seq, x, gain, w, normed_out, raw_out, totals, normed, raw, sems, *scratch):
     share = SeqShare(n_seq, *scratch)
     head_width = w.shape[1] // 3
     tile = 256
@@ -1726,31 +1784,53 @@
         normed[rows, :] = low
         result = dot(low, w[...], 1, 0)
         raw[rows, :] = result
+        for copy in away(i):
+            copy.start()
         for part in range(2):
             piece = result[:, part * head_width : (part + 1) * head_width]
             share.own[part : part + 1, rows] = row_sums(piece * piece)[0:1]
         return carry
 
+    def away(i):
+        rows = pl.ds(pl.multiple_of(i * tile, tile), tile)
+        return [
+            pltpu.make_async_copy(normed.at[rows], normed_out.at[rows], sems.at[0, i]),
+            pltpu.make_async_copy(raw.at[rows], raw_out.at[rows], sems.at[1, i]),
+        ]
+
+    def gone(i, carry):
+        for copy in away(i):
+            copy.wait()
+        return carry
+
     share.own[...] = jnp.zeros_like(share.own)
     lax.fori_loop(0, x.shape[0] // tile, some, 0)
     totals[...] = share.total()
+    lax.fori_loop(0, x.shape[0] // tile, gone, 0)
 
 
 def front(x, gains, w, n_seq, collective_id):
     rows, width = x.shape
     vmem = pl.BlockSpec(memory_space=pltpu.VMEM)
+    hbm = pl.BlockSpec(memory_space=pltpu.HBM)
     return pl.pallas_call(
-        functools.partial(front_kernel, n_seq),
+        loading(functools.partial(front_kernel, n_seq), functools.partial(greet_seq, n_seq), 3),
         out_shape=[
             jax.ShapeDtypeStruct((rows, width), BF),
             jax.ShapeDtypeStruct((rows, w.shape[1]), F32),
             jax.ShapeDtypeStruct((8, rows), F32),
         ],
-        in_specs=[vmem] * 3,
-        out_specs=[vmem] * 3,
-        scratch_shapes=share_scratch(n_seq, (8, rows)),
+        in_specs=[hbm] * 3,
+        out_specs=[hbm, hbm, vmem],
+        scratch_shapes=[
+            pltpu.VMEM((rows, width), BF),
+            pltpu.VMEM((rows, w.shape[1]), F32),
+            pltpu.SemaphoreType.DMA((2, rows // 256)),
+        ]
+        + share_scratch(n_seq, (8, rows))
+        + load_scratch([x, gains, w]),
         compiler_params=pltpu.CompilerParams(
-            collective_id=collective_id, has_side_effects=True, vmem_limit_bytes=40 << 20
+            collective_id=collective_id, has_side_effects=True, vmem_limit_bytes=62 << 20
         ),
         name="front",
     )(x, gains, w)
@@ -1836,6 +1916,7 @@
         cost_estimate=pl.CostEstimate(
             flops=4 * heads * slot_len * slot_len * hd, bytes_accessed=1 << 23, transcendentals=0
         ),
+        compiler_params=pltpu.CompilerParams(vmem_limit_bytes=62 << 20),
         name="attend",
     )(length, raw, raw, raw, totals, totals, gains, cosine, sine, cosine, sine)
 
@@ -1955,6 +2036,7 @@
         cost_estimate=pl.CostEstimate(
             flops=20 * heads * slot_len * slot_len * hd, bytes_accessed=1 << 24, transcendentals=0
         ),
+        compiler_params=pltpu.CompilerParams(vmem_limit_bytes=62 << 20),
         name="attend_back",
     )(
         length,
@@ -1977,7 +2059,6 @@
 def raw_back_kernel(
     n_seq, n_fsdp, width, dq, dk, dv, raw, totals, gain, dots, terms, out, terms_out, *scratch
 ):
-    greet_lines(n_seq, n_fsdp)
     share = SeqShare(n_seq, *scratch[:4])
     term_sum = TermSum(n_seq, n_fsdp, None, *scratch[4:6], None, None, *scratch[6:])
     term_sum.start_fsdp(terms[...])
@@ -2007,12 +2088,16 @@
     vmem = pl.BlockSpec(memory_space=pltpu.VMEM)
     dma = pltpu.SemaphoreType.DMA
     return pl.pallas_call(
-        functools.partial(raw_back_kernel, n_seq, n_fsdp, width),
+        loading(
+            functools.partial(raw_back_kernel, n_seq, n_fsdp, width),
+            functools.partial(greet_lines, n_seq, n_fsdp),
+            8,
+        ),
         out_shape=[
             jax.ShapeDtypeStruct(raw.shape, BF),
             jax.ShapeDtypeStruct(terms.shape, F32),
         ],
-        in_specs=[vmem] * 8,
+        in_specs=[pl.BlockSpec(memory_space=pltpu.HBM)] * 8,
         out_specs=[vmem] * 2,
         scratch_shapes=share_scratch(n_seq, dots.shape)
         + [
@@ -2020,9 +2105,10 @@
             pltpu.VMEM((n_fsdp,) + terms.shape, F32),
             dma((n_fsdp,)),
             dma((n_fsdp,)),
-        ],
+        ]
+        + load_scratch([dq, dk, dv, raw, totals, gains, dots, terms]),
         compiler_params=pltpu.CompilerParams(
-            collective_id=collective_id, has_side_effects=True, vmem_limit_bytes=40 << 20
+            collective_id=collective_id, has_side_effects=True, vmem_limit_bytes=62 << 20
         ),
         name="raw_back",
     )(dq, dk, dv, raw, totals, gains, dots, terms)
@@ -2116,8 +2202,6 @@
 
     normed_one, raw, totals = front(slot_tokens, gains, qkv_local, n_seq, collective_id=1)
 
-    masked_later = lax.optimization_barrier((masked_low, raw))[0]
-    plane_masked = lax.all_gather(masked_later, "fsdp", axis=0)
 
     def rms(values):
         return lax.rsqrt(jnp.mean(values * values, axis=-1, keepdims=True) + epsilon)
@@ -2143,7 +2227,7 @@
         normed_two,
         to_places,
         gate_send,
-        plane_masked,
+        masked_low,
         cot_all,
         expert_up,
         expert_down,

time: 664 us -> 645 us (0.971)
  local copies, waits for them, and re-layouts: 41.5 us -> 19.8 us
    unnamed x81 -> x25, local copies, waits for them, and re-layouts: 31.6 us -> 8.11 us
  transfers between devices with their start and end apart: 5 -> 4, of which waited for: 1 -> 1; matrix products, arithmetic and copies ran while one was open for 4% -> 4% of each run, Pallas kernels for 29% -> 25%
where the time goes in v5:
time: 645 us; the launch traced here: 635 us
  Pallas kernels  555 us (86%)
  local copies, waits for them, and re-layouts  19.8 us (3%)
  other arithmetic  18.6 us (3%)
  between operations  17.3 us (3%)
  matrix products  12.8 us (2%)
  starting transfers between devices  9.95 us (2%)
    pallas_call x1, Pallas kernels, dispatch_rows(): pl.pallas_call(functools.partial(dispatch_kernel, n_seq, n_fsdp, pieces),...  129 us
    pallas_call x1, Pallas kernels, return_rows(): pl.pallas_call(functools.partial(return_kernel, n_seq, n_fsdp, pieces), o...  86.1 us
    pallas_call x1, Pallas kernels, first_gather(): pl.pallas_call(loading(functools.partial(first_kernel, n_seq, n_fsdp, pie...  83.8 us
    pallas_call x1, Pallas kernels, last_reduce(): pl.pallas_call(functools.partial(last_kernel, n_seq, n_fsdp), out_shape=[...  68.3 us
    pallas_call x4, Pallas kernels, weight_grad(): pl.pallas_call(weight_grad_kernel, out_shape=jax.ShapeDtypeStruct((pieces...  41.3 us
    pallas_call x1, Pallas kernels, gather_seq(): pl.pallas_call(functools.partial(gather_kernel, n_seq, n_fsdp), out_shape...  34.9 us
    pallas_call x1, Pallas kernels, product_reduced(): pl.pallas_call(loading(functools.partial(reduce_kernel, n_seq, w_dim), fu...  30.8 us
    pallas_call x2, Pallas kernels, expert_backward(): pl.pallas_call(expert_backward_kernel, out_shape=[jax.ShapeDtypeStruct((2...  23.6 us
  transfers between devices with their start and end apart: 4, of which 1 were waited for; matrix products, arithmetic and copies ran while one was open for 4% of the time, Pallas kernels for 25%

profile of v5, /device:TPU:0, one launch (start us, length us, event | category | flops | bytes accessed | tf_op | source)
XLA Modules:
  0.0 634.6 jit_solution(557024093841310427)
XLA Ops:
  7.2 0.8 reshape.123
  8.7 1.2 dynamic_slice.12.length
  10.6 1.9 bitcast_select_fusion.refs_3_.masked
  12.6 1.3 fusion.15.refs_0_
  13.8 83.8 %first_gather.1 = (bf16[32,48,128]{2,1,0:T(8,128)(2,1)}, f32[8,2048]{1,0:T(8,128)}, bf16[8,128,2048]{2,1,0:T(8,128)(2,1)}, bf16[8,4,64,768]{3,2,1,0:T(8,128)(2,1...) custom-call(bf16[48,128]{1,0:T(8,128)(2,1)} %fusion.15.refs_0_, ...), custom_call_target="tpu_custom_call" | custom-call | tf_op jit(solution)/shard_map/first_gather/pallas_call | solution.py:613
  97.7 0.9 slice.42
  98.6 16.4 %front.1 = (bf16[1024,2048]{1,0:T(8,128)(2,1)}, f32[1024,768]{1,0:T(8,128)}, f32[8,1024]{1,0:T(8,128)}) custom-call(bf16[1024,2048]{1,0:T(8,128)(2,1)} %bitcast.61, f32[8,2048]{1,0:T(8,128)} %get-tuple-element.66.refs_1_.gains, bf16[2048,768]{1,0:T(8,128)(2,1)} %bitcast.57), custom_call_target="tpu_custom_call" | custom-call | tf_op jit(solution)/shard_map/front/pallas_call | solution.py:1816
  115.3 1.3 constant_dynamic-slice_fusion.1.gain.refs_5_
  116.6 1.9 fusion.2
  118.5 1.3 pad_maximum_fusion
  119.8 10.9 %attend.1 = (bf16[1024,256]{1,0:T(8,128)(2,1)}, bf16[1024,256]{1,0:T(8,128)(2,1)}, bf16[1024,256]{1,0:T(8,128)(2,1)}, bf16[1024,256]{1,0:T(8,128)(2,1)}) custom-call(s32[1]{0:T(128)} %dynamic_slice.12.length, f32[1024,768]{1,0:T(8,128)} %get-tuple-element.68.raw_q.raw_k.raw_v.refs_3_, f32[1024,768]{1,0:T(8,128)} %get-tuple-element.68.raw_q.raw_k.raw_v.refs_3_, ...), custom_call_target="tpu_custom_call" | custom-call | flops 1073741824 | bytes 8388608 | tf_op jit(solution)/shard_map/attend/pallas_call | solution.py:1896
  130.9 30.8 %product_reduced.1 = f32[128,2048]{1,0:T(8,128)} custom-call(bf16[8,128,256]{2,1,0:T(8,128)(2,1)} %bitcast.68, bf16[256,2048]{1,0:T(8,128)(2,1)} %all-gather.2.cloned.1.call-done.refs_1_), custom_call_target="tpu_custom_call" | custom-call | tf_op jit(solution)/shard_map/product_reduced/pallas_call | solution.py:927
  161.8 1.6 multiply_reduce_fusion.2
  164.9 129.0 %dispatch_rows.1 = (bf16[8,2,4,24,2048]{4,3,2,1,0:T(8,128)(2,1)}, f32[2,768,1]{2,1,0:T(8,128)}, bf16[8,2,4,24,2048]{4,3,2,1,0:T(8,128)(2,1)}, bf16[8,4,24,2048]{...) custom-call(bf16[128,2048]{1,0:T(8,128)(2,1)} %copy-done.1, ...), custom_call_target="tpu_custom_call", output_to_operand_aliasing={{0}: (4, {})} | custom-call | tf_op jit(solution)/shard_map/dispatch_rows/pallas_call | solution.py:1408
  294.0 5.1 all-to-all-start
  300.3 0.7 divide_bitcast_fusion
  301.0 0.9 slice_bitcast_fusion.1
  302.0 11.8 %expert_backward.3 = (bf16[2,768,1024]{2,1,0:T(8,128)(2,1)}, bf16[768,2048]{1,0:T(8,128)(2,1)}, f32[8,768]{1,0:T(8,128)}) custom-call(bf16[8,2,4,24,2048]{4,3,2,1,0:T(8,128)(2,1)} %get-tuple-element.79.masked, f32[768,1]{1,0:T(8,128)} %get-tuple-element.161.gates, bf16[768,2048]{1,0:T(8,128)(2,1)} %get-tuple-element.84.piece_out, ...), custom_call_target="tpu_custom_call" | custom-call | flops 3221225472 | bytes 9437184 | tf_op jit(solution)/shard_map/expert_backward/pallas_call | solution.py:1700
  313.7 0.8 slice_reduce_fusion
  314.6 11.8 %expert_backward.2 = (bf16[2,768,1024]{2,1,0:T(8,128)(2,1)}, bf16[768,2048]{1,0:T(8,128)(2,1)}, f32[8,768]{1,0:T(8,128)}) custom-call(bf16[8,2,4,24,2048]{4,3,2,1,0:T(8,128)(2,1)} %get-tuple-element.79.masked, f32[768,1]{1,0:T(8,128)} %get-tuple-element.160.gates, bf16[768,2048]{1,0:T(8,128)(2,1)} %get-tuple-element.81.piece_out, ...), custom_call_target="tpu_custom_call" | custom-call | flops 3221225472 | bytes 9437184 | tf_op jit(solution)/shard_map/expert_backward/pallas_call | solution.py:1700
  326.4 0.8 slice_reduce_fusion.1
  327.3 0.8 copy.36.gates
  328.2 8.0 %weight_grad.6.refs_0_ = f32[2,1024,2048]{2,1,0:T(8,128)} custom-call(bf16[768,1024]{1,0:T(8,128)(2,1)} %get-tuple-element.94.a, bf16[1,768,2048]{2,1,0:T(8,128)(2,1)} %bitcast.65), custom_call_target="tpu_custom_call" | custom-call | flops 3221225472 | bytes 8388608 | tf_op jit(solution)/shard_map/weight_grad/pallas_call | solution.py:1641
  336.2 8.0 %weight_grad.7 = f32[2,1024,2048]{2,1,0:T(8,128)} custom-call(bf16[768,1024]{1,0:T(8,128)(2,1)} %get-tuple-element.92.a, bf16[1,768,2048]{2,1,0:T(8,128)(2,1)} %bitcast.64, f32[2,1024,2048]{2,1,0:T(8,128)} %weight_grad.6.refs_0_), custom_call_target="tpu_custom_call", output_to_operand_aliasing={{}: (2, {})} | custom-call | flops 3221225472 | bytes 8388608 | tf_op jit(solution)/shard_map/weight_grad/pallas_call | solution.py:1641
  344.2 12.7 %weight_grad.4.refs_0_ = f32[2,2048,2048]{2,1,0:T(8,128)} custom-call(bf16[768,2048]{1,0:T(8,128)(2,1)} %bitcast.63, bf16[2,768,1024]{2,1,0:T(8,128)(2,1)} %get-tuple-element.87.b), custom_call_target="tpu_custom_call" | custom-call | flops 6442450944 | bytes 16777216 | tf_op jit(solution)/shard_map/weight_grad/pallas_call | solution.py:1641
  356.9 12.7 %weight_grad.5 = f32[2,2048,2048]{2,1,0:T(8,128)} custom-call(bf16[768,2048]{1,0:T(8,128)(2,1)} %bitcast.62, bf16[2,768,1024]{2,1,0:T(8,128)(2,1)} %get-tuple-element.88.b, f32[2,2048,2048]{2,1,0:T(8,128)} %weight_grad.4.refs_0_), custom_call_target="tpu_custom_call", output_to_operand_aliasing={{}: (2, {})} | custom-call | flops 6442450944 | bytes 16777216 | tf_op jit(solution)/shard_map/weight_grad/pallas_call | solution.py:1641
  369.5 1.4 all-to-all-done.ready
  370.9 86.1 %return_rows.1 = (f32[128,2048]{1,0:T(8,128)}, f32[32,8,128]{2,1,0:T(8,128)}, bf16[4,128,2048]{2,1,0:T(8,128)(2,1)}) custom-call(bf16[4,128,384]{2,1,0:T(8,128)(2,1)} %get-tuple-element.75.hot, f32[32,8,128]{2,1,0:T(8,128)} %copy.36.gates, bf16[8,2,4,24,2048]{4,3,2,1,0:T(8,128)(2,1)} %all-to-all-done.ready, bf16[2,2048,2048]{2,1,0:T(8,128)(2,1)} %w_up.3, ...), custom_call_target="tpu_custom_call" | custom-call | tf_op jit(solution)/shard_map/return_rows/pallas_call | solution.py:1596
  457.0 0.9 copy.40
  458.5 1.2 fusion.16.terms
  459.8 2.2 multiply_reduce_fusion
  462.0 4.8 all-to-all-start.1
  466.8 2.6 fusion.19
  469.4 34.9 %gather_seq.1 = (bf16[8,128,2048]{2,1,0:T(8,128)(2,1)}, f32[64,256]{1,0:T(8,128)}) custom-call(bf16[128,2048]{1,0:T(8,128)(2,1)} %get-tuple-element.152.x, f32[64,2048]{1,0:T(8,128)} %fusion.16.terms), custom_call_target="tpu_custom_call" | custom-call | bytes 67108864 | tf_op jit(solution)/shard_map/gather_seq/pallas_call | solution.py:777
  504.3 4.5 convolution_convert_fusion
  508.9 4.3 convolution_convert_fusion.1.g_ref
  513.2 17.1 %attend_back.1 = (f32[1024,256]{1,0:T(8,128)}, f32[1024,256]{1,0:T(8,128)}, bf16[1024,256]{1,0:T(8,128)(2,1)}, f32[8,1024]{1,0:T(8,128)}, f32[8,256]{1,0:T(8,128)}) custom-call(s32[1]{0:T(128)} %dynamic_slice.12.length, bf16[1024,256]{1,0:T(8,128)(2,1)} %get-tuple-element.70.q_ref, bf16[1024,256]{1,0:T(8,128)(2,1)} %get-tuple-element.71.k_ref, ...), custom_call_target="tpu_custom_call" | custom-call | flops 5368709120 | bytes 16777216 | tf_op jit(solution)/shard_map/attend_back/pallas_call | solution.py:2000
  530.3 0.7 slice.50
  531.6 12.5 %raw_back.1 = (bf16[1024,768]{1,0:T(8,128)(2,1)}, f32[64,256]{1,0:T(8,128)}) custom-call(f32[1024,256]{1,0:T(8,128)} %get-tuple-element.103.refs_0_, f32[1024,256]{1,0:T(8,128)} %get-tuple-element.104.refs_1_, bf16[1024,256]{1,0:T(8,128)(2,1)} %get-tuple-element.105.refs_2_, f32[1024,768]{1,0:T(8,128)} %get-tuple-element.68.raw_q.raw_k.raw_v.refs_3_, ...), custom_call_target="tpu_custom_call" | custom-call | tf_op jit(solution)/shard_map/raw_back/pallas_call | solution.py:2090
  544.2 0.8 dynamic-slice_bitcast_fusion
  545.0 0.7 copy.35
  546.4 1.8 convert_element_type.87
  548.1 68.3 %last_reduce.1 = (bf16[128,2048]{1,0:T(8,128)(2,1)}, f32[64,6144]{1,0:T(8,128)}, f32[8,256]{1,0:T(8,128)}, bf16[128,2048]{1,0:T(8,128)(2,1)}) custom-call(bf16[8,128,768]{2,1,0:T(8,128)(2,1)} %bitcast.67, bf16[2048,768]{1,0:T(8,128)(2,1)} %bitcast.58, bf16[1024,2048]{1,0:T(8,128)(2,1)} %get-tuple-element.111.normed, bf16[128,2048]{1,0:T(8,128)(2,1)} %bitcast.60, ...), custom_call_target="tpu_custom_call" | custom-call | bytes 134217728 | tf_op jit(solution)/shard_map/last_reduce/pallas_call | solution.py:1132
  616.4 0.8 constant_dynamic-slice_fusion
  617.2 1.3 divide_reduce_fusion
  619.7 1.9 copy.47
  621.6 1.9 copy.48
  623.5 2.7 copy.49
  (60 shorter events, 6.9 us)
Async XLA Ops:
  7.2 123.8 %all-gather.2.cloned.1.call-start = ((), (), s32[]{:S(2)}) async-start(), calls=%async_computation.3 | async-start | bytes 1310720 | tf_op jit(solution)/shard_map/all_gather | solution.py:2198
  97.7 17.3 %copy-start.6 = (bf16[32,48,128]{2,1,0:T(8,128)(2,1)S(1)}, bf16[32,48,128]{2,1,0:T(8,128)(2,1)}, u32[]{:S(2)}) copy-start(bf16[32,48,128]{2,1,0:T(8,128)(2,1)} %get-tuple-element.77) | copy-start | bytes 1179652
  119.8 10.9 %copy-start.7 = (s32[1,128,8]{1,2,0:T(8,128)S(1)}, s32[1,128,8]{1,2,0:T(8,128)}, u32[]{:S(2)}) copy-start(s32[1,128,8]{1,2,0:T(8,128)} %param.13) | copy-start | bytes 12292
  163.3 303.5 %copy-start = (f32[128,2048]{1,0:T(8,128)}, f32[128,2048]{1,0:T(8,128)S(1)}, u32[]{:S(2)}) copy-start(f32[128,2048]{1,0:T(8,128)S(1)} %get-tuple-element.157.resid) | copy-start | bytes 3145732
  163.5 1.4 copy-start.1
  294.0 5.1 copy-start.8
  294.0 7.1 %copy-start.4 = (f32[2,768,1]{2,1,0:T(8,128)S(1)}, f32[2,768,1]{2,1,0:T(8,128)}, u32[]{:S(2)}) copy-start(f32[2,768,1]{2,1,0:T(8,128)} %get-tuple-element.80) | copy-start | bytes 18436
  294.0 76.9 %all-to-all-start = ((bf16[8,2,4,24,2048]{4,3,2,1,0:T(8,128)(2,1)}), bf16[8,2,4,24,2048]{4,3,2,1,0:T(8,128)(2,1)}, u32[]{:S(2)}, u32[]{:S(2)}) async-start(bf16[8,2,4,24,2048]{4,3,2,1,0:T(8,128)(2,1)} %get-tuple-element.89), calls=%async_computation | async-start | bytes 12582912 | tf_op jit(solution)/shard_map/all_to_all | solution.py:2201
  370.9 87.6 %copy-start.2 = (bf16[128,2048]{1,0:T(8,128)(2,1)S(1)}, bf16[128,2048]{1,0:T(8,128)(2,1)}, u32[]{:S(2)}) copy-start(bf16[128,2048]{1,0:T(8,128)(2,1)} %copy-done.1) | copy-start | bytes 1572868
  462.0 42.4 %copy-start.5 = (bf16[1024,256]{1,0:T(8,128)(2,1)S(1)}, bf16[1024,256]{1,0:T(8,128)(2,1)}, u32[]{:S(2)}) copy-start(bf16[1024,256]{1,0:T(8,128)(2,1)} %get-tuple-element.73) | copy-start | bytes 1572868
  462.0 86.2 %all-to-all-start.1 = ((bf16[4,128,2048]{2,1,0:T(8,128)(2,1)}), bf16[4,128,2048]{2,1,0:T(8,128)(2,1)}, u32[]{:S(2)}, u32[]{:S(2)}) async-start(bf16[4,128,2048]{2,1,0:T(8,128)(2,1)} %get-tuple-element.109), calls=%async_computation.1 | async-start | bytes 4194304 | tf_op jit(solution)/shard_map/all_to_all | solution.py:2292
  466.8 79.6 %reduce-scatter.2.cloned.1.call-start = ((), (), s32[]{:S(2)}) async-start(), calls=%async_computation.4 | async-start | bytes 1310720 | tf_op jit(solution)/shard_map/reduce_scatter | solution.py:2351
  504.3 4.6 copy-start.3
Sparse Core Ops, SparseCore 0:
  97.8 26.8 all-gather.1
  509.0 27.3 reduce-scatter.1

commit v6 on v5

--- a/solution.py
+++ b/solution.py
@@ -2,6 +2,7 @@
 
 import jax
 import jax.numpy as jnp
+import numpy as np
 from jax import lax
 from jax.experimental import pallas as pl
 from jax.experimental.pallas import tpu as pltpu
@@ -332,6 +333,7 @@
     to_places,
     to_rows,
     counts,
+    own_gains,
     send,
     own_sem,
     small_send,
@@ -544,6 +546,7 @@
             some = jnp.where(lane < owned, small_all[j * each + k, :8, :].astype(F32), 0.0)
             total = total + (pltpu.roll(some, k * owned, 1) if k else some)
         gains[:, j * 128 : (j + 1) * 128] = total
+    own_gains[...] = gains[:, pl.ds(pl.multiple_of(me_s * head_width, 128), head_width)]
 
     all_ids = lax.broadcasted_iota(jnp.int32, (counts.shape[1], 1), 0)
     position = lax.broadcasted_iota(jnp.int32, (1, tokens.shape[0]), 1)
@@ -625,9 +628,10 @@
             jax.ShapeDtypeStruct((n_fsdp, places_all, rows), BF),
             jax.ShapeDtypeStruct((n_fsdp, rows, places_all), BF),
             jax.ShapeDtypeStruct((8, experts), F32),
+            jax.ShapeDtypeStruct((8, head_width), F32),
         ],
         in_specs=[pl.BlockSpec(memory_space=pltpu.HBM)] * 4 + [pl.BlockSpec(memory_space=pltpu.SMEM)],
-        out_specs=[vmem, vmem, any_space, any_space, any_space, vmem, vmem, vmem],
+        out_specs=[vmem, vmem, any_space, any_space, any_space, vmem, vmem, vmem, vmem],
         scratch_shapes=[
             pltpu.VMEM((n_seq, pieces, capacity, width), BF),
             dma((5,)),
@@ -1472,18 +1476,20 @@
             ready.at[:, :, block], some_ready.at[block % 2], ready_sem.at[block % 2]
         )
 
-    def row_copy(block, i, place):
+    def row_copy(block, i, piece, place):
         other = (me_s + i) % n_seq
         return remote(
-            rows.at[block, other],
-            got.at[block, place],
-            row_send.at[block, i],
-            row_recv.at[block, place],
+            rows.at[block, other, piece],
+            got.at[block, place, piece],
+            row_send.at[block, i, piece],
+            row_recv.at[block, place, piece],
             (other, me_f),
         )
 
-    def own_copy(block):
-        return pltpu.make_async_copy(rows.at[block, me_s], got.at[block, me_s], own_sem.at[block])
+    def own_copy(block, piece):
+        return pltpu.make_async_copy(
+            rows.at[block, me_s, piece], got.at[block, me_s, piece], own_sem.at[block, piece]
+        )
 
     def part_copy(j):
         block = (me_f + j) % n_fsdp
@@ -1522,15 +1528,16 @@
                 return carry
 
             lax.fori_loop(0, chunks, some, 0)
-        for i in range(1, n_seq):
-            row_copy(block, i, me_s).start()
-        own_copy(block).start()
+            for i in range(1, n_seq):
+                row_copy(block, i, piece, me_s).start()
+            own_copy(block, piece).start()
 
     def finish(j):
         block = (me_f + j) % n_fsdp
-        own_copy(block).wait()
-        for i in range(1, n_seq):
-            row_copy(block, i, (me_s + i) % n_seq).wait_recv()
+        for piece in range(pieces):
+            own_copy(block, piece).wait()
+            for i in range(1, n_seq):
+                row_copy(block, i, piece, (me_s + i) % n_seq).wait_recv()
 
         def some(columns):
             arrived = got[block, :, :, :, columns].reshape(n_seq * pieces * capacity, -1)
@@ -1580,8 +1587,9 @@
     for j in range(1, n_fsdp):
         part_copy(j).wait_send()
     for block in range(n_fsdp):
-        for i in range(1, n_seq):
-            row_copy(block, i, me_s).wait_send()
+        for piece in range(pieces):
+            for i in range(1, n_seq):
+                row_copy(block, i, piece, me_s).wait_send()
     gate_exchange.finish()
 
 
@@ -1613,9 +1621,9 @@
             dma((pieces, width // min(256, width))),
             dma((pieces,)),
             dma((2,)),
-            dma((n_fsdp,)),
-            dma((n_fsdp, n_seq)),
-            dma((n_fsdp, n_seq)),
+            dma((n_fsdp, pieces)),
+            dma((n_fsdp, n_seq, pieces)),
+            dma((n_fsdp, n_seq, pieces)),
             dma((n_fsdp,)),
             dma((n_fsdp,)),
         ]
@@ -2114,12 +2122,13 @@
     )(dq, dk, dv, raw, totals, gains, dots, terms)
 
 
-def rope_tables(positions, head_dim):
+def rope_tables(count, head_dim):
     half = head_dim // 2
-    frequency = rope_base ** (-jnp.arange(half, dtype=F32) * 2.0 / head_dim)
-    angles = positions.astype(F32)[:, None] * frequency[None, :]
-    cosine, sine = jnp.cos(angles), jnp.sin(angles)
-    return jnp.concatenate([cosine, cosine], axis=1), jnp.concatenate([-sine, sine], axis=1)
+    frequency = rope_base ** (-np.arange(half, dtype=np.float64) * 2.0 / head_dim)
+    angles = np.arange(count, dtype=np.float64)[:, None] * frequency[None, :]
+    cosine, sine = np.cos(angles), np.sin(angles)
+    both = np.concatenate([cosine, cosine], axis=1), np.concatenate([-sine, sine], axis=1)
+    return tuple(jnp.asarray(table, F32) for table in both)
 
 
 def places(block_routes, experts, capacity):
@@ -2175,7 +2184,7 @@
             rows_of(router_weight.reshape(-1), 16),
         ]
     )
-    small, gains, slot_tokens, qkv_local, cot_all, to_places, to_rows, counts = first_gather(
+    small, gains, slot_tokens, qkv_local, cot_all, to_places, to_rows, *more = first_gather(
         own_small,
         tokens[0],
         qkv_weight,
@@ -2190,6 +2199,7 @@
         experts,
         collective_id=0,
     )
+    counts, own_gains = more
     slot_tokens = slot_tokens.reshape(slot_len, width)
     qkv_local = qkv_local.reshape(width, 3 * head_width)
     router = small[:, 8 + top_count :].reshape(n_dev, -1)[:, : owned * experts]
@@ -2206,8 +2216,7 @@
     def rms(values):
         return lax.rsqrt(jnp.mean(values * values, axis=-1, keepdims=True) + epsilon)
 
-    own_gains = lax.dynamic_slice_in_dim(gains, me_s * head_width, head_width, 1)
-    cosine, sine = rope_tables(jnp.arange(slot_len, dtype=jnp.int32), head_dim)
+    cosine, sine = rope_tables(slot_len, head_dim)
     attended, query, key, value = attend(
         raw, totals, own_gains, cosine, sine, length, block, width
     )

time: 645 us -> 638 us (0.989)
  no operation moved by 1% of the time
where the time goes in v6:
time: 638 us; the launch traced here: 628 us
  Pallas kernels  553 us (87%)
  local copies, waits for them, and re-layouts  18.5 us (3%)
  between operations  17.3 us (3%)
  other arithmetic  15.4 us (2%)
  matrix products  12.8 us (2%)
  starting transfers between devices  9.73 us (2%)
    pallas_call x1, Pallas kernels, dispatch_rows(): pl.pallas_call(functools.partial(dispatch_kernel, n_seq, n_fsdp, pieces),...  129 us
    pallas_call x1, Pallas kernels, return_rows(): pl.pallas_call(functools.partial(return_kernel, n_seq, n_fsdp, pieces), o...  85 us
    pallas_call x1, Pallas kernels, first_gather(): pl.pallas_call(loading(functools.partial(first_kernel, n_seq, n_fsdp, pie...  83.8 us
    pallas_call x1, Pallas kernels, last_reduce(): pl.pallas_call(functools.partial(last_kernel, n_seq, n_fsdp), out_shape=[...  68.2 us
    pallas_call x4, Pallas kernels, weight_grad(): pl.pallas_call(weight_grad_kernel, out_shape=jax.ShapeDtypeStruct((pieces...  41.4 us
    pallas_call x1, Pallas kernels, gather_seq(): pl.pallas_call(functools.partial(gather_kernel, n_seq, n_fsdp), out_shape...  34 us
    pallas_call x1, Pallas kernels, product_reduced(): pl.pallas_call(loading(functools.partial(reduce_kernel, n_seq, w_dim), fu...  30.9 us
    pallas_call x2, Pallas kernels, expert_backward(): pl.pallas_call(expert_backward_kernel, out_shape=[jax.ShapeDtypeStruct((2...  23.6 us
  transfers between devices with their start and end apart: 4, of which 1 were waited for; matrix products, arithmetic and copies ran while one was open for 4% of the time, Pallas kernels for 25%

profile of v6, /device:TPU:0, one launch (start us, length us, event | category | flops | bytes accessed | tf_op | source)
XLA Modules:
  0.0 627.9 jit_solution(11843879259297624292)
XLA Ops:
  7.2 0.8 reshape.113
  8.0 0.7 convert_bitcast_fusion
  8.7 1.2 dynamic_slice.9.length
  10.6 1.9 bitcast_select_fusion.refs_3_.masked
  12.6 1.3 fusion.14.refs_0_
  13.8 83.8 %first_gather.1 = (bf16[32,48,128]{2,1,0:T(8,128)(2,1)}, f32[8,2048]{1,0:T(8,128)}, bf16[8,128,2048]{2,1,0:T(8,128)(2,1)}, bf16[8,4,64,768]{3,2,1,0:T(8,128)(2,1...) custom-call(bf16[48,128]{1,0:T(8,128)(2,1)} %fusion.14.refs_0_, ...), custom_call_target="tpu_custom_call" | custom-call | tf_op jit(solution)/shard_map/first_gather/pallas_call | solution.py:616
  97.7 0.9 slice.42
  98.6 16.3 %front.1 = (bf16[1024,2048]{1,0:T(8,128)(2,1)}, f32[1024,768]{1,0:T(8,128)}, f32[8,1024]{1,0:T(8,128)}) custom-call(bf16[1024,2048]{1,0:T(8,128)(2,1)} %bitcast.61, f32[8,2048]{1,0:T(8,128)} %get-tuple-element.67.refs_1_.gains, bf16[2048,768]{1,0:T(8,128)(2,1)} %bitcast.57), custom_call_target="tpu_custom_call" | custom-call | tf_op jit(solution)/shard_map/front/pallas_call | solution.py:1824
  115.2 10.8 %attend.1 = (bf16[1024,256]{1,0:T(8,128)(2,1)}, bf16[1024,256]{1,0:T(8,128)(2,1)}, bf16[1024,256]{1,0:T(8,128)(2,1)}, bf16[1024,256]{1,0:T(8,128)(2,1)}) custom-call(s32[1]{0:T(128)} %dynamic_slice.9.length, f32[1024,768]{1,0:T(8,128)} %get-tuple-element.69.raw_q.raw_k.raw_v.refs_3_, f32[1024,768]{1,0:T(8,128)} %get-tuple-element.69.raw_q.raw_k.raw_v.refs_3_, ...), custom_call_target="tpu_custom_call" | custom-call | flops 1073741824 | bytes 8388608 | tf_op jit(solution)/shard_map/attend/pallas_call | solution.py:1904
  126.3 30.9 %product_reduced.1 = f32[128,2048]{1,0:T(8,128)} custom-call(bf16[8,128,256]{2,1,0:T(8,128)(2,1)} %bitcast.68, bf16[256,2048]{1,0:T(8,128)(2,1)} %all-gather.2.cloned.1.call-done.refs_1_), custom_call_target="tpu_custom_call" | custom-call | tf_op jit(solution)/shard_map/product_reduced/pallas_call | solution.py:931
  157.2 1.6 multiply_reduce_fusion.2
  159.7 0.7 pad.25.gates
  160.4 129.1 %dispatch_rows.1 = (bf16[8,2,4,24,2048]{4,3,2,1,0:T(8,128)(2,1)}, f32[2,768,1]{2,1,0:T(8,128)}, bf16[8,2,4,24,2048]{4,3,2,1,0:T(8,128)(2,1)}, bf16[8,4,24,2048]{...) custom-call(bf16[128,2048]{1,0:T(8,128)(2,1)} %copy-done.1, ...), custom_call_target="tpu_custom_call", output_to_operand_aliasing={{0}: (4, {})} | custom-call | tf_op jit(solution)/shard_map/dispatch_rows/pallas_call | solution.py:1412
  289.5 5.1 all-to-all-start
  295.8 0.7 divide_bitcast_fusion
  296.5 0.9 slice_bitcast_fusion.1
  297.5 11.8 %expert_backward.3 = (bf16[2,768,1024]{2,1,0:T(8,128)(2,1)}, bf16[768,2048]{1,0:T(8,128)(2,1)}, f32[8,768]{1,0:T(8,128)}) custom-call(bf16[8,2,4,24,2048]{4,3,2,1,0:T(8,128)(2,1)} %get-tuple-element.81.masked, f32[768,1]{1,0:T(8,128)} %get-tuple-element.163.gates, bf16[768,2048]{1,0:T(8,128)(2,1)} %get-tuple-element.86.piece_out, ...), custom_call_target="tpu_custom_call" | custom-call | flops 3221225472 | bytes 9437184 | tf_op jit(solution)/shard_map/expert_backward/pallas_call | solution.py:1708
  309.2 0.8 slice_reduce_fusion
  310.1 11.8 %expert_backward.2 = (bf16[2,768,1024]{2,1,0:T(8,128)(2,1)}, bf16[768,2048]{1,0:T(8,128)(2,1)}, f32[8,768]{1,0:T(8,128)}) custom-call(bf16[8,2,4,24,2048]{4,3,2,1,0:T(8,128)(2,1)} %get-tuple-element.81.masked, f32[768,1]{1,0:T(8,128)} %get-tuple-element.162.gates, bf16[768,2048]{1,0:T(8,128)(2,1)} %get-tuple-element.83.piece_out, ...), custom_call_target="tpu_custom_call" | custom-call | flops 3221225472 | bytes 9437184 | tf_op jit(solution)/shard_map/expert_backward/pallas_call | solution.py:1708
  321.9 0.8 slice_reduce_fusion.1
  322.8 0.8 copy.38.gates
  323.7 8.0 %weight_grad.6.refs_0_ = f32[2,1024,2048]{2,1,0:T(8,128)} custom-call(bf16[768,1024]{1,0:T(8,128)(2,1)} %get-tuple-element.96.a, bf16[1,768,2048]{2,1,0:T(8,128)(2,1)} %bitcast.65), custom_call_target="tpu_custom_call" | custom-call | flops 3221225472 | bytes 8388608 | tf_op jit(solution)/shard_map/weight_grad/pallas_call | solution.py:1649
  331.7 8.0 %weight_grad.7 = f32[2,1024,2048]{2,1,0:T(8,128)} custom-call(bf16[768,1024]{1,0:T(8,128)(2,1)} %get-tuple-element.94.a, bf16[1,768,2048]{2,1,0:T(8,128)(2,1)} %bitcast.64, f32[2,1024,2048]{2,1,0:T(8,128)} %weight_grad.6.refs_0_), custom_call_target="tpu_custom_call", output_to_operand_aliasing={{}: (2, {})} | custom-call | flops 3221225472 | bytes 8388608 | tf_op jit(solution)/shard_map/weight_grad/pallas_call | solution.py:1649
  339.7 12.7 %weight_grad.4.refs_0_ = f32[2,2048,2048]{2,1,0:T(8,128)} custom-call(bf16[768,2048]{1,0:T(8,128)(2,1)} %bitcast.63, bf16[2,768,1024]{2,1,0:T(8,128)(2,1)} %get-tuple-element.89.b), custom_call_target="tpu_custom_call" | custom-call | flops 6442450944 | bytes 16777216 | tf_op jit(solution)/shard_map/weight_grad/pallas_call | solution.py:1649
  352.4 12.7 %weight_grad.5 = f32[2,2048,2048]{2,1,0:T(8,128)} custom-call(bf16[768,2048]{1,0:T(8,128)(2,1)} %bitcast.62, bf16[2,768,1024]{2,1,0:T(8,128)(2,1)} %get-tuple-element.90.b, f32[2,2048,2048]{2,1,0:T(8,128)} %weight_grad.4.refs_0_), custom_call_target="tpu_custom_call", output_to_operand_aliasing={{}: (2, {})} | custom-call | flops 6442450944 | bytes 16777216 | tf_op jit(solution)/shard_map/weight_grad/pallas_call | solution.py:1649
  365.0 1.4 all-to-all-done.ready
  366.4 85.0 %return_rows.1 = (f32[128,2048]{1,0:T(8,128)}, f32[32,8,128]{2,1,0:T(8,128)}, bf16[4,128,2048]{2,1,0:T(8,128)(2,1)}) custom-call(bf16[4,128,384]{2,1,0:T(8,128)(2,1)} %get-tuple-element.77.hot, f32[32,8,128]{2,1,0:T(8,128)} %copy.38.gates, bf16[8,2,4,24,2048]{4,3,2,1,0:T(8,128)(2,1)} %all-to-all-done.ready, bf16[2,2048,2048]{2,1,0:T(8,128)(2,1)} %w_up.3, ...), custom_call_target="tpu_custom_call" | custom-call | tf_op jit(solution)/shard_map/return_rows/pallas_call | solution.py:1604
  451.4 0.9 copy.42
  452.9 1.2 fusion.15.terms
  454.1 2.2 multiply_reduce_fusion
  456.4 4.6 all-to-all-start.1
  461.0 2.6 fusion.18
  463.6 34.0 %gather_seq.1 = (bf16[8,128,2048]{2,1,0:T(8,128)(2,1)}, f32[64,256]{1,0:T(8,128)}) custom-call(bf16[128,2048]{1,0:T(8,128)(2,1)} %get-tuple-element.154.x, f32[64,2048]{1,0:T(8,128)} %fusion.15.terms), custom_call_target="tpu_custom_call" | custom-call | bytes 67108864 | tf_op jit(solution)/shard_map/gather_seq/pallas_call | solution.py:781
  497.6 4.5 convolution_convert_fusion
  502.2 4.3 convolution_convert_fusion.1.g_ref
  506.4 17.0 %attend_back.1 = (f32[1024,256]{1,0:T(8,128)}, f32[1024,256]{1,0:T(8,128)}, bf16[1024,256]{1,0:T(8,128)(2,1)}, f32[8,1024]{1,0:T(8,128)}, f32[8,256]{1,0:T(8,128)}) custom-call(s32[1]{0:T(128)} %dynamic_slice.9.length, bf16[1024,256]{1,0:T(8,128)(2,1)} %get-tuple-element.72.q_ref, bf16[1024,256]{1,0:T(8,128)(2,1)} %get-tuple-element.73.k_ref, ...), custom_call_target="tpu_custom_call" | custom-call | flops 5368709120 | bytes 16777216 | tf_op jit(solution)/shard_map/attend_back/pallas_call | solution.py:2008
  523.4 0.7 slice.50
  524.7 12.8 %raw_back.1 = (bf16[1024,768]{1,0:T(8,128)(2,1)}, f32[64,256]{1,0:T(8,128)}) custom-call(f32[1024,256]{1,0:T(8,128)} %get-tuple-element.105.refs_0_, f32[1024,256]{1,0:T(8,128)} %get-tuple-element.106.refs_1_, bf16[1024,256]{1,0:T(8,128)(2,1)} %get-tuple-element.107.refs_2_, f32[1024,768]{1,0:T(8,128)} %get-tuple-element.69.raw_q.raw_k.raw_v.refs_3_, ...), custom_call_target="tpu_custom_call" | custom-call | tf_op jit(solution)/shard_map/raw_back/pallas_call | solution.py:2098
  537.6 0.8 dynamic-slice_bitcast_fusion
  538.4 0.7 copy.37
  539.1 0.7 select_maximum_fusion.terms_in
  539.8 1.8 convert_element_type.73
  541.6 68.2 %last_reduce.1 = (bf16[128,2048]{1,0:T(8,128)(2,1)}, f32[64,6144]{1,0:T(8,128)}, f32[8,256]{1,0:T(8,128)}, bf16[128,2048]{1,0:T(8,128)(2,1)}) custom-call(bf16[8,128,768]{2,1,0:T(8,128)(2,1)} %bitcast.67, bf16[2048,768]{1,0:T(8,128)(2,1)} %bitcast.58, bf16[1024,2048]{1,0:T(8,128)(2,1)} %get-tuple-element.113.normed, bf16[128,2048]{1,0:T(8,128)(2,1)} %bitcast.60, ...), custom_call_target="tpu_custom_call" | custom-call | bytes 134217728 | tf_op jit(solution)/shard_map/last_reduce/pallas_call | solution.py:1136
  609.8 0.8 constant_dynamic-slice_fusion
  610.6 1.3 divide_reduce_fusion
  613.1 1.9 copy.49
  615.0 1.9 copy.50
  616.9 2.7 copy.51
  (55 shorter events, 4.9 us)
Async XLA Ops:
  7.2 119.2 %all-gather.2.cloned.1.call-start = ((), (), s32[]{:S(2)}) async-start(), calls=%async_computation.3 | async-start | bytes 1310720 | tf_op jit(solution)/shard_map/all_gather | solution.py:2208
  97.7 17.3 %copy-start.6 = (bf16[32,48,128]{2,1,0:T(8,128)(2,1)S(1)}, bf16[32,48,128]{2,1,0:T(8,128)(2,1)}, u32[]{:S(2)}) copy-start(bf16[32,48,128]{2,1,0:T(8,128)(2,1)} %get-tuple-element.79) | copy-start | bytes 1179652
  115.2 10.9 %copy-start.7 = (s32[1,128,8]{1,2,0:T(8,128)S(1)}, s32[1,128,8]{1,2,0:T(8,128)}, u32[]{:S(2)}) copy-start(s32[1,128,8]{1,2,0:T(8,128)} %param.15) | copy-start | bytes 12292
  158.8 302.2 %copy-start = (f32[128,2048]{1,0:T(8,128)}, f32[128,2048]{1,0:T(8,128)S(1)}, u32[]{:S(2)}) copy-start(f32[128,2048]{1,0:T(8,128)S(1)} %get-tuple-element.159.resid) | copy-start | bytes 3145732
  159.0 1.4 copy-start.1
  289.4 5.1 copy-start.8
  289.5 7.1 %copy-start.4 = (f32[2,768,1]{2,1,0:T(8,128)S(1)}, f32[2,768,1]{2,1,0:T(8,128)}, u32[]{:S(2)}) copy-start(f32[2,768,1]{2,1,0:T(8,128)} %get-tuple-element.82) | copy-start | bytes 18436
  289.5 76.9 %all-to-all-start = ((bf16[8,2,4,24,2048]{4,3,2,1,0:T(8,128)(2,1)}), bf16[8,2,4,24,2048]{4,3,2,1,0:T(8,128)(2,1)}, u32[]{:S(2)}, u32[]{:S(2)}) async-start(bf16[8,2,4,24,2048]{4,3,2,1,0:T(8,128)(2,1)} %get-tuple-element.91), calls=%async_computation | async-start | bytes 12582912 | tf_op jit(solution)/shard_map/all_to_all | solution.py:2211
  366.4 86.5 %copy-start.2 = (bf16[128,2048]{1,0:T(8,128)(2,1)S(1)}, bf16[128,2048]{1,0:T(8,128)(2,1)}, u32[]{:S(2)}) copy-start(bf16[128,2048]{1,0:T(8,128)(2,1)} %copy-done.1) | copy-start | bytes 1572868
  456.3 41.2 %copy-start.5 = (bf16[1024,256]{1,0:T(8,128)(2,1)S(1)}, bf16[1024,256]{1,0:T(8,128)(2,1)}, u32[]{:S(2)}) copy-start(bf16[1024,256]{1,0:T(8,128)(2,1)} %get-tuple-element.75) | copy-start | bytes 1572868
  456.4 85.2 %all-to-all-start.1 = ((bf16[4,128,2048]{2,1,0:T(8,128)(2,1)}), bf16[4,128,2048]{2,1,0:T(8,128)(2,1)}, u32[]{:S(2)}, u32[]{:S(2)}) async-start(bf16[4,128,2048]{2,1,0:T(8,128)(2,1)} %get-tuple-element.111), calls=%async_computation.1 | async-start | bytes 4194304 | tf_op jit(solution)/shard_map/all_to_all | solution.py:2301
  460.9 78.8 %reduce-scatter.2.cloned.1.call-start = ((), (), s32[]{:S(2)}) async-start(), calls=%async_computation.4 | async-start | bytes 1310720 | tf_op jit(solution)/shard_map/reduce_scatter | solution.py:2360
  497.5 4.6 copy-start.3
Sparse Core Ops, SparseCore 0:
  97.8 26.8 all-gather.1
  502.2 27.6 reduce-scatter.1

commit v7 on v6

--- a/solution.py
+++ b/solution.py
@@ -323,7 +323,7 @@
     small,
     tokens,
     qkv,
-    masked,
+    cotangent,
     lengths,
     small_all,
     gains,
@@ -334,6 +334,7 @@
     to_rows,
     counts,
     own_gains,
+    masked,
     send,
     own_sem,
     small_send,
@@ -455,6 +456,15 @@
         hot = block_places(routes, ids, capacity)
         to_places[block] = hot.astype(BF)
         to_rows[block] = hot.T.astype(BF)
+
+    row = lax.broadcasted_iota(jnp.int32, (tokens.shape[0], 1), 0) + me_s * tokens.shape[0]
+    valid = row < lengths[me_f]
+
+    def mask(lanes):
+        values = cotangent[:, lanes].astype(F32)
+        masked[:, lanes] = jnp.where(valid, values, 0.0).astype(BF)
+
+    chunked(width, 512, mask)
 
     def scatter():
         def some(lanes):
@@ -629,9 +639,10 @@
             jax.ShapeDtypeStruct((n_fsdp, rows, places_all), BF),
             jax.ShapeDtypeStruct((8, experts), F32),
             jax.ShapeDtypeStruct((8, head_width), F32),
+            jax.ShapeDtypeStruct((rows, width), BF),
         ],
         in_specs=[pl.BlockSpec(memory_space=pltpu.HBM)] * 4 + [pl.BlockSpec(memory_space=pltpu.SMEM)],
-        out_specs=[vmem, vmem, any_space, any_space, any_space, vmem, vmem, vmem, vmem],
+        out_specs=[vmem, vmem, any_space, any_space, any_space] + [vmem] * 5,
         scratch_shapes=[
             pltpu.VMEM((n_seq, pieces, capacity, width), BF),
             dma((5,)),
@@ -2176,7 +2187,6 @@
     push_all = functools.partial(push, n_seq=n_seq, n_fsdp=n_fsdp, scope="all")
     push_seq = functools.partial(push, n_seq=n_seq, n_fsdp=n_fsdp, scope="seq")
 
-    masked_low = jnp.where(row_valid[:, None] > 0, cotangent[0], jnp.zeros((), BF))
     own_small = jnp.concatenate(
         [
             jnp.pad(norm_gains, ((0, 4), (0, 128 - owned))),
@@ -2188,7 +2198,7 @@
         own_small,
         tokens[0],
         qkv_weight,
-        masked_low,
+        cotangent[0],
         lengths,
         n_seq,
         n_fsdp,
@@ -2199,7 +2209,7 @@
         experts,
         collective_id=0,
     )
-    counts, own_gains = more
+    counts, own_gains, masked_low = more
     slot_tokens = slot_tokens.reshape(slot_len, width)
     qkv_local = qkv_local.reshape(width, 3 * head_width)
     router = small[:, 8 + top_count :].reshape(n_dev, -1)[:, : owned * experts]

time: 638 us -> 636 us (level)
  no operation moved by 1% of the time
where the time goes in v7:
time: 636 us; the launch traced here: 626 us
  Pallas kernels  553 us (87%)
  local copies, waits for them, and re-layouts  18.5 us (3%)
  between operations  17.3 us (3%)
  other arithmetic  13.4 us (2%)
  matrix products  12.8 us (2%)
  starting transfers between devices  9.73 us (2%)
    pallas_call x1, Pallas kernels, dispatch_rows(): pl.pallas_call(functools.partial(dispatch_kernel, n_seq, n_fsdp, pieces),...  129 us
    pallas_call x1, Pallas kernels, return_rows(): pl.pallas_call(functools.partial(return_kernel, n_seq, n_fsdp, pieces), o...  85.5 us
    pallas_call x1, Pallas kernels, first_gather(): pl.pallas_call(loading(functools.partial(first_kernel, n_seq, n_fsdp, pie...  83.9 us
    pallas_call x1, Pallas kernels, last_reduce(): pl.pallas_call(functools.partial(last_kernel, n_seq, n_fsdp), out_shape=[...  68.2 us
    pallas_call x4, Pallas kernels, weight_grad(): pl.pallas_call(weight_grad_kernel, out_shape=jax.ShapeDtypeStruct((pieces...  41.4 us
    pallas_call x1, Pallas kernels, gather_seq(): pl.pallas_call(functools.partial(gather_kernel, n_seq, n_fsdp), out_shape...  34 us
    pallas_call x1, Pallas kernels, product_reduced(): pl.pallas_call(loading(functools.partial(reduce_kernel, n_seq, w_dim), fu...  30.9 us
    pallas_call x2, Pallas kernels, expert_backward(): pl.pallas_call(expert_backward_kernel, out_shape=[jax.ShapeDtypeStruct((2...  23.5 us
  transfers between devices with their start and end apart: 4, of which 1 were waited for; matrix products, arithmetic and copies ran while one was open for 4% of the time, Pallas kernels for 25%

profile of v7, /device:TPU:0, one launch (start us, length us, event | category | flops | bytes accessed | tf_op | source)
XLA Modules:
  0.0 625.9 jit_solution(13273543678436640495)
XLA Ops:
  7.2 0.8 reshape.109
  8.0 0.7 convert_bitcast_fusion
  8.7 1.3 fusion.14.refs_0_
  10.0 83.9 %first_gather.1 = (bf16[32,48,128]{2,1,0:T(8,128)(2,1)}, f32[8,2048]{1,0:T(8,128)}, bf16[8,128,2048]{2,1,0:T(8,128)(2,1)}, bf16[8,4,64,768]{3,2,1,0:T(8,128)(2,1...) custom-call(bf16[48,128]{1,0:T(8,128)(2,1)} %fusion.14.refs_0_, ...), custom_call_target="tpu_custom_call" | custom-call | tf_op jit(solution)/shard_map/first_gather/pallas_call | solution.py:626
  94.0 1.3 dynamic_slice.9.length
  95.3 0.8 slice.42
  96.1 16.4 %front.1 = (bf16[1024,2048]{1,0:T(8,128)(2,1)}, f32[1024,768]{1,0:T(8,128)}, f32[8,1024]{1,0:T(8,128)}) custom-call(bf16[1024,2048]{1,0:T(8,128)(2,1)} %bitcast.58, f32[8,2048]{1,0:T(8,128)} %get-tuple-element.68.refs_1_.gains, bf16[2048,768]{1,0:T(8,128)(2,1)} %bitcast.54), custom_call_target="tpu_custom_call" | custom-call | tf_op jit(solution)/shard_map/front/pallas_call | solution.py:1835
  112.8 10.8 %attend.1 = (bf16[1024,256]{1,0:T(8,128)(2,1)}, bf16[1024,256]{1,0:T(8,128)(2,1)}, bf16[1024,256]{1,0:T(8,128)(2,1)}, bf16[1024,256]{1,0:T(8,128)(2,1)}) custom-call(s32[1]{0:T(128)} %dynamic_slice.9.length, f32[1024,768]{1,0:T(8,128)} %get-tuple-element.70.raw_q.raw_k.raw_v.refs_3_, f32[1024,768]{1,0:T(8,128)} %get-tuple-element.70.raw_q.raw_k.raw_v.refs_3_, ...), custom_call_target="tpu_custom_call" | custom-call | flops 1073741824 | bytes 8388608 | tf_op jit(solution)/shard_map/attend/pallas_call | solution.py:1915
  123.9 30.9 %product_reduced.1 = f32[128,2048]{1,0:T(8,128)} custom-call(bf16[8,128,256]{2,1,0:T(8,128)(2,1)} %bitcast.65, bf16[256,2048]{1,0:T(8,128)(2,1)} %all-gather.2.cloned.1.call-done.refs_1_), custom_call_target="tpu_custom_call" | custom-call | tf_op jit(solution)/shard_map/product_reduced/pallas_call | solution.py:942
  154.8 1.6 multiply_reduce_fusion.2
  157.3 0.7 pad.25.gates
  157.9 128.9 %dispatch_rows.1 = (bf16[8,2,4,24,2048]{4,3,2,1,0:T(8,128)(2,1)}, f32[2,768,1]{2,1,0:T(8,128)}, bf16[8,2,4,24,2048]{4,3,2,1,0:T(8,128)(2,1)}, bf16[8,4,24,2048]{...) custom-call(bf16[128,2048]{1,0:T(8,128)(2,1)} %copy-done.1, ...), custom_call_target="tpu_custom_call", output_to_operand_aliasing={{0}: (4, {})} | custom-call | tf_op jit(solution)/shard_map/dispatch_rows/pallas_call | solution.py:1423
  286.9 5.1 all-to-all-start
  293.3 0.7 compare_convert_fusion
  293.9 0.7 divide_bitcast_fusion
  294.6 0.9 slice_bitcast_fusion.1
  295.6 11.8 %expert_backward.3 = (bf16[2,768,1024]{2,1,0:T(8,128)(2,1)}, bf16[768,2048]{1,0:T(8,128)(2,1)}, f32[8,768]{1,0:T(8,128)}) custom-call(bf16[8,2,4,24,2048]{4,3,2,1,0:T(8,128)(2,1)} %get-tuple-element.83.masked, f32[768,1]{1,0:T(8,128)} %get-tuple-element.163.gates, bf16[768,2048]{1,0:T(8,128)(2,1)} %get-tuple-element.88.piece_out, ...), custom_call_target="tpu_custom_call" | custom-call | flops 3221225472 | bytes 9437184 | tf_op jit(solution)/shard_map/expert_backward/pallas_call | solution.py:1719
  307.3 0.8 slice_reduce_fusion
  308.2 11.8 %expert_backward.2 = (bf16[2,768,1024]{2,1,0:T(8,128)(2,1)}, bf16[768,2048]{1,0:T(8,128)(2,1)}, f32[8,768]{1,0:T(8,128)}) custom-call(bf16[8,2,4,24,2048]{4,3,2,1,0:T(8,128)(2,1)} %get-tuple-element.83.masked, f32[768,1]{1,0:T(8,128)} %get-tuple-element.162.gates, bf16[768,2048]{1,0:T(8,128)(2,1)} %get-tuple-element.85.piece_out, ...), custom_call_target="tpu_custom_call" | custom-call | flops 3221225472 | bytes 9437184 | tf_op jit(solution)/shard_map/expert_backward/pallas_call | solution.py:1719
  319.9 0.8 slice_reduce_fusion.1
  320.9 0.8 copy.38.gates
  321.7 8.0 %weight_grad.6.refs_0_ = f32[2,1024,2048]{2,1,0:T(8,128)} custom-call(bf16[768,1024]{1,0:T(8,128)(2,1)} %get-tuple-element.98.a, bf16[1,768,2048]{2,1,0:T(8,128)(2,1)} %bitcast.62), custom_call_target="tpu_custom_call" | custom-call | flops 3221225472 | bytes 8388608 | tf_op jit(solution)/shard_map/weight_grad/pallas_call | solution.py:1660
  329.7 8.0 %weight_grad.7 = f32[2,1024,2048]{2,1,0:T(8,128)} custom-call(bf16[768,1024]{1,0:T(8,128)(2,1)} %get-tuple-element.96.a, bf16[1,768,2048]{2,1,0:T(8,128)(2,1)} %bitcast.61, f32[2,1024,2048]{2,1,0:T(8,128)} %weight_grad.6.refs_0_), custom_call_target="tpu_custom_call", output_to_operand_aliasing={{}: (2, {})} | custom-call | flops 3221225472 | bytes 8388608 | tf_op jit(solution)/shard_map/weight_grad/pallas_call | solution.py:1660
  337.7 12.7 %weight_grad.4.refs_0_ = f32[2,2048,2048]{2,1,0:T(8,128)} custom-call(bf16[768,2048]{1,0:T(8,128)(2,1)} %bitcast.60, bf16[2,768,1024]{2,1,0:T(8,128)(2,1)} %get-tuple-element.91.b), custom_call_target="tpu_custom_call" | custom-call | flops 6442450944 | bytes 16777216 | tf_op jit(solution)/shard_map/weight_grad/pallas_call | solution.py:1660
  350.4 12.7 %weight_grad.5 = f32[2,2048,2048]{2,1,0:T(8,128)} custom-call(bf16[768,2048]{1,0:T(8,128)(2,1)} %bitcast.59, bf16[2,768,1024]{2,1,0:T(8,128)(2,1)} %get-tuple-element.92.b, f32[2,2048,2048]{2,1,0:T(8,128)} %weight_grad.4.refs_0_), custom_call_target="tpu_custom_call", output_to_operand_aliasing={{}: (2, {})} | custom-call | flops 6442450944 | bytes 16777216 | tf_op jit(solution)/shard_map/weight_grad/pallas_call | solution.py:1660
  363.1 0.8 all-to-all-done.ready
  363.8 85.5 %return_rows.1 = (f32[128,2048]{1,0:T(8,128)}, f32[32,8,128]{2,1,0:T(8,128)}, bf16[4,128,2048]{2,1,0:T(8,128)(2,1)}) custom-call(bf16[4,128,384]{2,1,0:T(8,128)(2,1)} %get-tuple-element.79.hot, f32[32,8,128]{2,1,0:T(8,128)} %copy.38.gates, bf16[8,2,4,24,2048]{4,3,2,1,0:T(8,128)(2,1)} %all-to-all-done.ready, bf16[2,2048,2048]{2,1,0:T(8,128)(2,1)} %w_up.3, ...), custom_call_target="tpu_custom_call" | custom-call | tf_op jit(solution)/shard_map/return_rows/pallas_call | solution.py:1615
  449.3 0.9 copy.42
  450.8 1.2 fusion.15.terms
  452.1 2.2 multiply_reduce_fusion
  454.3 4.6 all-to-all-start.1
  458.9 2.6 fusion.18
  461.5 34.0 %gather_seq.1 = (bf16[8,128,2048]{2,1,0:T(8,128)(2,1)}, f32[64,256]{1,0:T(8,128)}) custom-call(bf16[128,2048]{1,0:T(8,128)(2,1)} %get-tuple-element.156.x, f32[64,2048]{1,0:T(8,128)} %fusion.15.terms), custom_call_target="tpu_custom_call" | custom-call | bytes 67108864 | tf_op jit(solution)/shard_map/gather_seq/pallas_call | solution.py:792
  495.5 4.5 convolution_convert_fusion
  500.1 4.3 convolution_convert_fusion.1.g_ref
  504.4 17.0 %attend_back.1 = (f32[1024,256]{1,0:T(8,128)}, f32[1024,256]{1,0:T(8,128)}, bf16[1024,256]{1,0:T(8,128)(2,1)}, f32[8,1024]{1,0:T(8,128)}, f32[8,256]{1,0:T(8,128)}) custom-call(s32[1]{0:T(128)} %dynamic_slice.9.length, bf16[1024,256]{1,0:T(8,128)(2,1)} %get-tuple-element.73.q_ref, bf16[1024,256]{1,0:T(8,128)(2,1)} %get-tuple-element.74.k_ref, ...), custom_call_target="tpu_custom_call" | custom-call | flops 5368709120 | bytes 16777216 | tf_op jit(solution)/shard_map/attend_back/pallas_call | solution.py:2019
  521.5 0.7 slice.50
  522.8 12.8 %raw_back.1 = (bf16[1024,768]{1,0:T(8,128)(2,1)}, f32[64,256]{1,0:T(8,128)}) custom-call(f32[1024,256]{1,0:T(8,128)} %get-tuple-element.107.refs_0_, f32[1024,256]{1,0:T(8,128)} %get-tuple-element.108.refs_1_, bf16[1024,256]{1,0:T(8,128)(2,1)} %get-tuple-element.109.refs_2_, f32[1024,768]{1,0:T(8,128)} %get-tuple-element.70.raw_q.raw_k.raw_v.refs_3_, ...), custom_call_target="tpu_custom_call" | custom-call | tf_op jit(solution)/shard_map/raw_back/pallas_call | solution.py:2109
  535.6 0.8 dynamic-slice_bitcast_fusion
  536.4 0.7 copy.37
  537.2 0.7 select_maximum_fusion.terms_in
  537.8 1.8 convert_element_type.70
  539.6 68.2 %last_reduce.1 = (bf16[128,2048]{1,0:T(8,128)(2,1)}, f32[64,6144]{1,0:T(8,128)}, f32[8,256]{1,0:T(8,128)}, bf16[128,2048]{1,0:T(8,128)(2,1)}) custom-call(bf16[8,128,768]{2,1,0:T(8,128)(2,1)} %bitcast.64, bf16[2048,768]{1,0:T(8,128)(2,1)} %bitcast.55, bf16[1024,2048]{1,0:T(8,128)(2,1)} %get-tuple-element.115.normed, bf16[128,2048]{1,0:T(8,128)(2,1)} %bitcast.57, ...), custom_call_target="tpu_custom_call" | custom-call | bytes 134217728 | tf_op jit(solution)/shard_map/last_reduce/pallas_call | solution.py:1147
  607.8 0.8 constant_dynamic-slice_fusion
  608.6 1.3 divide_reduce_fusion
  611.1 1.9 copy.49
  613.0 1.9 copy.50
  614.9 2.7 copy.51
  (54 shorter events, 4.2 us)
Async XLA Ops:
  7.2 116.7 %all-gather.2.cloned.1.call-start = ((), (), s32[]{:S(2)}) async-start(), calls=%async_computation.3 | async-start | bytes 1310720 | tf_op jit(solution)/shard_map/all_gather | solution.py:2218
  93.9 18.6 %copy-start.6 = (bf16[32,48,128]{2,1,0:T(8,128)(2,1)S(1)}, bf16[32,48,128]{2,1,0:T(8,128)(2,1)}, u32[]{:S(2)}) copy-start(bf16[32,48,128]{2,1,0:T(8,128)(2,1)} %get-tuple-element.81) | copy-start | bytes 1179652
  112.8 10.8 %copy-start.7 = (s32[1,128,8]{1,2,0:T(8,128)S(1)}, s32[1,128,8]{1,2,0:T(8,128)}, u32[]{:S(2)}) copy-start(s32[1,128,8]{1,2,0:T(8,128)} %param.15) | copy-start | bytes 12292
  156.4 302.6 %copy-start = (f32[128,2048]{1,0:T(8,128)}, f32[128,2048]{1,0:T(8,128)S(1)}, u32[]{:S(2)}) copy-start(f32[128,2048]{1,0:T(8,128)S(1)} %get-tuple-element.161.resid) | copy-start | bytes 3145732
  156.5 1.4 copy-start.1
  286.9 5.1 copy-start.8
  286.9 7.7 %copy-start.4 = (f32[2,768,1]{2,1,0:T(8,128)S(1)}, f32[2,768,1]{2,1,0:T(8,128)}, u32[]{:S(2)}) copy-start(f32[2,768,1]{2,1,0:T(8,128)} %get-tuple-element.84) | copy-start | bytes 18436
  286.9 76.9 %all-to-all-start = ((bf16[8,2,4,24,2048]{4,3,2,1,0:T(8,128)(2,1)}), bf16[8,2,4,24,2048]{4,3,2,1,0:T(8,128)(2,1)}, u32[]{:S(2)}, u32[]{:S(2)}) async-start(bf16[8,2,4,24,2048]{4,3,2,1,0:T(8,128)(2,1)} %get-tuple-element.93), calls=%async_computation | async-start | bytes 12582912 | tf_op jit(solution)/shard_map/all_to_all | solution.py:2221
  363.8 87.0 %copy-start.2 = (bf16[128,2048]{1,0:T(8,128)(2,1)S(1)}, bf16[128,2048]{1,0:T(8,128)(2,1)}, u32[]{:S(2)}) copy-start(bf16[128,2048]{1,0:T(8,128)(2,1)} %copy-done.1) | copy-start | bytes 1572868
  454.3 41.3 %copy-start.5 = (bf16[1024,256]{1,0:T(8,128)(2,1)S(1)}, bf16[1024,256]{1,0:T(8,128)(2,1)}, u32[]{:S(2)}) copy-start(bf16[1024,256]{1,0:T(8,128)(2,1)} %get-tuple-element.77) | copy-start | bytes 1572868
  454.3 85.3 %all-to-all-start.1 = ((bf16[4,128,2048]{2,1,0:T(8,128)(2,1)}), bf16[4,128,2048]{2,1,0:T(8,128)(2,1)}, u32[]{:S(2)}, u32[]{:S(2)}) async-start(bf16[4,128,2048]{2,1,0:T(8,128)(2,1)} %get-tuple-element.113), calls=%async_computation.1 | async-start | bytes 4194304 | tf_op jit(solution)/shard_map/all_to_all | solution.py:2311
  458.9 79.0 %reduce-scatter.2.cloned.1.call-start = ((), (), s32[]{:S(2)}) async-start(), calls=%async_computation.4 | async-start | bytes 1310720 | tf_op jit(solution)/shard_map/reduce_scatter | solution.py:2370
  495.5 4.6 copy-start.3
Sparse Core Ops, SparseCore 0:
  94.1 26.8 all-gather.1
  500.2 27.6 reduce-scatter.1
